TPU v7x, 1024 devices: a whole 8x8x8 slice. The times are simulated.
1024 devices in a mesh: row: 32 (over x, y_lo), col: 32 (over y_hi, z, core).
Axes of the slice: x: 8, y: 8 (y_hi: 2, y_lo: 4; y = y_hi * 4 + y_lo), z: 8, core: 2. Of those that a mesh axis runs over, the one named last changes fastest.
Arguments:
- embeddings: bfloat16 [512, 256, 256], P('col'), may hold values from -0.375 to 0.375
- projection: bfloat16 [256, 64], replicated, may hold values from -4.1875 to 4.1875
- weight: bfloat16 [16384, 32768], P('row', 'col'), may hold values from -0.046875 to 0.046875
- act_grad: bfloat16 [512, 32768], P('row', 'col'), may hold values from -6 to 6
Outputs:
- activation: bfloat16 [512, 32768], P('row', 'col')
- weight_grad: float32 [16384, 32768], P('row', 'col')
- feature_grad: float32 [512, 16384], P('col', 'row')
All inputs are finite; a program needn't handle non-finite values.
Results may differ from a plain program's by a relative error of at most 0.0066.
Values may be sent and summed in bfloat16 or wider, within the bound.
No kernel may reach another device: no remote copies, remote signals or barrier semaphores. Data moves between devices by JAX's collectives and lax.ppermute only.
A program may use at most 32 MiB of HBM per device.

v0:
```python
import jax
import jax.numpy as jnp
from jax import lax
from jax.sharding import PartitionSpec as P


def silu_slope(values):
    sig = jax.nn.sigmoid(values)
    return sig * (1.0 + values * (1.0 - sig))


def shards(embeddings, projection, weight, act_grad):
    emb_rows = weight.shape[0] // projection.shape[1]
    emb_first = lax.axis_index("row") * emb_rows
    mine_emb = lax.dynamic_slice_in_dim(embeddings, emb_first, emb_rows, 1)
    interaction = jnp.einsum(
        "bid,bmd->bim", mine_emb, embeddings, preferred_element_type=jnp.float32
    ).astype(jnp.bfloat16)
    local_features = jnp.einsum(
        "bim,mr->bir", interaction, projection, preferred_element_type=jnp.float32
    )
    local_features = local_features.astype(jnp.bfloat16).reshape(embeddings.shape[0], -1)
    features_all = lax.all_gather(local_features, "col", axis=0, tiled=True)
    block = features_all
    preact = lax.psum_scatter(
        jnp.dot(block, weight, preferred_element_type=jnp.float32),
        "row",
        scatter_dimension=0,
        tiled=True,
    )
    activation = jax.nn.silu(preact).astype(jnp.bfloat16)
    slope_mine = (act_grad.astype(jnp.float32) * silu_slope(preact)).astype(jnp.bfloat16)
    slope_all = lax.all_gather(slope_mine, "row", axis=0, tiled=True)
    weight_grad = lax.dot_general(
        features_all, slope_all, (((0,), (0,)), ((), ())), preferred_element_type=jnp.float32
    )
    block = slope_all
    feature_grad = lax.psum_scatter(
        lax.dot_general(
            block, weight, (((1,), (1,)), ((), ())), preferred_element_type=jnp.float32
        ),
        "col",
        scatter_dimension=0,
        tiled=True,
    )
    return (activation, weight_grad, feature_grad)


def solution(mesh):
    return jax.shard_map(
        shards,
        mesh=mesh,
        in_specs=(P("col", None, None), P(), P("row", "col"), P("row", "col")),
        out_specs=(P("row", "col"), P("row", "col"), P("col", "row")),
        check_vma=False,
    )
```

profile of v0, /device:TPU:6, one launch (start us, length us, event | category | flops | bytes accessed | tf_op | source)
XLA Modules:
  0.0 551.7 jit_solution(12495531215645897127)
XLA Ops:
  7.2 0.0 copy-start
  7.2 0.0 reduce-scatter.3.cloned.1.call-start
  7.2 1.5 copy-done
  8.8 1.5 fusion.1
  10.3 0.1 reshape.9
  10.4 69.1 %all_gather.6 = bf16[512,512]{1,0:T(8,128)(2,1)S(1)} all-gather(bf16[16,512]{1,0:T(8,128)(2,1)S(1)} %reshape.9), channel_id=1, replica_groups=mesh['row'=32,'col'=32] {'col'}, dimensions={0}, use_global_device_ids=true | all-gather | bytes 540672 | tf_op jit(solution)/shard_map/all_gather | solution.py:23
  79.5 0.0 copy-start.1
  79.5 3.3 fusion.7
  82.8 0.0 reduce-scatter.3.cloned.1.call-update
  82.8 0.0 all-gather.2.cloned.1.call-start
  82.8 151.2 %reduce-scatter.3.cloned.1.call-done = f32[16,1024]{1,0:T(8,128)} async-done(((f32[512,1024]{1,0:T(8,128)}), f32[16,1024]{1,0:T(8,128)}) %reduce-scatter.3.cloned.1.call-update) | async-done | bytes 65552 | tf_op jit(solution)/shard_map/reduce_scatter | solution.py:25
  234.0 0.0 copy-done.1
  234.0 1.5 multiply_convert_fusion
  235.5 0.0 all-gather.2.cloned.1.call-update
  235.5 0.0 reduce-scatter.5.cloned.1.call-start
  235.6 157.2 %all-gather.2.cloned.1.call-done = bf16[512,1024]{1,0:T(8,128)(2,1)} async-done(((bf16[16,1024]{1,0:T(8,128)(2,1)}), bf16[512,1024]{1,0:T(8,128)(2,1)}) %all-gather.2.cloned.1.call-update) | async-done | bytes 1048592 | tf_op jit(solution)/shard_map/all_gather | solution.py:33
  392.8 3.3 fusion.9
  396.1 0.0 reduce-scatter.5.cloned.1.call-update
  396.1 3.3 fusion.8
  399.4 145.8 %reduce-scatter.5.cloned.1.call-done = f32[16,512]{1,0:T(8,128)} async-done(((f32[512,512]{1,0:T(8,128)}), f32[16,512]{1,0:T(8,128)}) %reduce-scatter.5.cloned.1.call-update) | async-done | bytes 32784 | tf_op jit(solution)/shard_map/reduce_scatter | solution.py:38
Async XLA Ops:
  7.2 1.6 copy-start
  7.2 226.8 %reduce-scatter.3.cloned.1.call-start = ((), (), s32[]{:S(2)}) async-start(), calls=%async_computation.2 | async-start | bytes 2162688 | tf_op jit(solution)/shard_map/reduce_scatter | solution.py:25
  79.5 154.5 %copy-start.1 = (bf16[16,1024]{1,0:T(8,128)(2,1)S(1)}, bf16[16,1024]{1,0:T(8,128)(2,1)}, u32[]{:S(2)}) copy-start(bf16[16,1024]{1,0:T(8,128)(2,1)} %param.7) | copy-start | bytes 98308
  82.8 310.0 %all-gather.2.cloned.1.call-start = ((), (), s32[]{:S(2)}) async-start(), calls=%async_computation.3 | async-start | bytes 1081344 | tf_op jit(solution)/shard_map/all_gather | solution.py:33
  235.5 309.7 %reduce-scatter.5.cloned.1.call-start = ((), (), s32[]{:S(2)}) async-start(), calls=%async_computation.4 | async-start | bytes 1081344 | tf_op jit(solution)/shard_map/reduce_scatter | solution.py:38
Sparse Core Ops, SparseCore 0:
  82.9 151.0 reduce-scatter.2
  237.6 155.1 all-gather.1
  400.2 144.9 reduce-scatter.4
where the time goes:
time: 552 us
  waiting for transfers between devices  454 us (82%)
  blocking collectives  69.1 us (13%)
  between operations  13.8 us (2%)
  matrix products  11.4 us (2%)
    all_gather x1, waiting for transfers between devices, shards(): slope_all = lax.all_gather(slope_mine, 'row', axis=0, tiled=True)  157 us
    reduce_scatter x1, waiting for transfers between devices, shards(): lax.psum_scatter(jnp.dot(block, weight, preferred_element_type=jnp.float3...  151 us
    reduce_scatter x1, waiting for transfers between devices, shards(): lax.psum_scatter(lax.dot_general(block, weight, (((1,), (1,)), ((), ())),...  146 us
    all_gather x1, blocking collectives, shards(): features_all = lax.all_gather(local_features, 'col', axis=0, tiled=True)  69.1 us
  transfers between devices with their start and end apart: 3, of which 3 were waited for; matrix products, arithmetic and copies ran while one was open for 1% of the time, Pallas kernels for 0%

commit v1 on v0

v1 whole, which is shorter than its diff:
```python
import jax
import jax.numpy as jnp
from jax import lax
from jax.sharding import PartitionSpec as P

BF16 = jnp.bfloat16
F32 = jnp.float32


def silu_slope(values):
    sig = jax.nn.sigmoid(values)
    return sig * (1.0 + values * (1.0 - sig))


def gather_rows(part, axis, size):
    copies = jnp.broadcast_to(part[None], (size, *part.shape))
    got = lax.all_to_all(copies, axis, 0, 0)
    return got.reshape(size * part.shape[0], *part.shape[1:])


def sum_scatter_rows(total, axis, size):
    shares = total.astype(BF16).reshape(size, total.shape[0] // size, *total.shape[1:])
    got = lax.all_to_all(shares, axis, 0, 0)
    return jnp.sum(got.astype(F32), axis=0)


def make_shards(rows, cols):
    def shards(embeddings, projection, weight, act_grad):
        emb_rows = weight.shape[0] // projection.shape[1]
        emb_first = lax.axis_index("row") * emb_rows
        mine_emb = lax.dynamic_slice_in_dim(embeddings, emb_first, emb_rows, 1)
        interaction = jnp.einsum(
            "bid,bmd->bim", mine_emb, embeddings, preferred_element_type=F32
        ).astype(BF16)
        local_features = jnp.einsum(
            "bim,mr->bir", interaction, projection, preferred_element_type=F32
        )
        local_features = local_features.astype(BF16).reshape(embeddings.shape[0], -1)
        features_all = gather_rows(local_features, "col", cols)
        preact = sum_scatter_rows(
            jnp.dot(features_all, weight, preferred_element_type=F32), "row", rows
        )
        activation = jax.nn.silu(preact).astype(BF16)
        slope_mine = (act_grad.astype(F32) * silu_slope(preact)).astype(BF16)
        slope_all = gather_rows(slope_mine, "row", rows)
        feature_grad = sum_scatter_rows(
            lax.dot_general(
                slope_all, weight, (((1,), (1,)), ((), ())), preferred_element_type=F32
            ),
            "col",
            cols,
        )
        weight_grad = lax.dot_general(
            features_all, slope_all, (((0,), (0,)), ((), ())), preferred_element_type=F32
        )
        return (activation, weight_grad, feature_grad)

    return shards


def solution(mesh):
    return jax.shard_map(
        make_shards(mesh.shape["row"], mesh.shape["col"]),
        mesh=mesh,
        in_specs=(P("col", None, None), P(), P("row", "col"), P("row", "col")),
        out_specs=(P("row", "col"), P("row", "col"), P("col", "row")),
        check_vma=False,
    )
```

time: 552 us -> 151 us (0.27)
  the two profiles are of different devices: /device:TPU:6 before, /device:TPU:16 now
where the time goes in v1:
time: 151 us; the launch traced here: 150 us
  blocking collectives  113 us (75%)
  waiting for transfers between devices  19.5 us (13%)
  matrix products  8.28 us (5%)
  starting transfers between devices  3.89 us (3%)
  local copies, waits for them, and re-layouts  2.85 us (2%)
  other arithmetic  1.51 us (1%)
    all_to_all x2, blocking collectives, gather_rows(): got = lax.all_to_all(copies, axis, 0, 0)  77.8 us
    all_to_all x1, blocking collectives, sum_scatter_rows(): got = lax.all_to_all(shares, axis, 0, 0)  35.5 us
    all_to_all x1, waiting for transfers between devices, sum_scatter_rows(): got = lax.all_to_all(shares, axis, 0, 0)  19.5 us
    all_to_all x1, starting transfers between devices, sum_scatter_rows(): got = lax.all_to_all(shares, axis, 0, 0)  3.89 us
    dot_general x1, matrix products, shards(): lax.dot_general(features_all, slope_all, (((0,), (0,)), ((), ())), prefer...  3.27 us
  transfers between devices with their start and end apart: 1, of which 1 were waited for; matrix products, arithmetic and copies ran while one was open for 2% of the time, Pallas kernels for 0%

profile of v1, /device:TPU:16, one launch (start us, length us, event | category | flops | bytes accessed | tf_op | source)
XLA Modules:
  0.0 150.1 jit_solution(11673892501668566717)
XLA Ops:
  0.6 0.0 copy-start
  0.6 1.6 %copy-done = bf16[16,256,256]{2,1,0:T(8,128)(2,1)S(1)} copy-done((bf16[16,256,256]{2,1,0:T(8,128)(2,1)S(1)}, bf16[16,256,256]{2,1,0:T(8,128)(2,1)}, u32[]{:S(2)}) %copy-start) | copy-done | bytes 2097176
  2.2 1.5 %fusion.1 = bf16[16,8,64]{2,1,0:T(8,128)(2,1)S(1)} fusion(bf16[16,256,256]{2,1,0:T(8,128)(2,1)S(1)} %copy-done, s32[]{:T(128)S(6)} %select_n.3, bf16[256,64]{0,1:T(8,128)(2,1)} %param.5), kind=kOutput, calls=%fused_computation.6 | convolution fusion | flops 21012480 | bytes 2211844 | tf_op jit(solution)/shard_map/bim,mr->bir/dot_general | solution.py:35
  3.7 0.1 broadcast_in_dim.6
  3.9 0.1 broadcast_in_dim.14
  3.9 44.6 %all_to_all.20 = bf16[32,16,512]{2,1,0:T(8,128)(2,1)S(1)} all-to-all(bf16[32,16,512]{2,1,0:T(8,128)(2,1)S(1)} %broadcast_in_dim.14), channel_id=1, replica_groups=mesh['row'=32,'col'=32] {'col'}, dimensions={0} | all-to-all | bytes 1048576 | tf_op jit(solution)/shard_map/all_to_all | solution.py:17
  48.5 1.9 %convolution_convert_fusion = bf16[512,1024]{1,0:T(8,128)(2,1)S(1)} fusion(bf16[512,512]{1,0:T(8,128)(2,1)S(1)} %bitcast.18, bf16[512,1024]{1,0:T(8,128)(2,1)} %param.6), kind=kOutput, calls=%fused_computation.2 | convolution fusion | flops 537395200 | bytes 2621440 | tf_op jit(solution)/shard_map/dot_general | solution.py:41
  50.4 0.0 copy-start.2
  50.4 35.5 %all_to_all.21 = bf16[32,16,1024]{2,1,0:T(8,128)(2,1)S(1)} all-to-all(bf16[32,16,1024]{2,1,0:T(8,128)(2,1)S(1)} %bitcast.17), channel_id=1, replica_groups=mesh['row'=32,'col'=32] {'row'}, dimensions={0} | all-to-all | bytes 2097152 | tf_op jit(solution)/shard_map/all_to_all | solution.py:23
  86.0 0.0 copy-start.3
  86.0 0.2 convert_reduce_fusion
  86.1 0.0 copy-done.2
  86.1 0.7 multiply_convert_fusion
  86.8 0.1 broadcast_in_dim.15
  86.9 33.3 %all_to_all.22 = bf16[32,16,1024]{2,1,0:T(8,128)(2,1)S(1)} all-to-all(bf16[32,16,1024]{2,1,0:T(8,128)(2,1)S(1)} %broadcast_in_dim.15), channel_id=1, replica_groups=mesh['row'=32,'col'=32] {'row'}, dimensions={0} | all-to-all | bytes 2097152 | tf_op jit(solution)/shard_map/all_to_all | solution.py:17
  120.2 0.0 copy-start.1
  120.2 1.0 copy-done.1
  121.2 0.0 copy-done.3
  121.2 1.6 %convolution_convert_fusion.1 = bf16[512,512]{1,0:T(8,128)(2,1)} fusion(bf16[512,1024]{1,0:T(8,128)(2,1)S(1)} %bitcast.16, bf16[512,1024]{1,0:T(8,128)(2,1)S(1)} %copy-done.3), kind=kOutput, calls=%fused_computation.3 | convolution fusion | flops 537133056 | bytes 2621440 | tf_op jit(solution)/shard_map/dot_general | solution.py:47
  122.7 3.9 %all-to-all-start.3 = ((bf16[32,16,512]{2,1,0:T(8,128)(2,1)}), bf16[32,16,512]{2,1,0:T(8,128)(2,1)S(1)}, u32[]{:S(2)}, u32[]{:S(2)}) async-start(bf16[32,16,512]{2,1,0:T(8,128)(2,1)} %bitcast.19), calls=%async_computation.3 | async-start | bytes 1048576 | tf_op jit(solution)/shard_map/all_to_all | solution.py:23
  126.6 3.3 %convolution_bitcast_fusion = f32[512,1024]{1,0:T(8,128)} fusion(bf16[32,16,512]{2,1,0:T(8,128)(2,1)S(1)} %all_to_all.20, bf16[32,16,1024]{2,1,0:T(8,128)(2,1)} %copy-done.1), kind=kOutput, calls=%fused_computation.1 | convolution fusion | flops 536870912 | bytes 3670016 | tf_op jit(solution)/shard_map/dot_general | solution.py:53
  129.9 19.5 %all-to-all-done.3 = bf16[32,16,512]{2,1,0:T(8,128)(2,1)S(1)} async-done(((bf16[32,16,512]{2,1,0:T(8,128)(2,1)}), bf16[32,16,512]{2,1,0:T(8,128)(2,1)S(1)}, u32[]{:S(2)}, u32[]{:S(2)}) %all-to-all-start.3) | async-done | bytes 524320 | tf_op jit(solution)/shard_map/all_to_all | solution.py:23
  149.4 0.7 convert_reduce_fusion.1
Async XLA Ops:
  0.6 1.6 %copy-start = (bf16[16,256,256]{2,1,0:T(8,128)(2,1)S(1)}, bf16[16,256,256]{2,1,0:T(8,128)(2,1)}, u32[]{:S(2)}) copy-start(bf16[16,256,256]{2,1,0:T(8,128)(2,1)} %param.4) | copy-start | bytes 6291460
  50.4 35.7 %copy-start.2 = (bf16[16,1024]{1,0:T(8,128)(2,1)S(1)}, bf16[16,1024]{1,0:T(8,128)(2,1)}, u32[]{:S(2)}) copy-start(bf16[16,1024]{1,0:T(8,128)(2,1)} %param.7) | copy-start | bytes 98308
  86.0 35.2 %copy-start.3 = (bf16[512,1024]{1,0:T(8,128)(2,1)S(1)}, bf16[512,1024]{1,0:T(8,128)(2,1)}, u32[]{:S(2)}) copy-start(bf16[512,1024]{1,0:T(8,128)(2,1)} %param.6) | copy-start | bytes 3145732
  120.2 1.0 copy-start.1
  122.7 26.7 %all-to-all-start.3 = ((bf16[32,16,512]{2,1,0:T(8,128)(2,1)}), bf16[32,16,512]{2,1,0:T(8,128)(2,1)S(1)}, u32[]{:S(2)}, u32[]{:S(2)}) async-start(bf16[32,16,512]{2,1,0:T(8,128)(2,1)} %bitcast.19), calls=%async_computation.3 | async-start | bytes 1048576 | tf_op jit(solution)/shard_map/all_to_all | solution.py:23

commit v2 on v1

v2 whole, which is shorter than its diff:
```python
import jax
import jax.numpy as jnp
from jax import lax
from jax.sharding import PartitionSpec as P

BF16 = jnp.bfloat16
F32 = jnp.float32


def silu_slope(values):
    sig = jax.nn.sigmoid(values)
    return sig * (1.0 + values * (1.0 - sig))


def send_copies(part, axis, groups):
    copies = jnp.broadcast_to(part[None], (len(groups[0]), *part.shape))
    return lax.all_to_all(copies, axis, 0, 0, axis_index_groups=groups)


def send_shares(shares, axis, groups):
    got = lax.all_to_all(shares, axis, 0, 0, axis_index_groups=groups)
    return jnp.sum(got.astype(F32), axis=0)


def make_shards(rows, cols):
    pairs = [[c, c + 1] for c in range(0, cols, 2)]
    cores = [list(range(core, cols, 2)) for core in range(2)]
    row_order = [[*range(0, rows, 2), *range(1, rows, 2)]]
    swap = [(c, c ^ 1) for c in range(cols)]

    def shards(embeddings, projection, weight, act_grad):
        mine_b = embeddings.shape[0]
        emb_rows = weight.shape[0] // projection.shape[1]
        emb_first = lax.axis_index("row") * emb_rows
        core = lax.axis_index("col") % 2
        mine_emb = lax.dynamic_slice_in_dim(embeddings, emb_first, emb_rows, 1)
        interaction = jnp.einsum(
            "bid,bmd->bim", mine_emb, embeddings, preferred_element_type=F32
        ).astype(BF16)
        local_features = jnp.einsum(
            "bim,mr->bir", interaction, projection, preferred_element_type=F32
        )
        local_features = local_features.astype(BF16).reshape(mine_b, -1)
        same_core = send_copies(local_features, "col", cores)
        same_core = same_core.reshape(-1, same_core.shape[-1])
        features_all = lax.all_gather(
            same_core, "col", axis=0, axis_index_groups=pairs, tiled=True
        )
        partial = jnp.dot(features_all, weight, preferred_element_type=F32).astype(BF16)
        preact = send_shares(
            partial.reshape(rows, -1, partial.shape[-1]), "row", row_order
        )
        slope_mine = (act_grad.astype(F32) * silu_slope(preact)).astype(BF16)
        activation = jax.nn.silu(preact).astype(BF16)
        slope_all = send_copies(slope_mine, "row", row_order)
        slope_all = slope_all.reshape(-1, slope_all.shape[-1])
        half = slope_all.shape[0] // 2

        def grad_of(which):
            mine = lax.dynamic_slice_in_dim(slope_all, which * half, half, 0)
            return lax.dot_general(
                mine, weight, (((1,), (1,)), ((), ())), preferred_element_type=F32
            )

        got = lax.ppermute(grad_of(1 - core).astype(BF16), "col", swap)
        chip_sum = (grad_of(core) + got.astype(F32)).astype(BF16)
        feature_grad = send_shares(
            chip_sum.reshape(cols // 2, mine_b, -1), "col", cores
        )
        weight_grad = lax.dot_general(
            features_all, slope_all, (((0,), (0,)), ((), ())), preferred_element_type=F32
        )
        return (activation, weight_grad, feature_grad)

    return shards


def solution(mesh):
    return jax.shard_map(
        make_shards(mesh.shape["row"], mesh.shape["col"]),
        mesh=mesh,
        in_specs=(P("col", None, None), P(), P("row", "col"), P("row", "col")),
        out_specs=(P("row", "col"), P("row", "col"), P("col", "row")),
        check_vma=False,
    )
```

time: 151 us -> 145 us (0.960)
  the two profiles are of different devices: /device:TPU:16 before, /device:TPU:34 now
where the time goes in v2:
time: 145 us
  blocking collectives  75.5 us (52%)
  waiting for transfers between devices  42.1 us (29%)
  starting transfers between devices  11.9 us (8%)
  matrix products  10.1 us (7%)
  local copies, waits for them, and re-layouts  2.81 us (2%)
  other arithmetic  1.47 us (1%)
    all_to_all x1, blocking collectives, send_shares(): got = lax.all_to_all(shares, axis, 0, 0, axis_index_groups=groups)  37.5 us
    all_to_all x1, blocking collectives, send_copies(): return lax.all_to_all(copies, axis, 0, 0, axis_index_groups=groups)  35.9 us
    all_to_all x1, waiting for transfers between devices, send_copies(): return lax.all_to_all(copies, axis, 0, 0, axis_index_groups=groups)  27.5 us
    all_to_all x1, waiting for transfers between devices, send_shares(): got = lax.all_to_all(shares, axis, 0, 0, axis_index_groups=groups)  12.9 us
    all_to_all x1, starting transfers between devices, send_copies(): return lax.all_to_all(copies, axis, 0, 0, axis_index_groups=groups)  6.37 us
    dot_general x2, matrix products, grad_of(): lax.dot_general(mine, weight, (((1,), (1,)), ((), ())), preferred_element...  4.8 us
    all_to_all x1, starting transfers between devices, send_shares(): got = lax.all_to_all(shares, axis, 0, 0, axis_index_groups=groups)  3.6 us
    dot_general x1, matrix products, shards(): lax.dot_general(features_all, slope_all, (((0,), (0,)), ((), ())), prefer...  3.09 us
  transfers between devices with their start and end apart: 3, of which 3 were waited for; matrix products, arithmetic and copies ran while one was open for 2% of the time, Pallas kernels for 0%

profile of v2, /device:TPU:34, one launch (start us, length us, event | category | flops | bytes accessed | tf_op | source)
XLA Modules:
  0.0 144.6 jit_solution(471835631929243588)
XLA Ops:
  0.6 0.0 copy-start
  0.6 0.0 copy-start.1
  0.7 1.6 %copy-done = bf16[16,256,256]{2,1,0:T(8,128)(2,1)S(1)} copy-done((bf16[16,256,256]{2,1,0:T(8,128)(2,1)S(1)}, bf16[16,256,256]{2,1,0:T(8,128)(2,1)}, u32[]{:S(2)}) %copy-start) | copy-done | bytes 2097176
  2.2 1.5 %fusion.1 = bf16[16,8,64]{2,1,0:T(8,128)(2,1)S(1)} fusion(bf16[16,256,256]{2,1,0:T(8,128)(2,1)S(1)} %copy-done, s32[]{:T(128)S(6)} %select_n.16, bf16[256,64]{0,1:T(8,128)(2,1)} %param.5), kind=kOutput, calls=%fused_computation.5 | convolution fusion | flops 21012480 | bytes 2211844 | tf_op jit(solution)/shard_map/bim,mr->bir/dot_general | solution.py:40
  3.8 0.1 broadcast_in_dim.6
  3.9 35.9 %all_to_all.20 = bf16[16,16,512]{2,1,0:T(8,128)(2,1)S(1)} all-to-all(bf16[16,16,512]{2,1,0:T(8,128)(2,1)S(1)} %broadcast_in_dim.14), channel_id=1, replica_groups={{0,2,4,6,8,10,12,14,16,18,20,22,24,26,28,30},{1,3,5,7,9,11,13,15,17,19,..., dimensions={0} | all-to-all | bytes 524288 | tf_op jit(solution)/shard_map/all_to_all | solution.py:17
  39.8 2.2 %all_gather.3 = bf16[512,512]{1,0:T(8,128)(2,1)S(1)} all-gather(bf16[256,512]{1,0:T(8,128)(2,1)S(1)} %bitcast.17), channel_id=1, replica_groups={{0,1},{2,3},{4,5},{6,7},{8,9},{10,11},{12,13},{14,15},{16,17},{18,19},{..., dimensions={0}, use_global_device_ids=true | all-gather | bytes 786432 | tf_op jit(solution)/shard_map/all_gather | solution.py:46
  41.9 0.0 copy-done.1
  41.9 0.0 copy-start.2
  41.9 0.7 convolution_convert_fusion
  42.6 0.0 copy-start.3
  42.7 37.5 %all_to_all.21 = bf16[32,16,1024]{2,1,0:T(8,128)(2,1)S(1)} all-to-all(bf16[32,16,1024]{2,1,0:T(8,128)(2,1)S(1)} %bitcast.18), channel_id=1, replica_groups={{0,64,128,192,256,320,384,448,512,576,640,704,768,832,896,960,32,96,160..., dimensions={0} | all-to-all | bytes 2097152 | tf_op jit(solution)/shard_map/all_to_all | solution.py:21
  80.1 0.0 copy-done.2
  80.1 0.2 convert_reduce_fusion
  80.3 0.0 copy-done.3
  80.3 0.7 multiply_convert_fusion
  81.0 1.1 broadcast_in_dim.15
  82.1 6.4 %all-to-all-start.2 = ((bf16[32,16,1024]{2,1,0:T(8,128)(2,1)}), bf16[32,16,1024]{2,1,0:T(8,128)(2,1)S(1)}, u32[]{:S(2)}, u32[]{:S(2)}) async-start(bf16[32,16,1024]{2,1,0:T(8,128)(2,1)} %broadcast_in_dim.15), calls=%async_computation.2 | async-start | bytes 2097152 | tf_op jit(solution)/shard_map/all_to_all | solution.py:17
  88.4 27.5 %all-to-all-done.2 = bf16[32,16,1024]{2,1,0:T(8,128)(2,1)S(1)} async-done(((bf16[32,16,1024]{2,1,0:T(8,128)(2,1)}), bf16[32,16,1024]{2,1,0:T(8,128)(2,1)S(1)}, u32[]{:S(2)}, u32[]{:S(2)}) %all-to-all-start.2) | async-done | bytes 1048608 | tf_op jit(solution)/shard_map/all_to_all | solution.py:17
  116.0 2.4 %convolution_convert_fusion.1 = bf16[256,512]{1,0:T(8,128)(2,1)} fusion(bf16[512,1024]{1,0:T(8,128)(2,1)} %param.6, bf16[512,1024]{1,0:T(8,128)(2,1)S(1)} %bitcast.14, s32[]{:T(128)S(6)} %select_n.19), kind=kOutput, calls=%fused_computation.2 | convolution fusion | flops 268566528 | bytes 1835012 | tf_op jit(solution)/shard_map/dot_general | solution.py:61
  118.4 1.9 %collective-permute-start = (bf16[256,512]{1,0:T(8,128)(2,1)}, bf16[256,512]{1,0:T(8,128)(2,1)S(1)}, u32[]{:S(2)}, u32[]{:S(2)}) collective-permute-start(bf16[256,512]{1,0:T(8,128)(2,1)} %convolution_convert_fusion.1), channel_id=1, source_target_pairs={{0,1},{1,0},{2,3},{3,2},{4,5},{5,4},{6,7},{7,6},{8,9},{9,8},{10,11... | collective-permute-start | bytes 786440 | tf_op jit(solution)/shard_map/ppermute | solution.py:65
  120.3 1.7 %collective-permute-done = bf16[256,512]{1,0:T(8,128)(2,1)S(1)} collective-permute-done((bf16[256,512]{1,0:T(8,128)(2,1)}, bf16[256,512]{1,0:T(8,128)(2,1)S(1)}, u32[]{:S(2)}, u32[]{:S(2)}) %collective-permute-start) | collective-permute-done | bytes 262176 | tf_op jit(solution)/shard_map/ppermute | solution.py:65
  122.0 2.4 %add_convert_fusion = bf16[256,512]{1,0:T(8,128)(2,1)} fusion(bf16[256,512]{1,0:T(8,128)(2,1)S(1)} %collective-permute-done, bf16[512,1024]{1,0:T(8,128)(2,1)} %param.6, bf16[512,1024]{1,0:T(8,128)(2,1)S(1)} %bitcast.15, s32[]{:T(128)S(6)} %select_n.18), kind=kOutput, calls=%fused_computation.7 | convolution fusion | flops 268828672 | bytes 2097156 | tf_op jit(solution)/shard_map/dot_general | solution.py:61
  124.4 3.6 %all-to-all-start.3 = ((bf16[16,16,512]{2,1,0:T(8,128)(2,1)}), bf16[16,16,512]{2,1,0:T(8,128)(2,1)S(1)}, u32[]{:S(2)}, u32[]{:S(2)}) async-start(bf16[16,16,512]{2,1,0:T(8,128)(2,1)} %bitcast.4), calls=%async_computation.3 | async-start | bytes 524288 | tf_op jit(solution)/shard_map/all_to_all | solution.py:21
  128.0 3.1 %fusion.14 = f32[512,1024]{1,0:T(8,128)} fusion(bf16[512,512]{1,0:T(8,128)(2,1)} %copy-done.2, bf16[512,1024]{1,0:T(8,128)(2,1)S(1)} %bitcast.16), kind=kOutput, calls=%fused_computation.19 | convolution fusion | flops 536870912 | bytes 3670016 | tf_op jit(solution)/shard_map/dot_general | solution.py:70
  131.1 12.9 %all-to-all-done.3 = bf16[16,16,512]{2,1,0:T(8,128)(2,1)S(1)} async-done(((bf16[16,16,512]{2,1,0:T(8,128)(2,1)}), bf16[16,16,512]{2,1,0:T(8,128)(2,1)S(1)}, u32[]{:S(2)}, u32[]{:S(2)}) %all-to-all-start.3) | async-done | bytes 262176 | tf_op jit(solution)/shard_map/all_to_all | solution.py:21
  144.0 0.7 convert_reduce_fusion.1
  (1 shorter events, 0.0 us)
Async XLA Ops:
  0.6 1.6 %copy-start = (bf16[16,256,256]{2,1,0:T(8,128)(2,1)S(1)}, bf16[16,256,256]{2,1,0:T(8,128)(2,1)}, u32[]{:S(2)}) copy-start(bf16[16,256,256]{2,1,0:T(8,128)(2,1)} %param.4) | copy-start | bytes 6291460
  0.6 41.3 %copy-start.1 = (bf16[512,1024]{1,0:T(8,128)(2,1)S(1)}, bf16[512,1024]{1,0:T(8,128)(2,1)}, u32[]{:S(2)}) copy-start(bf16[512,1024]{1,0:T(8,128)(2,1)} %param.6) | copy-start | bytes 3145732
  41.9 38.2 %copy-start.2 = (bf16[512,512]{1,0:T(8,128)(2,1)}, bf16[512,512]{1,0:T(8,128)(2,1)S(1)}, u32[]{:S(2)}) copy-start(bf16[512,512]{1,0:T(8,128)(2,1)S(1)} %all_gather.3) | copy-start | bytes 1572868
  42.6 37.6 %copy-start.3 = (bf16[16,1024]{1,0:T(8,128)(2,1)S(1)}, bf16[16,1024]{1,0:T(8,128)(2,1)}, u32[]{:S(2)}) copy-start(bf16[16,1024]{1,0:T(8,128)(2,1)} %param.7) | copy-start | bytes 98308
  82.1 33.9 %all-to-all-start.2 = ((bf16[32,16,1024]{2,1,0:T(8,128)(2,1)}), bf16[32,16,1024]{2,1,0:T(8,128)(2,1)S(1)}, u32[]{:S(2)}, u32[]{:S(2)}) async-start(bf16[32,16,1024]{2,1,0:T(8,128)(2,1)} %broadcast_in_dim.15), calls=%async_computation.2 | async-start | bytes 2097152 | tf_op jit(solution)/shard_map/all_to_all | solution.py:17
  118.4 3.6 %collective-permute-start = (bf16[256,512]{1,0:T(8,128)(2,1)}, bf16[256,512]{1,0:T(8,128)(2,1)S(1)}, u32[]{:S(2)}, u32[]{:S(2)}) collective-permute-start(bf16[256,512]{1,0:T(8,128)(2,1)} %convolution_convert_fusion.1), channel_id=1, source_target_pairs={{0,1},{1,0},{2,3},{3,2},{4,5},{5,4},{6,7},{7,6},{8,9},{9,8},{10,11... | collective-permute-start | bytes 786440 | tf_op jit(solution)/shard_map/ppermute | solution.py:65
  124.4 19.6 %all-to-all-start.3 = ((bf16[16,16,512]{2,1,0:T(8,128)(2,1)}), bf16[16,16,512]{2,1,0:T(8,128)(2,1)S(1)}, u32[]{:S(2)}, u32[]{:S(2)}) async-start(bf16[16,16,512]{2,1,0:T(8,128)(2,1)} %bitcast.4), calls=%async_computation.3 | async-start | bytes 524288 | tf_op jit(solution)/shard_map/all_to_all | solution.py:21

commit v3 on v2

--- a/solution.py
+++ b/solution.py
@@ -26,13 +26,11 @@
     pairs = [[c, c + 1] for c in range(0, cols, 2)]
     cores = [list(range(core, cols, 2)) for core in range(2)]
     row_order = [[*range(0, rows, 2), *range(1, rows, 2)]]
-    swap = [(c, c ^ 1) for c in range(cols)]
 
     def shards(embeddings, projection, weight, act_grad):
         mine_b = embeddings.shape[0]
         emb_rows = weight.shape[0] // projection.shape[1]
         emb_first = lax.axis_index("row") * emb_rows
-        core = lax.axis_index("col") % 2
         mine_emb = lax.dynamic_slice_in_dim(embeddings, emb_first, emb_rows, 1)
         interaction = jnp.einsum(
             "bid,bmd->bim", mine_emb, embeddings, preferred_element_type=F32
@@ -54,16 +52,12 @@
         activation = jax.nn.silu(preact).astype(BF16)
         slope_all = send_copies(slope_mine, "row", row_order)
         slope_all = slope_all.reshape(-1, slope_all.shape[-1])
-        half = slope_all.shape[0] // 2
-
-        def grad_of(which):
-            mine = lax.dynamic_slice_in_dim(slope_all, which * half, half, 0)
-            return lax.dot_general(
-                mine, weight, (((1,), (1,)), ((), ())), preferred_element_type=F32
-            )
-
-        got = lax.ppermute(grad_of(1 - core).astype(BF16), "col", swap)
-        chip_sum = (grad_of(core) + got.astype(F32)).astype(BF16)
+        partial_grad = lax.dot_general(
+            slope_all, weight, (((1,), (1,)), ((), ())), preferred_element_type=F32
+        ).astype(BF16)
+        chip_sum = send_shares(
+            partial_grad.reshape(2, -1, partial_grad.shape[-1]), "col", pairs
+        ).astype(BF16)
         feature_grad = send_shares(
             chip_sum.reshape(cols // 2, mine_b, -1), "col", cores
         )

time: 145 us -> 143 us (0.986)
  blocking collectives: 75.5 us -> 114 us
  waiting for transfers between devices: 42.1 us -> 12.9 us
  starting transfers between devices: 11.9 us -> 3.59 us
  matrix products: 10.1 us -> 6.06 us
  other arithmetic: 1.47 us -> 3.39 us
    all_to_all x1 -> x2, blocking collectives: 35.9 us -> 69.6 us  [send_copies(): return lax.all_to_all(copies, axis, 0, 0, axis_index_groups=groups)]
    all_to_all x1 -> x0, waiting for transfers between devices: 27.5 us -> none  [send_copies(): return lax.all_to_all(copies, axis, 0, 0, axis_index_groups=groups)]
    all_to_all x1 -> x0, starting transfers between devices: 6.37 us -> none  [send_copies(): return lax.all_to_all(copies, axis, 0, 0, axis_index_groups=groups)]
    all_to_all x1 -> x2, blocking collectives: 37.5 us -> 42.4 us  [send_shares(): got = lax.all_to_all(shares, axis, 0, 0, axis_index_groups=groups)]
    dot_general x2 -> x1, matrix products: 4.8 us -> 0.74 us  [shards(): lax.dot_general(slope_all, weight, (((1,), (1,)), ((), ())), preferred_el...]
    reduce_sum x2 -> x3, other arithmetic: 0.81 us -> 2.73 us  [send_shares(): return jnp.sum(got.astype(F32), axis=0)]
    ppermute x1 -> x0, starting transfers between devices: 1.91 us -> none  [shards(): got = lax.ppermute(grad_of(1 - core).astype(BF16), 'col', swap)]
    ppermute x1 -> x0, waiting for transfers between devices: 1.7 us -> none  [shards(): got = lax.ppermute(grad_of(1 - core).astype(BF16), 'col', swap)]
  transfers between devices with their start and end apart: 3 -> 1, of which waited for: 3 -> 1; matrix products, arithmetic and copies ran while one was open for 2% -> 2% of each run, Pallas kernels for 0% -> 0%
where the time goes in v3:
time: 143 us
  blocking collectives  114 us (80%)
  waiting for transfers between devices  12.9 us (9%)
  matrix products  6.06 us (4%)
  starting transfers between devices  3.59 us (3%)
  other arithmetic  3.39 us (2%)
  local copies, waits for them, and re-layouts  1.84 us (1%)
    all_to_all x2, blocking collectives, send_copies(): return lax.all_to_all(copies, axis, 0, 0, axis_index_groups=groups)  69.6 us
    all_to_all x2, blocking collectives, send_shares(): got = lax.all_to_all(shares, axis, 0, 0, axis_index_groups=groups)  42.4 us
    all_to_all x1, waiting for transfers between devices, send_shares(): got = lax.all_to_all(shares, axis, 0, 0, axis_index_groups=groups)  12.9 us
    all_to_all x1, starting transfers between devices, send_shares(): got = lax.all_to_all(shares, axis, 0, 0, axis_index_groups=groups)  3.59 us
    dot_general x1, matrix products, shards(): lax.dot_general(features_all, slope_all, (((0,), (0,)), ((), ())), prefer...  3.09 us
  transfers between devices with their start and end apart: 1, of which 1 were waited for; matrix products, arithmetic and copies ran while one was open for 2% of the time, Pallas kernels for 0%

profile of v3, /device:TPU:34, one launch (start us, length us, event | category | flops | bytes accessed | tf_op | source)
XLA Modules:
  0.0 142.6 jit_solution(2200560868776354589)
XLA Ops:
  0.6 0.0 copy-start
  0.6 0.0 copy-start.3
  0.7 1.6 %copy-done = bf16[16,256,256]{2,1,0:T(8,128)(2,1)S(1)} copy-done((bf16[16,256,256]{2,1,0:T(8,128)(2,1)S(1)}, bf16[16,256,256]{2,1,0:T(8,128)(2,1)}, u32[]{:S(2)}) %copy-start) | copy-done | bytes 2097176
  2.2 1.5 %fusion.1 = bf16[16,8,64]{2,1,0:T(8,128)(2,1)S(1)} fusion(bf16[16,256,256]{2,1,0:T(8,128)(2,1)S(1)} %copy-done, s32[]{:T(128)S(6)} %select_n.3, bf16[256,64]{0,1:T(8,128)(2,1)} %param.5), kind=kOutput, calls=%fused_computation.5 | convolution fusion | flops 21012480 | bytes 2211844 | tf_op jit(solution)/shard_map/bim,mr->bir/dot_general | solution.py:38
  3.8 0.1 broadcast_in_dim.6
  3.9 35.9 %all_to_all.25 = bf16[16,16,512]{2,1,0:T(8,128)(2,1)S(1)} all-to-all(bf16[16,16,512]{2,1,0:T(8,128)(2,1)S(1)} %broadcast_in_dim.14), channel_id=1, replica_groups={{0,2,4,6,8,10,12,14,16,18,20,22,24,26,28,30},{1,3,5,7,9,11,13,15,17,19,..., dimensions={0} | all-to-all | bytes 524288 | tf_op jit(solution)/shard_map/all_to_all | solution.py:17
  39.8 2.2 %all_gather.3 = bf16[512,512]{1,0:T(8,128)(2,1)S(1)} all-gather(bf16[256,512]{1,0:T(8,128)(2,1)S(1)} %bitcast.17), channel_id=1, replica_groups={{0,1},{2,3},{4,5},{6,7},{8,9},{10,11},{12,13},{14,15},{16,17},{18,19},{..., dimensions={0}, use_global_device_ids=true | all-gather | bytes 786432 | tf_op jit(solution)/shard_map/all_gather | solution.py:44
  41.9 0.0 copy-done.3
  41.9 0.0 copy-start.1
  41.9 0.7 convolution_convert_fusion
  42.6 0.0 copy-start.2
  42.7 37.5 %all_to_all.26 = bf16[32,16,1024]{2,1,0:T(8,128)(2,1)S(1)} all-to-all(bf16[32,16,1024]{2,1,0:T(8,128)(2,1)S(1)} %bitcast.18), channel_id=1, replica_groups={{0,64,128,192,256,320,384,448,512,576,640,704,768,832,896,960,32,96,160..., dimensions={0} | all-to-all | bytes 2097152 | tf_op jit(solution)/shard_map/all_to_all | solution.py:21
  80.1 0.0 copy-done.1
  80.1 0.0 copy-start.4
  80.1 0.2 convert_reduce_fusion
  80.3 0.0 copy-done.2
  80.3 0.7 multiply_convert_fusion
  81.0 0.1 broadcast_in_dim.15
  81.1 33.7 %all_to_all.27 = bf16[32,16,1024]{2,1,0:T(8,128)(2,1)S(1)} all-to-all(bf16[32,16,1024]{2,1,0:T(8,128)(2,1)S(1)} %broadcast_in_dim.15), channel_id=1, replica_groups={{0,64,128,192,256,320,384,448,512,576,640,704,768,832,896,960,32,96,160..., dimensions={0} | all-to-all | bytes 2097152 | tf_op jit(solution)/shard_map/all_to_all | solution.py:17
  114.8 0.0 copy-done.4
  114.8 0.7 convolution_convert_fusion.1
  115.5 4.9 %all_to_all.28 = bf16[2,256,512]{2,1,0:T(8,128)(2,1)} all-to-all(bf16[2,256,512]{2,1,0:T(8,128)(2,1)S(1)} %bitcast.20), channel_id=1, replica_groups={{0,1},{2,3},{4,5},{6,7},{8,9},{10,11},{12,13},{14,15},{16,17},{18,19},{..., dimensions={0} | all-to-all | bytes 1048576 | tf_op jit(solution)/shard_map/all_to_all | solution.py:21
  120.4 1.9 %reduce_sum.31 = bf16[256,512]{1,0:T(8,128)(2,1)} reduce(bf16[2,256,512]{2,1,0:T(8,128)(2,1)} %all_to_all.28, bf16[]{:T(256)} %constant.18.clone.1), dimensions={0}, to_apply=%region_1.2 | reduce | flops 131072 | bytes 786434 | tf_op jit(solution)/shard_map/reduce_sum | solution.py:22
  122.3 3.6 %all-to-all-start.4 = ((bf16[16,16,512]{2,1,0:T(8,128)(2,1)}), bf16[16,16,512]{2,1,0:T(8,128)(2,1)S(1)}, u32[]{:S(2)}, u32[]{:S(2)}) async-start(bf16[16,16,512]{2,1,0:T(8,128)(2,1)} %bitcast.19), calls=%async_computation.4 | async-start | bytes 524288 | tf_op jit(solution)/shard_map/all_to_all | solution.py:21
  125.9 3.1 %fusion.7 = f32[512,1024]{1,0:T(8,128)} fusion(bf16[512,512]{1,0:T(8,128)(2,1)} %copy-done.1, bf16[512,1024]{1,0:T(8,128)(2,1)S(1)} %bitcast.16), kind=kOutput, calls=%fused_computation.13 | convolution fusion | flops 536870912 | bytes 3670016 | tf_op jit(solution)/shard_map/dot_general | solution.py:64
  129.0 12.9 %all-to-all-done.4 = bf16[16,16,512]{2,1,0:T(8,128)(2,1)S(1)} async-done(((bf16[16,16,512]{2,1,0:T(8,128)(2,1)}), bf16[16,16,512]{2,1,0:T(8,128)(2,1)S(1)}, u32[]{:S(2)}, u32[]{:S(2)}) %all-to-all-start.4) | async-done | bytes 262176 | tf_op jit(solution)/shard_map/all_to_all | solution.py:21
  141.9 0.7 convert_reduce_fusion.1
  (1 shorter events, 0.0 us)
Async XLA Ops:
  0.6 1.6 %copy-start = (bf16[16,256,256]{2,1,0:T(8,128)(2,1)S(1)}, bf16[16,256,256]{2,1,0:T(8,128)(2,1)}, u32[]{:S(2)}) copy-start(bf16[16,256,256]{2,1,0:T(8,128)(2,1)} %param.4) | copy-start | bytes 6291460
  0.6 41.3 %copy-start.3 = (bf16[512,1024]{1,0:T(8,128)(2,1)S(1)}, bf16[512,1024]{1,0:T(8,128)(2,1)}, u32[]{:S(2)}) copy-start(bf16[512,1024]{1,0:T(8,128)(2,1)} %param.6) | copy-start | bytes 3145732
  41.9 38.2 %copy-start.1 = (bf16[512,512]{1,0:T(8,128)(2,1)}, bf16[512,512]{1,0:T(8,128)(2,1)S(1)}, u32[]{:S(2)}) copy-start(bf16[512,512]{1,0:T(8,128)(2,1)S(1)} %all_gather.3) | copy-start | bytes 1572868
  42.6 37.7 %copy-start.2 = (bf16[16,1024]{1,0:T(8,128)(2,1)S(1)}, bf16[16,1024]{1,0:T(8,128)(2,1)}, u32[]{:S(2)}) copy-start(bf16[16,1024]{1,0:T(8,128)(2,1)} %param.7) | copy-start | bytes 98308
  80.1 34.6 %copy-start.4 = (bf16[512,1024]{1,0:T(8,128)(2,1)S(1)}, bf16[512,1024]{1,0:T(8,128)(2,1)}, u32[]{:S(2)}) copy-start(bf16[512,1024]{1,0:T(8,128)(2,1)} %param.6) | copy-start | bytes 3145732
  122.3 19.6 %all-to-all-start.4 = ((bf16[16,16,512]{2,1,0:T(8,128)(2,1)}), bf16[16,16,512]{2,1,0:T(8,128)(2,1)S(1)}, u32[]{:S(2)}, u32[]{:S(2)}) async-start(bf16[16,16,512]{2,1,0:T(8,128)(2,1)} %bitcast.19), calls=%async_computation.4 | async-start | bytes 524288 | tf_op jit(solution)/shard_map/all_to_all | solution.py:21

commit v4 on v3

v4 whole, which is shorter than its diff:
```python
import jax
import jax.numpy as jnp
from jax import lax
from jax.sharding import PartitionSpec as P

BF16 = jnp.bfloat16
F32 = jnp.float32


def silu_slope(values):
    sig = jax.nn.sigmoid(values)
    return sig * (1.0 + values * (1.0 - sig))


def send_copies(part, axis, groups=None):
    size = len(groups[0]) if groups else lax.axis_size(axis)
    copies = jnp.broadcast_to(part[None], (size, *part.shape))
    got = lax.all_to_all(copies, axis, 0, 0, axis_index_groups=groups)
    return got.reshape(-1, got.shape[-1])


def send_shares(shares, axis, groups=None):
    got = lax.all_to_all(shares, axis, 0, 0, axis_index_groups=groups)
    return jnp.sum(got.astype(F32), axis=0)


def either(flag, first, second, axis):
    return jnp.where(
        flag,
        jnp.concatenate([first, second], axis),
        jnp.concatenate([second, first], axis),
    )


def make_shards(rows, cols):
    cores = [list(range(core, cols, 2)) for core in range(2)]
    swap = [(c, c ^ 1) for c in range(cols)]
    spread, spread_far = [], []
    for row in range(rows):
        for col in range(cols):
            h, k = row % 2, col % 2
            spread.append((row * cols + col, (row - h + k) * cols + col - k + h))
            spread_far.append((row * cols + col, (row - h + 1 - k) * cols + col - k + h))
    collect = [(b, a) for a, b in spread]
    collect_far = [(b, a) for a, b in spread_far]

    def shards(embeddings, projection, weight, act_grad):
        mine_b, width = act_grad.shape
        half = mine_b // 2
        emb_rows = weight.shape[0] // projection.shape[1]
        emb_first = lax.axis_index("row") * emb_rows
        h, k = lax.axis_index("row") % 2, lax.axis_index("col") % 2

        mine_emb = lax.dynamic_slice_in_dim(embeddings, emb_first, emb_rows, 1)
        interaction = jnp.einsum(
            "bid,bmd->bim", mine_emb, embeddings, preferred_element_type=F32
        ).astype(BF16)
        local_features = jnp.einsum(
            "bim,mr->bir", interaction, projection, preferred_element_type=F32
        )
        local_features = local_features.astype(BF16).reshape(mine_b, -1)
        local_features, weight_late = lax.optimization_barrier((local_features, weight))
        features = send_copies(local_features, "col", cores)

        both_weights = jnp.concatenate(
            [weight, lax.ppermute(weight_late, "col", swap)], 1
        )
        halves = act_grad.reshape(2, half, width)
        near = lax.ppermute(
            lax.dynamic_index_in_dim(halves, k, 0, False), ("row", "col"), spread
        )
        far = lax.ppermute(
            lax.dynamic_index_in_dim(halves, 1 - k, 0, False), ("row", "col"), spread_far
        )
        both_grads = either(h == k, near, far, 1).astype(F32)

        partial = jnp.dot(features, both_weights, preferred_element_type=F32)
        preact = send_shares(partial.astype(BF16).reshape(rows, half, -1), "row")
        slope_mine = (both_grads * silu_slope(preact)).astype(BF16)
        slope = send_copies(slope_mine, "row")

        acts = jax.nn.silu(preact).astype(BF16)
        acts = either(h == k, acts[:, :width], acts[:, width:], 0).reshape(2, half, width)
        near = lax.ppermute(acts[0], ("row", "col"), collect)
        far = lax.ppermute(acts[1], ("row", "col"), collect_far)
        activation = either(k == 0, near, far, 0)

        partial_grad = lax.dot_general(
            slope, both_weights, (((1,), (1,)), ((), ())), preferred_element_type=F32
        ).astype(BF16)
        partial_grad, slope_late = lax.optimization_barrier((partial_grad, slope))
        grad_shares = lax.all_to_all(
            partial_grad.reshape(cols // 2, mine_b, -1),
            "col", 0, 0, axis_index_groups=cores,
        )

        features_all = jnp.concatenate([features, lax.ppermute(features, "col", swap)])
        slope_all = jnp.concatenate(
            [slope_late[:, :width], lax.ppermute(slope_late[:, width:], "col", swap)]
        )
        weight_grad = lax.dot_general(
            features_all, slope_all, (((0,), (0,)), ((), ())), preferred_element_type=F32
        )
        grad_shares, weight_grad = lax.optimization_barrier((grad_shares, weight_grad))
        feature_grad = jnp.sum(grad_shares.astype(F32), axis=0)
        return (activation, weight_grad, feature_grad)

    return shards


def solution(mesh):
    return jax.shard_map(
        make_shards(mesh.shape["row"], mesh.shape["col"]),
        mesh=mesh,
        in_specs=(P("col", None, None), P(), P("row", "col"), P("row", "col")),
        out_specs=(P("row", "col"), P("row", "col"), P("col", "row")),
        check_vma=False,
    )
```

time: 143 us -> 146 us (1.021)
  the two profiles are of different devices: /device:TPU:34 before, /device:TPU:32 now
where the time goes in v4:
time: 146 us; the launch traced here: 145 us
  waiting for transfers between devices  71.4 us (49%)
  starting transfers between devices  52.5 us (36%)
  matrix products  11 us (8%)
  local copies, waits for them, and re-layouts  7.9 us (5%)
  other arithmetic  1.49 us (1%)
    all_to_all x2, waiting for transfers between devices, send_copies(): got = lax.all_to_all(copies, axis, 0, 0, axis_index_groups=groups)  38.8 us
    all_to_all x2, starting transfers between devices, send_copies(): got = lax.all_to_all(copies, axis, 0, 0, axis_index_groups=groups)  26 us
    all_to_all x1, waiting for transfers between devices, send_shares(): got = lax.all_to_all(shares, axis, 0, 0, axis_index_groups=groups)  23.1 us
    all_to_all x1, starting transfers between devices, send_shares(): got = lax.all_to_all(shares, axis, 0, 0, axis_index_groups=groups)  9.27 us
    all_to_all x1, waiting for transfers between devices, shards(): lax.all_to_all(partial_grad.reshape(cols // 2, mine_b, -1), 'col', 0, 0,...  6.69 us
    all_to_all x1, starting transfers between devices, shards(): lax.all_to_all(partial_grad.reshape(cols // 2, mine_b, -1), 'col', 0, 0,...  4.66 us
    ppermute x1, starting transfers between devices, shards(): lax.ppermute(lax.dynamic_index_in_dim(halves, 1 - k, 0, False), ('row', '...  3.37 us
    dot_general x1, matrix products, shards(): partial = jnp.dot(features, both_weights, preferred_element_type=F32)  3.3 us
  transfers between devices with their start and end apart: 11, of which 5 were waited for; matrix products, arithmetic and copies ran while one was open for 8% of the time, Pallas kernels for 0%

profile of v4, /device:TPU:32, one launch (start us, length us, event | category | flops | bytes accessed | tf_op | source)
XLA Modules:
  0.0 145.2 jit_solution(14112836417417339838)
XLA Ops:
  0.6 0.0 copy-start
  0.7 1.6 %copy-done = bf16[16,256,256]{2,1,0:T(8,128)(2,1)S(1)} copy-done((bf16[16,256,256]{2,1,0:T(8,128)(2,1)S(1)}, bf16[16,256,256]{2,1,0:T(8,128)(2,1)}, u32[]{:S(2)}) %copy-start) | copy-done | bytes 2097176
  2.2 1.5 %fusion.2 = bf16[16,8,64]{2,1,0:T(8,128)(2,1)S(1)} fusion(bf16[16,256,256]{2,1,0:T(8,128)(2,1)S(1)} %copy-done, s32[]{:T(128)S(6)} %select_n.51, bf16[256,64]{0,1:T(8,128)(2,1)} %param.5), kind=kOutput, calls=%fused_computation.6 | convolution fusion | flops 21012480 | bytes 2211844 | tf_op jit(solution)/shard_map/bim,mr->bir/dot_general | solution.py:58
  3.8 0.1 reshape.72
  3.9 1.9 %collective-permute-start = (bf16[512,1024]{1,0:T(8,128)(2,1)S(1)}, bf16[512,1024]{1,0:T(8,128)(2,1)}, u32[]{:S(2)}, u32[]{:S(2)}) collective-permute-start(bf16[512,1024]{1,0:T(8,128)(2,1)S(1)} %copy-done.1), channel_id=1, source_target_pairs={{0,1},{1,0},{2,3},{3,2},{4,5},{5,4},{6,7},{7,6},{8,9},{9,8},{10,11... | collective-permute-start | bytes 3145736 | tf_op jit(solution)/shard_map/ppermute | solution.py:66
  5.8 0.7 broadcast_in_dim.4
  6.5 20.7 %all-to-all-start = ((bf16[16,16,512]{2,1,0:T(8,128)(2,1)}), bf16[16,16,512]{2,1,0:T(8,128)(2,1)S(1)}, u32[]{:S(2)}, u32[]{:S(2)}) async-start(bf16[16,16,512]{2,1,0:T(8,128)(2,1)} %broadcast_in_dim.4), calls=%async_computation | async-start | bytes 524288 | tf_op jit(solution)/shard_map/all_to_all | solution.py:18
  27.2 1.0 constant_dynamic-update-slice_fusion.1
  28.3 0.0 collective-permute-done
  28.3 2.3 %constant_dynamic-update-slice_fusion = bf16[512,2048]{1,0:T(8,128)(2,1)} fusion(bf16[512,2048]{1,0:T(8,128)(2,1)} %constant_dynamic-update-slice_fusion.1, bf16[512,1024]{1,0:T(8,128)(2,1)} %collective-permute-done), kind=kLoop, calls=%fused_computation.25 | loop fusion | bytes 2097152 | tf_op jit(solution)/shard_map/concatenate | solution.py:65
  30.6 12.5 %all-to-all-done = bf16[16,16,512]{2,1,0:T(8,128)(2,1)S(1)} async-done(((bf16[16,16,512]{2,1,0:T(8,128)(2,1)}), bf16[16,16,512]{2,1,0:T(8,128)(2,1)S(1)}, u32[]{:S(2)}, u32[]{:S(2)}) %all-to-all-start) | async-done | bytes 262176 | tf_op jit(solution)/shard_map/all_to_all | solution.py:18
  43.1 3.3 %fusion = bf16[32,8,2048]{2,1,0:T(8,128)(2,1)} fusion(bf16[256,512]{1,0:T(8,128)(2,1)S(1)} %bitcast.20, bf16[512,2048]{1,0:T(8,128)(2,1)} %constant_dynamic-update-slice_fusion), kind=kOutput, calls=%fused_computation.1 | convolution fusion | flops 537395200 | bytes 3407872 | tf_op jit(solution)/shard_map/dot_general | solution.py:77
  46.4 9.3 %all-to-all-start.1 = ((bf16[32,8,2048]{2,1,0:T(8,128)(2,1)}), bf16[32,8,2048]{2,1,0:T(8,128)(2,1)S(1)}, u32[]{:S(2)}, u32[]{:S(2)}) async-start(bf16[32,8,2048]{2,1,0:T(8,128)(2,1)} %fusion), calls=%async_computation.1 | async-start | bytes 2097152 | tf_op jit(solution)/shard_map/all_to_all | solution.py:23
  55.7 3.4 %collective-permute-start.4 = (bf16[8,1024]{1,0:T(8,128)(2,1)S(1)}, bf16[8,1024]{1,0:T(8,128)(2,1)S(1)}, u32[]{:S(2)}, u32[]{:S(2)}) collective-permute-start(bf16[8,1024]{1,0:T(8,128)(2,1)S(1)} %get-tuple-element.20), channel_id=1, source_target_pairs={{0,32},{1,0},{2,34},{3,2},{4,36},{5,4},{6,38},{7,6},{8,40},{9,8},{... | collective-permute-start | bytes 49160 | tf_op jit(solution)/shard_map/ppermute | solution.py:72
  59.1 0.7 collective-permute-start.3
  59.8 23.1 %all-to-all-done.1 = bf16[32,8,2048]{2,1,0:T(8,128)(2,1)S(1)} async-done(((bf16[32,8,2048]{2,1,0:T(8,128)(2,1)}), bf16[32,8,2048]{2,1,0:T(8,128)(2,1)S(1)}, u32[]{:S(2)}, u32[]{:S(2)}) %all-to-all-start.1) | async-done | bytes 1048608 | tf_op jit(solution)/shard_map/all_to_all | solution.py:23
  82.9 0.2 convert_reduce_fusion
  83.1 1.1 broadcast_in_dim.5
  84.2 5.3 %all-to-all-start.2 = ((bf16[32,8,2048]{2,1,0:T(8,128)(2,1)}), bf16[32,8,2048]{2,1,0:T(8,128)(2,1)S(1)}, u32[]{:S(2)}, u32[]{:S(2)}) async-start(bf16[32,8,2048]{2,1,0:T(8,128)(2,1)} %broadcast_in_dim.5), calls=%async_computation.2 | async-start | bytes 2097152 | tf_op jit(solution)/shard_map/all_to_all | solution.py:18
  89.5 1.9 %collective-permute-start.5 = (bf16[256,512]{1,0:T(8,128)(2,1)S(1)}, bf16[256,512]{1,0:T(8,128)(2,1)}, u32[]{:S(2)}, u32[]{:S(2)}) collective-permute-start(bf16[256,512]{1,0:T(8,128)(2,1)S(1)} %bitcast.21), channel_id=1, source_target_pairs={{0,1},{1,0},{2,3},{3,2},{4,5},{5,4},{6,7},{7,6},{8,9},{9,8},{10,11... | collective-permute-start | bytes 786440 | tf_op jit(solution)/shard_map/ppermute | solution.py:97
  91.4 26.3 %all-to-all-done.2 = bf16[32,8,2048]{2,1,0:T(8,128)(2,1)S(1)} async-done(((bf16[32,8,2048]{2,1,0:T(8,128)(2,1)}), bf16[32,8,2048]{2,1,0:T(8,128)(2,1)S(1)}, u32[]{:S(2)}, u32[]{:S(2)}) %all-to-all-start.2) | async-done | bytes 1048608 | tf_op jit(solution)/shard_map/all_to_all | solution.py:18
  117.7 3.0 %convolution_convert_fusion.1 = bf16[256,512]{1,0:T(8,128)(2,1)} fusion(bf16[512,2048]{1,0:T(8,128)(2,1)} %constant_dynamic-update-slice_fusion, bf16[32,8,2048]{2,1,0:T(8,128)(2,1)S(1)} %all-to-all-done.2), kind=kOutput, calls=%fused_computation.3 | convolution fusion | flops 537001984 | bytes 3407872 | tf_op jit(solution)/shard_map/dot_general | solution.py:88
  120.7 1.0 fusion.17
  121.8 1.9 %collective-permute-start.6 = (bf16[256,1024]{1,0:T(8,128)(2,1)}, bf16[256,1024]{1,0:T(8,128)(2,1)S(1)}, u32[]{:S(2)}, u32[]{:S(2)}) collective-permute-start(bf16[256,1024]{1,0:T(8,128)(2,1)} %get-tuple-element.16), channel_id=1, source_target_pairs={{0,1},{1,0},{2,3},{3,2},{4,5},{5,4},{6,7},{7,6},{8,9},{9,8},{10,11... | collective-permute-start | bytes 1572872 | tf_op jit(solution)/shard_map/ppermute | solution.py:99
  123.7 4.7 %all-to-all-start.3 = ((bf16[16,16,512]{2,1,0:T(8,128)(2,1)}), bf16[16,16,512]{2,1,0:T(8,128)(2,1)S(1)}, u32[]{:S(2)}, u32[]{:S(2)}) async-start(bf16[16,16,512]{2,1,0:T(8,128)(2,1)} %bitcast.23), calls=%async_computation.3 | async-start | bytes 524288 | tf_op jit(solution)/shard_map/all_to_all | solution.py:92
  128.4 2.1 %collective-permute-start.2 = (bf16[8,1024]{1,0:T(8,128)(2,1)S(1)}, bf16[8,1024]{1,0:T(8,128)(2,1)S(1)}, u32[]{:S(2)}, u32[]{:S(2)}) collective-permute-start(bf16[8,1024]{1,0:T(8,128)(2,1)S(1)} %get-tuple-element.22), channel_id=1, source_target_pairs={{32,0},{0,1},{34,2},{2,3},{36,4},{4,5},{38,6},{6,7},{40,8},{8,9},{... | collective-permute-start | bytes 49160 | tf_op jit(solution)/shard_map/ppermute | solution.py:85
  130.6 0.7 collective-permute-start.1
  131.2 2.8 %collective-permute-done.2 = bf16[8,1024]{1,0:T(8,128)(2,1)S(1)} collective-permute-done((bf16[8,1024]{1,0:T(8,128)(2,1)S(1)}, bf16[8,1024]{1,0:T(8,128)(2,1)S(1)}, u32[]{:S(2)}, u32[]{:S(2)}) %collective-permute-start.2) | collective-permute-done | bytes 16416 | tf_op jit(solution)/shard_map/ppermute | solution.py:85
  134.1 0.6 maximum_select_fusion.1
  134.7 3.2 %fusion.3 = f32[512,1024]{1,0:T(8,128)} fusion(bf16[256,1024]{1,0:T(8,128)(2,1)S(1)} %collective-permute-done.6, bf16[256,1024]{1,0:T(8,128)(2,1)} %get-tuple-element.15, bf16[256,512]{1,0:T(8,128)(2,1)} %collective-permute-done.5, bf16[256,512]{1,0:T(8,128)(2,1)S(1)} %bitcast.22), kind=kOutput, calls=%fused_computation.7 | convolution fusion | flops 540016640 | bytes 3670016 | tf_op jit(solution)/shard_map/dot_general | solution.py:101
  137.9 6.7 %all-to-all-done.3 = bf16[16,16,512]{2,1,0:T(8,128)(2,1)S(1)} async-done(((bf16[16,16,512]{2,1,0:T(8,128)(2,1)}), bf16[16,16,512]{2,1,0:T(8,128)(2,1)S(1)}, u32[]{:S(2)}, u32[]{:S(2)}) %all-to-all-start.3) | async-done | bytes 262176 | tf_op jit(solution)/shard_map/all_to_all | solution.py:92
  144.6 0.7 convert_reduce_fusion.1
  (14 shorter events, 0.1 us)
Async XLA Ops:
  0.6 1.6 %copy-start = (bf16[16,256,256]{2,1,0:T(8,128)(2,1)S(1)}, bf16[16,256,256]{2,1,0:T(8,128)(2,1)}, u32[]{:S(2)}) copy-start(bf16[16,256,256]{2,1,0:T(8,128)(2,1)} %param.4) | copy-start | bytes 6291460
  0.6 3.2 %copy-start.1 = (bf16[512,1024]{1,0:T(8,128)(2,1)S(1)}, bf16[512,1024]{1,0:T(8,128)(2,1)}, u32[]{:S(2)}) copy-start(bf16[512,1024]{1,0:T(8,128)(2,1)} %param.6) | copy-start | bytes 3145732
  3.9 24.4 %collective-permute-start = (bf16[512,1024]{1,0:T(8,128)(2,1)S(1)}, bf16[512,1024]{1,0:T(8,128)(2,1)}, u32[]{:S(2)}, u32[]{:S(2)}) collective-permute-start(bf16[512,1024]{1,0:T(8,128)(2,1)S(1)} %copy-done.1), channel_id=1, source_target_pairs={{0,1},{1,0},{2,3},{3,2},{4,5},{5,4},{6,7},{7,6},{8,9},{9,8},{10,11... | collective-permute-start | bytes 3145736 | tf_op jit(solution)/shard_map/ppermute | solution.py:66
  6.5 36.5 %all-to-all-start = ((bf16[16,16,512]{2,1,0:T(8,128)(2,1)}), bf16[16,16,512]{2,1,0:T(8,128)(2,1)S(1)}, u32[]{:S(2)}, u32[]{:S(2)}) async-start(bf16[16,16,512]{2,1,0:T(8,128)(2,1)} %broadcast_in_dim.4), calls=%async_computation | async-start | bytes 524288 | tf_op jit(solution)/shard_map/all_to_all | solution.py:18
  43.1 12.6 %copy-start.2 = (bf16[16,1024]{1,0:T(8,128)(2,1)S(1)}, bf16[16,1024]{1,0:T(8,128)(2,1)}, u32[]{:S(2)}) copy-start(bf16[16,1024]{1,0:T(8,128)(2,1)} %param.7) | copy-start | bytes 98308
  46.4 36.5 %all-to-all-start.1 = ((bf16[32,8,2048]{2,1,0:T(8,128)(2,1)}), bf16[32,8,2048]{2,1,0:T(8,128)(2,1)S(1)}, u32[]{:S(2)}, u32[]{:S(2)}) async-start(bf16[32,8,2048]{2,1,0:T(8,128)(2,1)} %fusion), calls=%async_computation.1 | async-start | bytes 2097152 | tf_op jit(solution)/shard_map/all_to_all | solution.py:23
  55.7 27.3 %collective-permute-start.4 = (bf16[8,1024]{1,0:T(8,128)(2,1)S(1)}, bf16[8,1024]{1,0:T(8,128)(2,1)S(1)}, u32[]{:S(2)}, u32[]{:S(2)}) collective-permute-start(bf16[8,1024]{1,0:T(8,128)(2,1)S(1)} %get-tuple-element.20), channel_id=1, source_target_pairs={{0,32},{1,0},{2,34},{3,2},{4,36},{5,4},{6,38},{7,6},{8,40},{9,8},{... | collective-permute-start | bytes 49160 | tf_op jit(solution)/shard_map/ppermute | solution.py:72
  59.1 24.0 %collective-permute-start.3 = (bf16[8,1024]{1,0:T(8,128)(2,1)S(1)}, bf16[8,1024]{1,0:T(8,128)(2,1)S(1)}, u32[]{:S(2)}, u32[]{:S(2)}) collective-permute-start(bf16[8,1024]{1,0:T(8,128)(2,1)S(1)} %get-tuple-element.19), channel_id=1, source_target_pairs={{0,0},{1,32},{2,2},{3,34},{4,4},{5,36},{6,6},{7,38},{8,8},{9,40},{... | collective-permute-start | bytes 49160 | tf_op jit(solution)/shard_map/ppermute | solution.py:69
  84.2 33.5 %all-to-all-start.2 = ((bf16[32,8,2048]{2,1,0:T(8,128)(2,1)}), bf16[32,8,2048]{2,1,0:T(8,128)(2,1)S(1)}, u32[]{:S(2)}, u32[]{:S(2)}) async-start(bf16[32,8,2048]{2,1,0:T(8,128)(2,1)} %broadcast_in_dim.5), calls=%async_computation.2 | async-start | bytes 2097152 | tf_op jit(solution)/shard_map/all_to_all | solution.py:18
  89.5 45.2 %collective-permute-start.5 = (bf16[256,512]{1,0:T(8,128)(2,1)S(1)}, bf16[256,512]{1,0:T(8,128)(2,1)}, u32[]{:S(2)}, u32[]{:S(2)}) collective-permute-start(bf16[256,512]{1,0:T(8,128)(2,1)S(1)} %bitcast.21), channel_id=1, source_target_pairs={{0,1},{1,0},{2,3},{3,2},{4,5},{5,4},{6,7},{7,6},{8,9},{9,8},{10,11... | collective-permute-start | bytes 786440 | tf_op jit(solution)/shard_map/ppermute | solution.py:97
  121.8 12.9 %collective-permute-start.6 = (bf16[256,1024]{1,0:T(8,128)(2,1)}, bf16[256,1024]{1,0:T(8,128)(2,1)S(1)}, u32[]{:S(2)}, u32[]{:S(2)}) collective-permute-start(bf16[256,1024]{1,0:T(8,128)(2,1)} %get-tuple-element.16), channel_id=1, source_target_pairs={{0,1},{1,0},{2,3},{3,2},{4,5},{5,4},{6,7},{7,6},{8,9},{9,8},{10,11... | collective-permute-start | bytes 1572872 | tf_op jit(solution)/shard_map/ppermute | solution.py:99
  123.7 20.8 %all-to-all-start.3 = ((bf16[16,16,512]{2,1,0:T(8,128)(2,1)}), bf16[16,16,512]{2,1,0:T(8,128)(2,1)S(1)}, u32[]{:S(2)}, u32[]{:S(2)}) async-start(bf16[16,16,512]{2,1,0:T(8,128)(2,1)} %bitcast.23), calls=%async_computation.3 | async-start | bytes 524288 | tf_op jit(solution)/shard_map/all_to_all | solution.py:92
  128.4 5.6 %collective-permute-start.2 = (bf16[8,1024]{1,0:T(8,128)(2,1)S(1)}, bf16[8,1024]{1,0:T(8,128)(2,1)S(1)}, u32[]{:S(2)}, u32[]{:S(2)}) collective-permute-start(bf16[8,1024]{1,0:T(8,128)(2,1)S(1)} %get-tuple-element.22), channel_id=1, source_target_pairs={{32,0},{0,1},{34,2},{2,3},{36,4},{4,5},{38,6},{6,7},{40,8},{8,9},{... | collective-permute-start | bytes 49160 | tf_op jit(solution)/shard_map/ppermute | solution.py:85
  130.6 3.5 %collective-permute-start.1 = (bf16[8,1024]{1,0:T(8,128)(2,1)S(1)}, bf16[8,1024]{1,0:T(8,128)(2,1)S(1)}, u32[]{:S(2)}, u32[]{:S(2)}) collective-permute-start(bf16[8,1024]{1,0:T(8,128)(2,1)S(1)} %get-tuple-element.21), channel_id=1, source_target_pairs={{0,0},{32,1},{2,2},{34,3},{4,4},{36,5},{6,6},{38,7},{8,8},{40,9},{... | collective-permute-start | bytes 49160 | tf_op jit(solution)/shard_map/ppermute | solution.py:84

commit v5 on v4

--- a/solution.py
+++ b/solution.py
@@ -1,6 +1,8 @@
 import jax
 import jax.numpy as jnp
 from jax import lax
+from jax.experimental import pallas as pl
+from jax.experimental.pallas import tpu as pltpu
 from jax.sharding import PartitionSpec as P
 
 BF16 = jnp.bfloat16
@@ -22,6 +24,57 @@
 def send_shares(shares, axis, groups=None):
     got = lax.all_to_all(shares, axis, 0, 0, axis_index_groups=groups)
     return jnp.sum(got.astype(F32), axis=0)
+
+
+def in_vmem(array):
+    return pltpu.with_memory_space_constraint(array, pltpu.VMEM)
+
+
+def forward_kernel(features, own, other, out):
+    width = own.shape[1]
+    out[:, :width] = jnp.dot(features[...], own[...], preferred_element_type=F32).astype(BF16)
+    out[:, width:] = jnp.dot(features[...], other[...], preferred_element_type=F32).astype(BF16)
+
+
+WHOLE = pl.BlockSpec(memory_space=pltpu.VMEM)
+
+
+def times_weights(features, own, other, steps=2):
+    (batch, depth), width = features.shape, own.shape[1]
+    rows = batch // steps
+    return pl.pallas_call(
+        forward_kernel,
+        out_shape=jax.ShapeDtypeStruct((batch, 2 * width), BF16),
+        grid=(steps,),
+        in_specs=[pl.BlockSpec((rows, depth), lambda i: (i, 0)), WHOLE, WHOLE],
+        out_specs=pl.BlockSpec((rows, 2 * width), lambda i: (i, 0)),
+        name="times_weights",
+    )(features, in_vmem(own), in_vmem(other))
+
+
+def backward_kernel(slope, own, other, out):
+    width = own.shape[1]
+    dims = (((1,), (1,)), ((), ()))
+    total = lax.dot_general(slope[:, :width], own[...], dims, preferred_element_type=F32)
+    total += lax.dot_general(slope[:, width:], other[...], dims, preferred_element_type=F32)
+    out[...] = total.astype(BF16)
+
+
+def times_weights_back(slope, own, other, steps=2):
+    batch, (depth, width) = slope.shape[0], own.shape
+    block = depth // steps
+    return pl.pallas_call(
+        backward_kernel,
+        out_shape=jax.ShapeDtypeStruct((batch, depth), BF16),
+        grid=(steps,),
+        in_specs=[
+            WHOLE,
+            pl.BlockSpec((block, width), lambda i: (i, 0)),
+            pl.BlockSpec((block, width), lambda i: (i, 0)),
+        ],
+        out_specs=pl.BlockSpec((batch, block), lambda i: (0, i)),
+        name="times_weights_back",
+    )(in_vmem(slope), own, other)
 
 
 def either(flag, first, second, axis):
@@ -59,12 +112,9 @@
             "bim,mr->bir", interaction, projection, preferred_element_type=F32
         )
         local_features = local_features.astype(BF16).reshape(mine_b, -1)
-        local_features, weight_late = lax.optimization_barrier((local_features, weight))
         features = send_copies(local_features, "col", cores)
 
-        both_weights = jnp.concatenate(
-            [weight, lax.ppermute(weight_late, "col", swap)], 1
-        )
+        other_weight = lax.ppermute(weight, "col", swap)
         halves = act_grad.reshape(2, half, width)
         near = lax.ppermute(
             lax.dynamic_index_in_dim(halves, k, 0, False), ("row", "col"), spread
@@ -74,8 +124,8 @@
         )
         both_grads = either(h == k, near, far, 1).astype(F32)
 
-        partial = jnp.dot(features, both_weights, preferred_element_type=F32)
-        preact = send_shares(partial.astype(BF16).reshape(rows, half, -1), "row")
+        partial = times_weights(features, weight, other_weight)
+        preact = send_shares(partial.reshape(rows, half, -1), "row")
         slope_mine = (both_grads * silu_slope(preact)).astype(BF16)
         slope = send_copies(slope_mine, "row")
 
@@ -85,19 +135,24 @@
         far = lax.ppermute(acts[1], ("row", "col"), collect_far)
         activation = either(k == 0, near, far, 0)
 
-        partial_grad = lax.dot_general(
-            slope, both_weights, (((1,), (1,)), ((), ())), preferred_element_type=F32
-        ).astype(BF16)
+        other_features = lax.ppermute(features, "col", swap)
+        slope, activation, other_features = lax.optimization_barrier(
+            (slope, activation, other_features)
+        )
+        partial_grad = times_weights_back(slope, weight, other_weight)
         partial_grad, slope_late = lax.optimization_barrier((partial_grad, slope))
         grad_shares = lax.all_to_all(
             partial_grad.reshape(cols // 2, mine_b, -1),
             "col", 0, 0, axis_index_groups=cores,
         )
 
-        features_all = jnp.concatenate([features, lax.ppermute(features, "col", swap)])
-        slope_all = jnp.concatenate(
-            [slope_late[:, :width], lax.ppermute(slope_late[:, width:], "col", swap)]
-        )
+        features_all = jnp.concatenate([features, other_features])
+        gathered = [
+            lax.all_gather(piece, "col", axis_index_groups=[[c, c + 1] for c in range(0, cols, 2)])
+            for piece in jnp.split(slope_late[:, width:], 2)
+        ]
+        other_slope = jnp.concatenate([lax.dynamic_index_in_dim(g, 1 - k, 0, False) for g in gathered])
+        slope_all = jnp.concatenate([slope_late[:, :width], other_slope])
         weight_grad = lax.dot_general(
             features_all, slope_all, (((0,), (0,)), ((), ())), preferred_element_type=F32
         )

time: 146 us -> 139 us (0.952)
  blocking collectives: 0 us -> 40.8 us
  waiting for transfers between devices: 71.4 us -> 49.5 us
  starting transfers between devices: 52.5 us -> 33.9 us
  local copies, waits for them, and re-layouts: 7.9 us -> 1.38 us
  matrix products: 11 us -> 4.49 us
  Pallas kernels: 0 us -> 5.61 us
    all_to_all x0 -> x1, blocking collectives: none -> 36.4 us  [send_copies(): got = lax.all_to_all(copies, axis, 0, 0, axis_index_groups=groups)]
    all_to_all x2 -> x1, waiting for transfers between devices: 38.8 us -> 17.8 us  [send_copies(): got = lax.all_to_all(copies, axis, 0, 0, axis_index_groups=groups)]
    all_to_all x2 -> x1, starting transfers between devices: 26 us -> 5.29 us  [send_copies(): got = lax.all_to_all(copies, axis, 0, 0, axis_index_groups=groups)]
    dot_general x2 -> x0, matrix products: 6.34 us -> none  [the longest x1 3.3 us: shards(): partial = jnp.dot(features, both_weights, preferred_element_type=F32)]
    pallas_call x0 -> x2, Pallas kernels: none -> 5.61 us  [the longest x1 2.82 us: times_weights_back(): pl.pallas_call(backward_kernel, out_shape=jax.ShapeDtypeStruct((batch, de...]
    all_gather x0 -> x2, blocking collectives: none -> 4.36 us  [shards(): lax.all_gather(piece, 'col', axis_index_groups=[[c, c + 1] for c in range...]
    ppermute x1, starting transfers between devices: 2.13 us -> 4.73 us  [shards(): far = lax.ppermute(acts[1], ('row', 'col'), collect_far)]
    unnamed x7 -> x10, local copies, waits for them, and re-layouts: 2.62 us -> 0.03 us
  transfers between devices with their start and end apart: 11 -> 9, of which waited for: 5 -> 4; matrix products, arithmetic and copies ran while one was open for 8% -> 4% of each run, Pallas kernels for 0% -> 0%
where the time goes in v5:
time: 139 us; the launch traced here: 138 us
  waiting for transfers between devices  49.5 us (36%)
  blocking collectives  40.8 us (29%)
  starting transfers between devices  33.9 us (24%)
  Pallas kernels  5.61 us (4%)
  matrix products  4.49 us (3%)
  other arithmetic  1.49 us (1%)
    all_to_all x1, blocking collectives, send_copies(): got = lax.all_to_all(copies, axis, 0, 0, axis_index_groups=groups)  36.4 us
    all_to_all x1, waiting for transfers between devices, send_shares(): got = lax.all_to_all(shares, axis, 0, 0, axis_index_groups=groups)  21.9 us
    all_to_all x1, waiting for transfers between devices, send_copies(): got = lax.all_to_all(copies, axis, 0, 0, axis_index_groups=groups)  17.8 us
    all_to_all x1, starting transfers between devices, send_shares(): got = lax.all_to_all(shares, axis, 0, 0, axis_index_groups=groups)  9.27 us
    all_to_all x1, waiting for transfers between devices, shards(): lax.all_to_all(partial_grad.reshape(cols // 2, mine_b, -1), 'col', 0, 0,...  7.51 us
    all_to_all x1, starting transfers between devices, send_copies(): got = lax.all_to_all(copies, axis, 0, 0, axis_index_groups=groups)  5.29 us
    ppermute x1, starting transfers between devices, shards(): far = lax.ppermute(acts[1], ('row', 'col'), collect_far)  4.73 us
    all_to_all x1, starting transfers between devices, shards(): lax.all_to_all(partial_grad.reshape(cols // 2, mine_b, -1), 'col', 0, 0,...  4.65 us
  transfers between devices with their start and end apart: 9, of which 4 were waited for; matrix products, arithmetic and copies ran while one was open for 4% of the time, Pallas kernels for 0%

profile of v5, /device:TPU:32, one launch (start us, length us, event | category | flops | bytes accessed | tf_op | source)
XLA Modules:
  0.0 138.1 jit_solution(10691439757972254349)
XLA Ops:
  0.6 0.0 copy-start
  0.6 0.0 copy-start.1
  0.7 2.1 %collective-permute-start.2 = (bf16[512,1024]{1,0:T(8,128)(2,1)}, bf16[512,1024]{1,0:T(8,128)(2,1)S(1)}, u32[]{:S(2)}, u32[]{:S(2)}) collective-permute-start(bf16[512,1024]{1,0:T(8,128)(2,1)} %own.3), channel_id=1, source_target_pairs={{0,1},{1,0},{2,3},{3,2},{4,5},{5,4},{6,7},{7,6},{8,9},{9,8},{10,11... | collective-permute-start | bytes 3145736 | tf_op jit(solution)/shard_map/ppermute | solution.py:117
  2.7 2.4 %fusion.1 = bf16[16,8,64]{2,1,0:T(8,128)(2,1)S(1)} fusion(bf16[16,256,256]{2,1,0:T(8,128)(2,1)} %param.4, s32[]{:T(128)S(6)} %select_n.56, bf16[256,64]{0,1:T(8,128)(2,1)S(1)} %copy-done), kind=kOutput, calls=%fused_computation.3 | convolution fusion | flops 21012480 | bytes 2211844 | tf_op jit(solution)/shard_map/bim,mr->bir/dot_general | solution.py:111
  5.2 0.1 broadcast_in_dim.6
  5.3 36.4 %all_to_all.20 = bf16[16,16,512]{2,1,0:T(8,128)(2,1)} all-to-all(bf16[16,16,512]{2,1,0:T(8,128)(2,1)S(1)} %broadcast_in_dim.14), channel_id=1, replica_groups={{0,2,4,6,8,10,12,14,16,18,20,22,24,26,28,30},{1,3,5,7,9,11,13,15,17,19,..., dimensions={0} | all-to-all | bytes 524288 | tf_op jit(solution)/shard_map/all_to_all | solution.py:20
  41.8 0.0 collective-permute-done.2.other
  41.8 0.0 copy-start.4
  41.8 2.8 %times_weights.1 = bf16[256,2048]{1,0:T(8,128)(2,1)} custom-call(bf16[256,512]{1,0:T(8,128)(2,1)} %bitcast.25, bf16[512,1024]{1,0:T(8,128)(2,1)S(1)} %copy-done.1, bf16[512,1024]{1,0:T(8,128)(2,1)S(1)} %collective-permute-done.2.other), custom_call_target="tpu_custom_call" | custom-call | tf_op jit(solution)/shard_map/times_weights/pallas_call | solution.py:45
  44.6 9.3 %all-to-all-start.1 = ((bf16[32,8,2048]{2,1,0:T(8,128)(2,1)}), bf16[32,8,2048]{2,1,0:T(8,128)(2,1)S(1)}, u32[]{:S(2)}, u32[]{:S(2)}) async-start(bf16[32,8,2048]{2,1,0:T(8,128)(2,1)} %bitcast.22), calls=%async_computation.1 | async-start | bytes 2097152 | tf_op jit(solution)/shard_map/all_to_all | solution.py:25
  53.9 0.7 collective-permute-start
  54.6 4.6 %collective-permute-start.1 = (bf16[8,1024]{1,0:T(8,128)(2,1)S(1)}, bf16[8,1024]{1,0:T(8,128)(2,1)S(1)}, u32[]{:S(2)}, u32[]{:S(2)}) collective-permute-start(bf16[8,1024]{1,0:T(8,128)(2,1)S(1)} %get-tuple-element.26), channel_id=1, source_target_pairs={{0,32},{1,0},{2,34},{3,2},{4,36},{5,4},{6,38},{7,6},{8,40},{9,8},{... | collective-permute-start | bytes 49160 | tf_op jit(solution)/shard_map/ppermute | solution.py:122
  59.2 21.9 %all-to-all-done.1 = bf16[32,8,2048]{2,1,0:T(8,128)(2,1)S(1)} async-done(((bf16[32,8,2048]{2,1,0:T(8,128)(2,1)}), bf16[32,8,2048]{2,1,0:T(8,128)(2,1)S(1)}, u32[]{:S(2)}, u32[]{:S(2)}) %all-to-all-start.1) | async-done | bytes 1048608 | tf_op jit(solution)/shard_map/all_to_all | solution.py:25
  81.1 0.2 convert_reduce_fusion
  81.2 0.0 collective-permute-done
  81.2 0.0 collective-permute-done.1
  81.3 1.1 broadcast_in_dim.15
  82.4 5.3 %all-to-all-start.2 = ((bf16[32,8,2048]{2,1,0:T(8,128)(2,1)}), bf16[32,8,2048]{2,1,0:T(8,128)(2,1)S(1)}, u32[]{:S(2)}, u32[]{:S(2)}) async-start(bf16[32,8,2048]{2,1,0:T(8,128)(2,1)} %broadcast_in_dim.15), calls=%async_computation.2 | async-start | bytes 2097152 | tf_op jit(solution)/shard_map/all_to_all | solution.py:20
  87.7 1.9 %collective-permute-start.5 = (bf16[256,512]{1,0:T(8,128)(2,1)S(1)}, bf16[256,512]{1,0:T(8,128)(2,1)S(1)}, u32[]{:S(2)}, u32[]{:S(2)}) collective-permute-start(bf16[256,512]{1,0:T(8,128)(2,1)S(1)} %bitcast.26), channel_id=1, source_target_pairs={{0,1},{1,0},{2,3},{3,2},{4,5},{5,4},{6,7},{7,6},{8,9},{9,8},{10,11... | collective-permute-start | bytes 786440 | tf_op jit(solution)/shard_map/ppermute | solution.py:138
  89.7 0.7 collective-permute-start.3
  90.3 4.7 %collective-permute-start.4 = (bf16[8,1024]{1,0:T(8,128)(2,1)S(1)}, bf16[8,1024]{1,0:T(8,128)(2,1)S(1)}, u32[]{:S(2)}, u32[]{:S(2)}) collective-permute-start(bf16[8,1024]{1,0:T(8,128)(2,1)S(1)} %get-tuple-element.22), channel_id=1, source_target_pairs={{32,0},{0,1},{34,2},{2,3},{36,4},{4,5},{38,6},{6,7},{40,8},{8,9},{... | collective-permute-start | bytes 49160 | tf_op jit(solution)/shard_map/ppermute | solution.py:135
  95.1 0.0 collective-permute-done.3
  95.1 2.3 %collective-permute-done.4 = bf16[8,1024]{1,0:T(8,128)(2,1)S(1)} collective-permute-done((bf16[8,1024]{1,0:T(8,128)(2,1)S(1)}, bf16[8,1024]{1,0:T(8,128)(2,1)S(1)}, u32[]{:S(2)}, u32[]{:S(2)}) %collective-permute-start.4) | collective-permute-done | bytes 16416 | tf_op jit(solution)/shard_map/ppermute | solution.py:135
  97.4 0.6 maximum_select_fusion.2
  98.0 17.8 %all-to-all-done.2 = bf16[32,8,2048]{2,1,0:T(8,128)(2,1)S(1)} async-done(((bf16[32,8,2048]{2,1,0:T(8,128)(2,1)}), bf16[32,8,2048]{2,1,0:T(8,128)(2,1)S(1)}, u32[]{:S(2)}, u32[]{:S(2)}) %all-to-all-start.2) | async-done | bytes 1048608 | tf_op jit(solution)/shard_map/all_to_all | solution.py:20
  115.9 2.8 %times_weights_back.1 = bf16[256,512]{1,0:T(8,128)(2,1)} custom-call(bf16[256,2048]{1,0:T(8,128)(2,1)S(1)} %bitcast.19, bf16[512,1024]{1,0:T(8,128)(2,1)} %own.3, bf16[512,1024]{1,0:T(8,128)(2,1)} %copy-done.2), custom_call_target="tpu_custom_call" | custom-call | tf_op jit(solution)/shard_map/times_weights_back/pallas_call | solution.py:66
  118.8 4.6 %all-to-all-start.3 = ((bf16[16,16,512]{2,1,0:T(8,128)(2,1)}), bf16[16,16,512]{2,1,0:T(8,128)(2,1)S(1)}, u32[]{:S(2)}, u32[]{:S(2)}) async-start(bf16[16,16,512]{2,1,0:T(8,128)(2,1)} %bitcast.7), calls=%async_computation.3 | async-start | bytes 524288 | tf_op jit(solution)/shard_map/all_to_all | solution.py:144
  123.4 2.2 %all-gather = bf16[256,1024]{1,0:T(8,128)(2,1)S(1)} all-gather(bf16[128,1024]{1,0:T(8,128)(2,1)S(1)} %get-tuple-element.17), channel_id=2, replica_groups={{0,1},{2,3},{4,5},{6,7},{8,9},{10,11},{12,13},{14,15},{16,17},{18,19},{..., dimensions={0}, use_global_device_ids=true | all-gather | bytes 786432 | tf_op jit(solution)/shard_map/all_gather | solution.py:151
  125.7 2.2 %all-gather.1 = bf16[256,1024]{1,0:T(8,128)(2,1)S(1)} all-gather(bf16[128,1024]{1,0:T(8,128)(2,1)S(1)} %get-tuple-element.18), channel_id=3, replica_groups={{0,1},{2,3},{4,5},{6,7},{8,9},{10,11},{12,13},{14,15},{16,17},{18,19},{..., dimensions={0}, use_global_device_ids=true | all-gather | bytes 786432 | tf_op jit(solution)/shard_map/all_gather | solution.py:151
  127.9 2.0 %fusion.2 = f32[512,1024]{1,0:T(8,128)} fusion(bf16[128,1024]{1,0:T(8,128)(2,1)S(1)} %dynamic-slice_bitcast_fusion, bf16[128,1024]{1,0:T(8,128)(2,1)S(1)} %dynamic-slice_bitcast_fusion.1, bf16[256,1024]{1,0:T(8,128)(2,1)S(1)} %slice.24, bf16[256,512]{1,0:T(8,128)(2,1)S(1)} %collective-permute-done.5, bf16[256,512]{1,0:T(8,128)(2,1)S(1)} %bitcast.27), kind=kOutput, calls=%fused_computation.4 | convolution fusion | flops 541065216 | bytes 3670016 | tf_op jit(solution)/shard_map/dot_general | solution.py:156
  129.9 7.5 %all-to-all-done.3 = bf16[16,16,512]{2,1,0:T(8,128)(2,1)S(1)} async-done(((bf16[16,16,512]{2,1,0:T(8,128)(2,1)}), bf16[16,16,512]{2,1,0:T(8,128)(2,1)S(1)}, u32[]{:S(2)}, u32[]{:S(2)}) %all-to-all-start.3) | async-done | bytes 262176 | tf_op jit(solution)/shard_map/all_to_all | solution.py:144
  137.4 0.7 convert_reduce_fusion.1
  (18 shorter events, 0.2 us)
Async XLA Ops:
  0.6 2.1 %copy-start = (bf16[256,64]{0,1:T(8,128)(2,1)S(1)}, bf16[256,64]{0,1:T(8,128)(2,1)}, u32[]{:S(2)}) copy-start(bf16[256,64]{0,1:T(8,128)(2,1)} %param.5) | copy-start | bytes 98308
  0.6 41.1 %copy-start.1 = (bf16[512,1024]{1,0:T(8,128)(2,1)S(1)}, bf16[512,1024]{1,0:T(8,128)(2,1)}, u32[]{:S(2)}) copy-start(bf16[512,1024]{1,0:T(8,128)(2,1)} %own.3) | copy-start | bytes 3145732
  0.7 41.1 %collective-permute-start.2 = (bf16[512,1024]{1,0:T(8,128)(2,1)}, bf16[512,1024]{1,0:T(8,128)(2,1)S(1)}, u32[]{:S(2)}, u32[]{:S(2)}) collective-permute-start(bf16[512,1024]{1,0:T(8,128)(2,1)} %own.3), channel_id=1, source_target_pairs={{0,1},{1,0},{2,3},{3,2},{4,5},{5,4},{6,7},{7,6},{8,9},{9,8},{10,11... | collective-permute-start | bytes 3145736 | tf_op jit(solution)/shard_map/ppermute | solution.py:117
  41.8 2.8 %copy-start.2 = (bf16[512,1024]{1,0:T(8,128)(2,1)}, bf16[512,1024]{1,0:T(8,128)(2,1)S(1)}, u32[]{:S(2)}) copy-start(bf16[512,1024]{1,0:T(8,128)(2,1)S(1)} %collective-permute-done.2.other) | copy-start | bytes 3145732
  41.8 12.1 %copy-start.4 = (bf16[16,1024]{1,0:T(8,128)(2,1)S(1)}, bf16[16,1024]{1,0:T(8,128)(2,1)}, u32[]{:S(2)}) copy-start(bf16[16,1024]{1,0:T(8,128)(2,1)} %param.7) | copy-start | bytes 98308
  44.6 36.5 %all-to-all-start.1 = ((bf16[32,8,2048]{2,1,0:T(8,128)(2,1)}), bf16[32,8,2048]{2,1,0:T(8,128)(2,1)S(1)}, u32[]{:S(2)}, u32[]{:S(2)}) async-start(bf16[32,8,2048]{2,1,0:T(8,128)(2,1)} %bitcast.22), calls=%async_computation.1 | async-start | bytes 2097152 | tf_op jit(solution)/shard_map/all_to_all | solution.py:25
  53.9 27.3 %collective-permute-start = (bf16[8,1024]{1,0:T(8,128)(2,1)S(1)}, bf16[8,1024]{1,0:T(8,128)(2,1)S(1)}, u32[]{:S(2)}, u32[]{:S(2)}) collective-permute-start(bf16[8,1024]{1,0:T(8,128)(2,1)S(1)} %get-tuple-element.25), channel_id=1, source_target_pairs={{0,0},{1,32},{2,2},{3,34},{4,4},{5,36},{6,6},{7,38},{8,8},{9,40},{... | collective-permute-start | bytes 49160 | tf_op jit(solution)/shard_map/ppermute | solution.py:119
  54.6 26.7 %collective-permute-start.1 = (bf16[8,1024]{1,0:T(8,128)(2,1)S(1)}, bf16[8,1024]{1,0:T(8,128)(2,1)S(1)}, u32[]{:S(2)}, u32[]{:S(2)}) collective-permute-start(bf16[8,1024]{1,0:T(8,128)(2,1)S(1)} %get-tuple-element.26), channel_id=1, source_target_pairs={{0,32},{1,0},{2,34},{3,2},{4,36},{5,4},{6,38},{7,6},{8,40},{9,8},{... | collective-permute-start | bytes 49160 | tf_op jit(solution)/shard_map/ppermute | solution.py:122
  59.2 28.5 %copy-start.3 = (bf16[16,16,512]{2,1,0:T(8,128)(2,1)S(1)}, bf16[16,16,512]{2,1,0:T(8,128)(2,1)}, u32[]{:S(2)}) copy-start(bf16[16,16,512]{2,1,0:T(8,128)(2,1)} %all_to_all.20) | copy-start | bytes 786436
  82.4 33.5 %all-to-all-start.2 = ((bf16[32,8,2048]{2,1,0:T(8,128)(2,1)}), bf16[32,8,2048]{2,1,0:T(8,128)(2,1)S(1)}, u32[]{:S(2)}, u32[]{:S(2)}) async-start(bf16[32,8,2048]{2,1,0:T(8,128)(2,1)} %broadcast_in_dim.15), calls=%async_computation.2 | async-start | bytes 2097152 | tf_op jit(solution)/shard_map/all_to_all | solution.py:20
  87.7 10.3 %collective-permute-start.5 = (bf16[256,512]{1,0:T(8,128)(2,1)S(1)}, bf16[256,512]{1,0:T(8,128)(2,1)S(1)}, u32[]{:S(2)}, u32[]{:S(2)}) collective-permute-start(bf16[256,512]{1,0:T(8,128)(2,1)S(1)} %bitcast.26), channel_id=1, source_target_pairs={{0,1},{1,0},{2,3},{3,2},{4,5},{5,4},{6,7},{7,6},{8,9},{9,8},{10,11... | collective-permute-start | bytes 786440 | tf_op jit(solution)/shard_map/ppermute | solution.py:138
  89.7 5.4 %collective-permute-start.3 = (bf16[8,1024]{1,0:T(8,128)(2,1)S(1)}, bf16[8,1024]{1,0:T(8,128)(2,1)S(1)}, u32[]{:S(2)}, u32[]{:S(2)}) collective-permute-start(bf16[8,1024]{1,0:T(8,128)(2,1)S(1)} %get-tuple-element.21), channel_id=1, source_target_pairs={{0,0},{32,1},{2,2},{34,3},{4,4},{36,5},{6,6},{38,7},{8,8},{40,9},{... | collective-permute-start | bytes 49160 | tf_op jit(solution)/shard_map/ppermute | solution.py:134
  90.3 7.1 %collective-permute-start.4 = (bf16[8,1024]{1,0:T(8,128)(2,1)S(1)}, bf16[8,1024]{1,0:T(8,128)(2,1)S(1)}, u32[]{:S(2)}, u32[]{:S(2)}) collective-permute-start(bf16[8,1024]{1,0:T(8,128)(2,1)S(1)} %get-tuple-element.22), channel_id=1, source_target_pairs={{32,0},{0,1},{34,2},{2,3},{36,4},{4,5},{38,6},{6,7},{40,8},{8,9},{... | collective-permute-start | bytes 49160 | tf_op jit(solution)/shard_map/ppermute | solution.py:135
  118.8 18.6 %all-to-all-start.3 = ((bf16[16,16,512]{2,1,0:T(8,128)(2,1)}), bf16[16,16,512]{2,1,0:T(8,128)(2,1)S(1)}, u32[]{:S(2)}, u32[]{:S(2)}) async-start(bf16[16,16,512]{2,1,0:T(8,128)(2,1)} %bitcast.7), calls=%async_computation.3 | async-start | bytes 524288 | tf_op jit(solution)/shard_map/all_to_all | solution.py:144

commit v6 on v4

v6 whole, which is shorter than its diff:
```python
import jax
import jax.numpy as jnp
from jax import lax
from jax.experimental import pallas as pl
from jax.experimental.pallas import tpu as pltpu
from jax.sharding import PartitionSpec as P

BF16 = jnp.bfloat16
F32 = jnp.float32


def silu_slope(values):
    sig = jax.nn.sigmoid(values)
    return sig * (1.0 + values * (1.0 - sig))


def send_copies(part, axis, groups=None):
    size = len(groups[0]) if groups else lax.axis_size(axis)
    copies = jnp.broadcast_to(part[None], (size, *part.shape))
    got = lax.all_to_all(copies, axis, 0, 0, axis_index_groups=groups)
    return got.reshape(-1, got.shape[-1])


def in_vmem(array):
    return pltpu.with_memory_space_constraint(array, pltpu.VMEM)


WHOLE = pl.BlockSpec(memory_space=pltpu.VMEM)
ANY = pl.BlockSpec(memory_space=pl.ANY)
SCALAR = pl.BlockSpec(memory_space=pltpu.SMEM)


def fetch_other(core, pairs, other, sems):
    rows = other.shape[0] // len(pairs)
    copies = []
    for i, pair in enumerate(pairs):
        copies.append(
            pltpu.make_async_copy(
                pair.at[1 - core], other.at[pl.ds(i * rows, rows)], sems.at[i]
            )
        )
        copies[-1].start()
    return copies


def forward_kernel(core, features, own, *rest):
    *pairs, out, other, left, right, sems, out_sems = rest
    width = own.shape[1]
    copies = fetch_other(core[0], pairs, other, sems)
    left[...] = jnp.dot(features[...], own[...], preferred_element_type=F32).astype(BF16)
    send_left = pltpu.make_async_copy(left, out.at[:, pl.ds(0, width)], out_sems.at[0])
    send_left.start()
    for copy in copies:
        copy.wait()
    right[...] = jnp.dot(features[...], other[...], preferred_element_type=F32).astype(BF16)
    send_right = pltpu.make_async_copy(right, out.at[:, pl.ds(width, width)], out_sems.at[1])
    send_right.start()
    send_left.wait()
    send_right.wait()


def times_weights(core, features, own, pairs):
    batch, (depth, width) = features.shape[0], own.shape
    return pl.pallas_call(
        forward_kernel,
        out_shape=jax.ShapeDtypeStruct((batch, 2 * width), BF16),
        in_specs=[SCALAR, WHOLE, WHOLE] + [ANY] * len(pairs),
        out_specs=ANY,
        scratch_shapes=[
            pltpu.VMEM((depth, width), BF16),
            pltpu.VMEM((batch, width), BF16),
            pltpu.VMEM((batch, width), BF16),
            pltpu.SemaphoreType.DMA((len(pairs),)),
            pltpu.SemaphoreType.DMA((2,)),
        ],
        name="times_weights",
    )(core, in_vmem(features), in_vmem(own), *pairs)


def backward_kernel(core, slope, own_in, *rest):
    *pairs, out, first, second, own, other, sems, own_sems, out_sems = rest
    width, rows = own.shape[1], own.shape[0] // len(pairs)
    half = first.shape[0]
    own_copies = []
    for i in range(len(pairs)):
        piece = pl.ds(i * rows, rows)
        own_copies.append(
            pltpu.make_async_copy(own_in.at[piece], own.at[piece], own_sems.at[i])
        )
        own_copies[-1].start()
    copies = fetch_other(core[0], pairs, other, sems)
    gives = [
        pltpu.make_async_copy(
            slope.at[pl.ds(i * half, half), pl.ds(width, width)], give, out_sems.at[i]
        )
        for i, give in enumerate((first, second))
    ]
    for give in gives:
        give.start()
    dims = (((1,), (1,)), ((), ()))
    for i in range(0, len(pairs), 2):
        piece = pl.ds(i * rows, 2 * rows)
        for copy in own_copies[i : i + 2] + copies[i : i + 2]:
            copy.wait()
        total = lax.dot_general(
            slope[:, :width], own[piece], dims, preferred_element_type=F32
        ) + lax.dot_general(
            slope[:, width:], other[piece], dims, preferred_element_type=F32
        )
        out[:, piece] = total.astype(BF16)
    for give in gives:
        give.wait()


def times_weights_back(core, slope, own, pairs):
    batch, (depth, width) = slope.shape[0], own.shape
    return pl.pallas_call(
        backward_kernel,
        out_shape=[jax.ShapeDtypeStruct((batch, depth), BF16)]
        + [jax.ShapeDtypeStruct((batch // 2, width), BF16)] * 2,
        in_specs=[SCALAR, WHOLE, ANY] + [ANY] * len(pairs),
        out_specs=[WHOLE, ANY, ANY],
        scratch_shapes=[
            pltpu.VMEM((depth, width), BF16),
            pltpu.VMEM((depth, width), BF16),
            pltpu.SemaphoreType.DMA((len(pairs),)),
            pltpu.SemaphoreType.DMA((len(pairs),)),
            pltpu.SemaphoreType.DMA((2,)),
        ],
        name="times_weights_back",
    )(core, in_vmem(slope), own, *pairs)


def weight_grad_kernel(core, features, other_features, slope, *rest):
    *pairs, out, other, sems = rest
    width = other.shape[1]
    copies = fetch_other(core[0], pairs, other, sems)
    for copy in copies:
        copy.wait()
    dims = (((0,), (0,)), ((), ()))
    out[...] = lax.dot_general(
        features[...], slope[:, :width], dims, preferred_element_type=F32
    ) + lax.dot_general(
        other_features[...], other[...], dims, preferred_element_type=F32
    )


def weight_grad_of(core, features, other_features, slope, pairs):
    depth, (batch, both) = features.shape[1], slope.shape
    return pl.pallas_call(
        weight_grad_kernel,
        out_shape=jax.ShapeDtypeStruct((depth, both // 2), F32),
        in_specs=[SCALAR, WHOLE, WHOLE, WHOLE] + [ANY] * len(pairs),
        out_specs=WHOLE,
        scratch_shapes=[
            pltpu.VMEM((batch, both // 2), BF16),
            pltpu.SemaphoreType.DMA((len(pairs),)),
        ],
        name="weight_grad",
    )(core, features, other_features, in_vmem(slope), *pairs)


def activate_kernel(shares, grads, acts, copies, slope, sem):
    preact = shares[0].astype(F32)
    for i in range(1, shares.shape[0]):
        preact += shares[i].astype(F32)
    acts[...] = jax.nn.silu(preact).astype(BF16)
    slope[...] = (grads[...].astype(F32) * silu_slope(preact)).astype(BF16)
    sends = [
        pltpu.make_async_copy(slope, copies.at[i], sem.at[i])
        for i in range(copies.shape[0])
    ]
    for send in sends:
        send.start()
    for send in sends:
        send.wait()


def activate(shares, grads):
    return pl.pallas_call(
        activate_kernel,
        out_shape=[
            jax.ShapeDtypeStruct(shares.shape[1:], BF16),
            jax.ShapeDtypeStruct(shares.shape, BF16),
        ],
        in_specs=[WHOLE, WHOLE],
        out_specs=[WHOLE, ANY],
        scratch_shapes=[
            pltpu.VMEM(shares.shape[1:], BF16),
            pltpu.SemaphoreType.DMA((shares.shape[0],)),
        ],
        name="activate",
    )(in_vmem(shares), in_vmem(grads))


def either(flag, first, second, axis):
    return jnp.where(
        flag,
        jnp.concatenate([first, second], axis),
        jnp.concatenate([second, first], axis),
    )


def make_shards(rows, cols):
    cores = [list(range(core, cols, 2)) for core in range(2)]
    chips = [[c, c + 1] for c in range(0, cols, 2)]
    swap = [(c, c ^ 1) for c in range(cols)]
    spread, spread_far = [], []
    for row in range(rows):
        for col in range(cols):
            h, k = row % 2, col % 2
            spread.append((row * cols + col, (row - h + k) * cols + col - k + h))
            spread_far.append((row * cols + col, (row - h + 1 - k) * cols + col - k + h))
    collect = [(b, a) for a, b in spread]
    collect_far = [(b, a) for a, b in spread_far]

    def shards(embeddings, projection, weight, act_grad):
        mine_b, width = act_grad.shape
        half = mine_b // 2
        emb_rows = weight.shape[0] // projection.shape[1]
        emb_first = lax.axis_index("row") * emb_rows
        h, k = lax.axis_index("row") % 2, lax.axis_index("col") % 2

        mine_emb = lax.dynamic_slice_in_dim(embeddings, emb_first, emb_rows, 1)
        interaction = jnp.einsum(
            "bid,bmd->bim", mine_emb, embeddings, preferred_element_type=F32
        ).astype(BF16)
        local_features = jnp.einsum(
            "bim,mr->bir", interaction, projection, preferred_element_type=F32
        )
        local_features = local_features.astype(BF16).reshape(mine_b, -1)
        features = send_copies(local_features, "col", cores)

        weight_pairs = [
            lax.all_gather(piece, "col", axis_index_groups=chips)
            for piece in jnp.split(weight, 4)
        ]
        core = k.reshape(1)
        halves = act_grad.reshape(2, half, width)
        near = lax.ppermute(
            lax.dynamic_index_in_dim(halves, k, 0, False), ("row", "col"), spread
        )
        far = lax.ppermute(
            lax.dynamic_index_in_dim(halves, 1 - k, 0, False), ("row", "col"), spread_far
        )
        both_grads = either(h == k, near, far, 1)

        partial = times_weights(core, features, weight, weight_pairs)
        shares = lax.all_to_all(partial.reshape(rows, half, -1), "row", 0, 0)
        acts, slope_copies = activate(shares, both_grads)
        slope = lax.all_to_all(slope_copies, "row", 0, 0).reshape(rows * half, -1)

        acts = either(h == k, acts[:, :width], acts[:, width:], 0).reshape(2, half, width)
        near = lax.ppermute(acts[0], ("row", "col"), collect)
        far = lax.ppermute(acts[1], ("row", "col"), collect_far)
        activation = either(k == 0, near, far, 0)

        other_features = lax.ppermute(features, "col", swap)
        slope, activation, other_features = lax.optimization_barrier(
            (slope, activation, other_features)
        )
        partial_grad, *given = times_weights_back(core, slope, weight, weight_pairs)
        grad_shares = lax.all_to_all(
            partial_grad.reshape(cols // 2, mine_b, -1),
            "col", 0, 0, axis_index_groups=cores,
        )

        slope_pairs = [
            lax.all_gather(piece, "col", axis_index_groups=chips) for piece in given
        ]
        weight_grad = weight_grad_of(core, features, other_features, slope, slope_pairs)
        grad_shares, weight_grad = lax.optimization_barrier((grad_shares, weight_grad))
        feature_grad = jnp.sum(grad_shares.astype(F32), axis=0)
        return (activation, weight_grad, feature_grad)

    return shards


def solution(mesh):
    return jax.shard_map(
        make_shards(mesh.shape["row"], mesh.shape["col"]),
        mesh=mesh,
        in_specs=(P("col", None, None), P(), P("row", "col"), P("row", "col")),
        out_specs=(P("row", "col"), P("row", "col"), P("col", "row")),
        check_vma=False,
    )
```

time: 146 us -> 149 us (1.021)
  the two profiles are of different devices: /device:TPU:32 before, /device:TPU:113 now
where the time goes in v6:
time: 149 us; the launch traced here: 148 us
  starting transfers between devices  61.3 us (41%)
  waiting for transfers between devices  40.7 us (27%)
  blocking collectives  25.6 us (17%)
  Pallas kernels  13.2 us (9%)
  local copies, waits for them, and re-layouts  3.34 us (2%)
  matrix products  1.52 us (1%)
    all_gather x6, blocking collectives, shards(): lax.all_gather(piece, 'col', axis_index_groups=chips)  25.6 us
    all_to_all x1, starting transfers between devices, send_copies(): got = lax.all_to_all(copies, axis, 0, 0, axis_index_groups=groups)  21.5 us
    all_to_all x1, waiting for transfers between devices, shards(): shares = lax.all_to_all(partial.reshape(rows, half, -1), 'row', 0, 0)  21.4 us
    all_to_all x1, waiting for transfers between devices, shards(): slope = lax.all_to_all(slope_copies, 'row', 0, 0).reshape(rows * half, -1)  16.3 us
    all_to_all x1, starting transfers between devices, shards(): lax.all_to_all(partial_grad.reshape(cols // 2, mine_b, -1), 'col', 0, 0,...  11.5 us
    all_to_all x1, starting transfers between devices, shards(): shares = lax.all_to_all(partial.reshape(rows, half, -1), 'row', 0, 0)  9.63 us
    ppermute x1, starting transfers between devices, shards(): lax.ppermute(lax.dynamic_index_in_dim(halves, 1 - k, 0, False), ('row', '...  5.22 us
    all_to_all x1, starting transfers between devices, shards(): slope = lax.all_to_all(slope_copies, 'row', 0, 0).reshape(rows * half, -1)  5.17 us
  transfers between devices with their start and end apart: 9, of which 4 were waited for; matrix products, arithmetic and copies ran while one was open for 1% of the time, Pallas kernels for 3%

profile of v6, /device:TPU:113, one launch (start us, length us, event | category | flops | bytes accessed | tf_op | source)
XLA Modules:
  0.0 147.9 jit_solution(9072305667497891843)
XLA Ops:
  0.6 0.0 copy-start
  0.7 1.6 %copy-done = bf16[16,256,256]{2,1,0:T(8,128)(2,1)S(1)} copy-done((bf16[16,256,256]{2,1,0:T(8,128)(2,1)S(1)}, bf16[16,256,256]{2,1,0:T(8,128)(2,1)}, u32[]{:S(2)}) %copy-start) | copy-done | bytes 2097176
  2.2 1.5 %fusion.1 = bf16[16,8,64]{2,1,0:T(8,128)(2,1)S(1)} fusion(bf16[16,256,256]{2,1,0:T(8,128)(2,1)S(1)} %copy-done, s32[]{:T(128)S(6)} %select_n.44, bf16[256,64]{0,1:T(8,128)(2,1)} %param.5), kind=kOutput, calls=%fused_computation.2 | convolution fusion | flops 21012480 | bytes 2211844 | tf_op jit(solution)/shard_map/bim,mr->bir/dot_general | solution.py:228
  3.8 0.1 broadcast_in_dim.7
  3.9 0.7 broadcast_in_dim.8
  4.6 21.5 %all-to-all-start = ((bf16[16,16,512]{2,1,0:T(8,128)(2,1)}), bf16[16,16,512]{2,1,0:T(8,128)(2,1)}, u32[]{:S(2)}, u32[]{:S(2)}) async-start(bf16[16,16,512]{2,1,0:T(8,128)(2,1)} %broadcast_in_dim.8), calls=%async_computation | async-start | bytes 524288 | tf_op jit(solution)/shard_map/all_to_all | solution.py:20
  26.1 0.9 fusion.7
  27.0 5.0 %all-gather.3 = bf16[256,1024]{1,0:T(8,128)(2,1)} all-gather(bf16[128,1024]{1,0:T(8,128)(2,1)} %get-tuple-element.23), channel_id=5, replica_groups={{0,1},{2,3},{4,5},{6,7},{8,9},{10,11},{12,13},{14,15},{16,17},{18,19},{..., dimensions={0}, use_global_device_ids=true | all-gather | bytes 786432 | tf_op jit(solution)/shard_map/all_gather | solution.py:235
  32.0 3.8 %all-gather.2 = bf16[256,1024]{1,0:T(8,128)(2,1)} all-gather(bf16[128,1024]{1,0:T(8,128)(2,1)} %get-tuple-element.24), channel_id=4, replica_groups={{0,1},{2,3},{4,5},{6,7},{8,9},{10,11},{12,13},{14,15},{16,17},{18,19},{..., dimensions={0}, use_global_device_ids=true | all-gather | bytes 786432 | tf_op jit(solution)/shard_map/all_gather | solution.py:235
  35.8 4.0 %all-gather.1 = bf16[256,1024]{1,0:T(8,128)(2,1)} all-gather(bf16[128,1024]{1,0:T(8,128)(2,1)} %get-tuple-element.25), channel_id=3, replica_groups={{0,1},{2,3},{4,5},{6,7},{8,9},{10,11},{12,13},{14,15},{16,17},{18,19},{..., dimensions={0}, use_global_device_ids=true | all-gather | bytes 786432 | tf_op jit(solution)/shard_map/all_gather | solution.py:235
  39.9 2.3 %all-gather = bf16[256,1024]{1,0:T(8,128)(2,1)} all-gather(bf16[128,1024]{1,0:T(8,128)(2,1)S(1)} %get-tuple-element.26), channel_id=2, replica_groups={{0,1},{2,3},{4,5},{6,7},{8,9},{10,11},{12,13},{14,15},{16,17},{18,19},{..., dimensions={0}, use_global_device_ids=true | all-gather | bytes 786432 | tf_op jit(solution)/shard_map/all_gather | solution.py:235
  42.2 3.4 %times_weights.1 = bf16[256,2048]{1,0:T(8,128)(2,1)} custom-call(s32[1]{0:T(128)} %bitcast.core, bf16[256,512]{1,0:T(8,128)(2,1)} %bitcast.2.features, bf16[512,1024]{1,0:T(8,128)(2,1)S(1)} %copy-done.2, bf16[2,128,1024]{2,1,0:T(8,128)(2,1)} %bitcast.28, bf16[2,128,1024]{2,1,0:T(8,128)(2,1)} %bitcast.26, bf16[2,128,1024]{2,1,0:T(8,128)(2,1)} %bitcast.24, ...), custom_call_target="tpu_custom_call" | custom-call | tf_op jit(solution)/shard_map/times_weights/pallas_call | solution.py:64
  45.6 0.0 copy-start.4
  45.6 9.6 %all-to-all-start.1 = ((bf16[32,8,2048]{2,1,0:T(8,128)(2,1)}), bf16[32,8,2048]{2,1,0:T(8,128)(2,1)S(1)}, u32[]{:S(2)}, u32[]{:S(2)}) async-start(bf16[32,8,2048]{2,1,0:T(8,128)(2,1)} %bitcast.30), calls=%async_computation.1 | async-start | bytes 2097152 | tf_op jit(solution)/shard_map/all_to_all | solution.py:249
  55.3 0.7 collective-permute-start
  56.0 5.2 %collective-permute-start.1 = (bf16[8,1024]{1,0:T(8,128)(2,1)S(1)}, bf16[8,1024]{1,0:T(8,128)(2,1)S(1)}, u32[]{:S(2)}, u32[]{:S(2)}) collective-permute-start(bf16[8,1024]{1,0:T(8,128)(2,1)S(1)} %get-tuple-element.32), channel_id=1, source_target_pairs={{0,32},{1,0},{2,34},{3,2},{4,36},{5,4},{6,38},{7,6},{8,40},{9,8},{... | collective-permute-start | bytes 49160 | tf_op jit(solution)/shard_map/ppermute | solution.py:243
  61.2 0.8 collective-permute-done.1
  62.1 21.4 %all-to-all-done.1.shares = bf16[32,8,2048]{2,1,0:T(8,128)(2,1)S(1)} async-done(((bf16[32,8,2048]{2,1,0:T(8,128)(2,1)}), bf16[32,8,2048]{2,1,0:T(8,128)(2,1)S(1)}, u32[]{:S(2)}, u32[]{:S(2)}) %all-to-all-start.1) | async-done | bytes 1048608 | tf_op jit(solution)/shard_map/all_to_all | solution.py:249
  83.4 2.0 %activate.1 = (bf16[8,2048]{1,0:T(8,128)(2,1)}, bf16[32,8,2048]{2,1,0:T(8,128)(2,1)}) custom-call(bf16[32,8,2048]{2,1,0:T(8,128)(2,1)S(1)} %all-to-all-done.1.shares, bf16[8,2048]{1,0:T(8,128)(2,1)S(1)} %maximum_select_fusion.grads), custom_call_target="tpu_custom_call" | custom-call | tf_op jit(solution)/shard_map/activate/pallas_call | solution.py:180
  85.5 5.2 %all-to-all-start.2 = ((bf16[32,8,2048]{2,1,0:T(8,128)(2,1)}), bf16[32,8,2048]{2,1,0:T(8,128)(2,1)S(1)}, u32[]{:S(2)}, u32[]{:S(2)}) async-start(bf16[32,8,2048]{2,1,0:T(8,128)(2,1)} %get-tuple-element.13), calls=%async_computation.2 | async-start | bytes 2097152 | tf_op jit(solution)/shard_map/all_to_all | solution.py:251
  90.6 3.2 %collective-permute-start.4 = (bf16[256,512]{1,0:T(8,128)(2,1)}, bf16[256,512]{1,0:T(8,128)(2,1)S(1)}, u32[]{:S(2)}, u32[]{:S(2)}) collective-permute-start(bf16[256,512]{1,0:T(8,128)(2,1)} %bitcast.2.features), channel_id=1, source_target_pairs={{0,1},{1,0},{2,3},{3,2},{4,5},{5,4},{6,7},{7,6},{8,9},{9,8},{10,11... | collective-permute-start | bytes 786440 | tf_op jit(solution)/shard_map/ppermute | solution.py:258
  93.9 0.7 collective-permute-start.2
  94.6 3.8 %collective-permute-start.3 = (bf16[8,1024]{1,0:T(8,128)(2,1)S(1)}, bf16[8,1024]{1,0:T(8,128)(2,1)S(1)}, u32[]{:S(2)}, u32[]{:S(2)}) collective-permute-start(bf16[8,1024]{1,0:T(8,128)(2,1)S(1)} %get-tuple-element.28), channel_id=1, source_target_pairs={{32,0},{0,1},{34,2},{2,3},{36,4},{4,5},{38,6},{6,7},{40,8},{8,9},{... | collective-permute-start | bytes 49160 | tf_op jit(solution)/shard_map/ppermute | solution.py:255
  98.4 2.2 %collective-permute-done.3 = bf16[8,1024]{1,0:T(8,128)(2,1)S(1)} collective-permute-done((bf16[8,1024]{1,0:T(8,128)(2,1)S(1)}, bf16[8,1024]{1,0:T(8,128)(2,1)S(1)}, u32[]{:S(2)}, u32[]{:S(2)}) %collective-permute-start.3) | collective-permute-done | bytes 16416 | tf_op jit(solution)/shard_map/ppermute | solution.py:255
  100.6 0.6 maximum_select_fusion.2
  101.2 16.3 %all-to-all-done.2 = bf16[32,8,2048]{2,1,0:T(8,128)(2,1)S(1)} async-done(((bf16[32,8,2048]{2,1,0:T(8,128)(2,1)}), bf16[32,8,2048]{2,1,0:T(8,128)(2,1)S(1)}, u32[]{:S(2)}, u32[]{:S(2)}) %all-to-all-start.2) | async-done | bytes 1048608 | tf_op jit(solution)/shard_map/all_to_all | solution.py:251
  117.6 3.6 %times_weights_back.1 = (bf16[256,512]{1,0:T(8,128)(2,1)}, bf16[128,1024]{1,0:T(8,128)(2,1)}, bf16[128,1024]{1,0:T(8,128)(2,1)}) custom-call(s32[1]{0:T(128)} %bitcast.core, bf16[256,2048]{1,0:T(8,128)(2,1)S(1)} %bitcast.20, bf16[512,1024]{1,0:T(8,128)(2,1)} %own_in.1, bf16[2,128,1024]{2,1,0:T(8,128)(2,1)} %bitcast.29, bf16[2,128,1024]{2,1,0:T(8,128)(2,1)} %bitcast.27, ...), custom_call_target="tpu_custom_call" | custom-call | tf_op jit(solution)/shard_map/times_weights_back/pallas_call | solution.py:117
  121.2 11.5 %all-to-all-start.3 = ((bf16[16,16,512]{2,1,0:T(8,128)(2,1)}), bf16[16,16,512]{2,1,0:T(8,128)(2,1)S(1)}, u32[]{:S(2)}, u32[]{:S(2)}) async-start(bf16[16,16,512]{2,1,0:T(8,128)(2,1)} %bitcast.33), calls=%async_computation.3 | async-start | bytes 524288 | tf_op jit(solution)/shard_map/all_to_all | solution.py:263
  132.7 6.6 %all-gather.4 = bf16[256,1024]{1,0:T(8,128)(2,1)} all-gather(bf16[128,1024]{1,0:T(8,128)(2,1)} %get-tuple-element.19), channel_id=6, replica_groups={{0,1},{2,3},{4,5},{6,7},{8,9},{10,11},{12,13},{14,15},{16,17},{18,19},{..., dimensions={0}, use_global_device_ids=true | all-gather | bytes 786432 | tf_op jit(solution)/shard_map/all_gather | solution.py:269
  139.3 3.8 %all-gather.5 = bf16[256,1024]{1,0:T(8,128)(2,1)} all-gather(bf16[128,1024]{1,0:T(8,128)(2,1)} %get-tuple-element.20), channel_id=7, replica_groups={{0,1},{2,3},{4,5},{6,7},{8,9},{10,11},{12,13},{14,15},{16,17},{18,19},{..., dimensions={0}, use_global_device_ids=true | all-gather | bytes 786432 | tf_op jit(solution)/shard_map/all_gather | solution.py:269
  143.1 4.1 %weight_grad.1 = f32[512,1024]{1,0:T(8,128)} custom-call(s32[1]{0:T(128)} %bitcast.core, bf16[256,512]{1,0:T(8,128)(2,1)} %bitcast.2.features, bf16[256,512]{1,0:T(8,128)(2,1)} %copy-done.3, bf16[256,2048]{1,0:T(8,128)(2,1)S(1)} %bitcast.21, bf16[2,128,1024]{2,1,0:T(8,128)(2,1)} %bitcast.31, bf16[2,128,1024]{2,1,0:T(8,128)(2,1)} %bitcast.32), custom_call_target="tpu_custom_call" | custom-call | tf_op jit(solution)/shard_map/weight_grad/pallas_call | solution.py:150
  147.2 0.7 convert_reduce_fusion
  (19 shorter events, 0.1 us)
Async XLA Ops:
  0.6 1.6 %copy-start = (bf16[16,256,256]{2,1,0:T(8,128)(2,1)S(1)}, bf16[16,256,256]{2,1,0:T(8,128)(2,1)}, u32[]{:S(2)}) copy-start(bf16[16,256,256]{2,1,0:T(8,128)(2,1)} %param.4) | copy-start | bytes 6291460
  0.6 25.5 %copy-start.1 = (bf16[512,1024]{1,0:T(8,128)(2,1)S(1)}, bf16[512,1024]{1,0:T(8,128)(2,1)}, u32[]{:S(2)}) copy-start(bf16[512,1024]{1,0:T(8,128)(2,1)} %own_in.1) | copy-start | bytes 3145732
  4.6 37.6 %all-to-all-start = ((bf16[16,16,512]{2,1,0:T(8,128)(2,1)}), bf16[16,16,512]{2,1,0:T(8,128)(2,1)}, u32[]{:S(2)}, u32[]{:S(2)}) async-start(bf16[16,16,512]{2,1,0:T(8,128)(2,1)} %broadcast_in_dim.8), calls=%async_computation | async-start | bytes 524288 | tf_op jit(solution)/shard_map/all_to_all | solution.py:20
  27.0 15.2 %copy-start.2 = (bf16[512,1024]{1,0:T(8,128)(2,1)S(1)}, bf16[512,1024]{1,0:T(8,128)(2,1)}, u32[]{:S(2)}) copy-start(bf16[512,1024]{1,0:T(8,128)(2,1)} %own_in.1) | copy-start | bytes 3145732
  45.6 9.7 %copy-start.4 = (bf16[16,1024]{1,0:T(8,128)(2,1)S(1)}, bf16[16,1024]{1,0:T(8,128)(2,1)}, u32[]{:S(2)}) copy-start(bf16[16,1024]{1,0:T(8,128)(2,1)} %param.7) | copy-start | bytes 98308
  45.6 37.8 %all-to-all-start.1 = ((bf16[32,8,2048]{2,1,0:T(8,128)(2,1)}), bf16[32,8,2048]{2,1,0:T(8,128)(2,1)S(1)}, u32[]{:S(2)}, u32[]{:S(2)}) async-start(bf16[32,8,2048]{2,1,0:T(8,128)(2,1)} %bitcast.30), calls=%async_computation.1 | async-start | bytes 2097152 | tf_op jit(solution)/shard_map/all_to_all | solution.py:249
  55.3 5.9 %collective-permute-start = (bf16[8,1024]{1,0:T(8,128)(2,1)S(1)}, bf16[8,1024]{1,0:T(8,128)(2,1)S(1)}, u32[]{:S(2)}, u32[]{:S(2)}) collective-permute-start(bf16[8,1024]{1,0:T(8,128)(2,1)S(1)} %get-tuple-element.31), channel_id=1, source_target_pairs={{0,0},{1,32},{2,2},{3,34},{4,4},{5,36},{6,6},{7,38},{8,8},{9,40},{... | collective-permute-start | bytes 49160 | tf_op jit(solution)/shard_map/ppermute | solution.py:240
  56.0 6.1 %collective-permute-start.1 = (bf16[8,1024]{1,0:T(8,128)(2,1)S(1)}, bf16[8,1024]{1,0:T(8,128)(2,1)S(1)}, u32[]{:S(2)}, u32[]{:S(2)}) collective-permute-start(bf16[8,1024]{1,0:T(8,128)(2,1)S(1)} %get-tuple-element.32), channel_id=1, source_target_pairs={{0,32},{1,0},{2,34},{3,2},{4,36},{5,4},{6,38},{7,6},{8,40},{9,8},{... | collective-permute-start | bytes 49160 | tf_op jit(solution)/shard_map/ppermute | solution.py:243
  85.4 8.4 %copy-start.5 = (bf16[8,2048]{1,0:T(8,128)(2,1)S(1)}, bf16[8,2048]{1,0:T(8,128)(2,1)}, u32[]{:S(2)}) copy-start(bf16[8,2048]{1,0:T(8,128)(2,1)} %get-tuple-element.14) | copy-start | bytes 98308
  85.5 32.1 %all-to-all-start.2 = ((bf16[32,8,2048]{2,1,0:T(8,128)(2,1)}), bf16[32,8,2048]{2,1,0:T(8,128)(2,1)S(1)}, u32[]{:S(2)}, u32[]{:S(2)}) async-start(bf16[32,8,2048]{2,1,0:T(8,128)(2,1)} %get-tuple-element.13), calls=%async_computation.2 | async-start | bytes 2097152 | tf_op jit(solution)/shard_map/all_to_all | solution.py:251
  90.6 10.6 %collective-permute-start.4 = (bf16[256,512]{1,0:T(8,128)(2,1)}, bf16[256,512]{1,0:T(8,128)(2,1)S(1)}, u32[]{:S(2)}, u32[]{:S(2)}) collective-permute-start(bf16[256,512]{1,0:T(8,128)(2,1)} %bitcast.2.features), channel_id=1, source_target_pairs={{0,1},{1,0},{2,3},{3,2},{4,5},{5,4},{6,7},{7,6},{8,9},{9,8},{10,11... | collective-permute-start | bytes 786440 | tf_op jit(solution)/shard_map/ppermute | solution.py:258
  93.9 4.5 %collective-permute-start.2 = (bf16[8,1024]{1,0:T(8,128)(2,1)S(1)}, bf16[8,1024]{1,0:T(8,128)(2,1)S(1)}, u32[]{:S(2)}, u32[]{:S(2)}) collective-permute-start(bf16[8,1024]{1,0:T(8,128)(2,1)S(1)} %get-tuple-element.27), channel_id=1, source_target_pairs={{0,0},{32,1},{2,2},{34,3},{4,4},{36,5},{6,6},{38,7},{8,8},{40,9},{... | collective-permute-start | bytes 49160 | tf_op jit(solution)/shard_map/ppermute | solution.py:254
  94.6 6.1 %collective-permute-start.3 = (bf16[8,1024]{1,0:T(8,128)(2,1)S(1)}, bf16[8,1024]{1,0:T(8,128)(2,1)S(1)}, u32[]{:S(2)}, u32[]{:S(2)}) collective-permute-start(bf16[8,1024]{1,0:T(8,128)(2,1)S(1)} %get-tuple-element.28), channel_id=1, source_target_pairs={{32,0},{0,1},{34,2},{2,3},{36,4},{4,5},{38,6},{6,7},{40,8},{8,9},{... | collective-permute-start | bytes 49160 | tf_op jit(solution)/shard_map/ppermute | solution.py:255
  101.2 20.0 %copy-start.3 = (bf16[256,512]{1,0:T(8,128)(2,1)}, bf16[256,512]{1,0:T(8,128)(2,1)S(1)}, u32[]{:S(2)}) copy-start(bf16[256,512]{1,0:T(8,128)(2,1)S(1)} %collective-permute-done.4.other_features) | copy-start | bytes 786436
  121.2 26.0 %all-to-all-start.3 = ((bf16[16,16,512]{2,1,0:T(8,128)(2,1)}), bf16[16,16,512]{2,1,0:T(8,128)(2,1)S(1)}, u32[]{:S(2)}, u32[]{:S(2)}) async-start(bf16[16,16,512]{2,1,0:T(8,128)(2,1)} %bitcast.33), calls=%async_computation.3 | async-start | bytes 524288 | tf_op jit(solution)/shard_map/all_to_all | solution.py:263

commit v7 on v5

--- a/solution.py
+++ b/solution.py
@@ -30,32 +30,42 @@
     return pltpu.with_memory_space_constraint(array, pltpu.VMEM)
 
 
-def forward_kernel(features, own, other, out):
-    width = own.shape[1]
-    out[:, :width] = jnp.dot(features[...], own[...], preferred_element_type=F32).astype(BF16)
-    out[:, width:] = jnp.dot(features[...], other[...], preferred_element_type=F32).astype(BF16)
-
-
 WHOLE = pl.BlockSpec(memory_space=pltpu.VMEM)
 
 
-def times_weights(features, own, other, steps=2):
+def forward_kernel(features, own, other, out):
+    step, block = pl.program_id(0), out.shape[1]
+    for i in range(2 * own.shape[1] // block):
+        weight, first = (own, i * block) if i * block < own.shape[1] else (other, i * block - own.shape[1])
+
+        @pl.when(step == i)
+        def _(weight=weight, first=first):
+            part = weight[:, first : first + block]
+            out[...] = jnp.dot(features[...], part, preferred_element_type=F32).astype(BF16)
+
+
+def times_weights(features, own, other, blocks=2):
     (batch, depth), width = features.shape, own.shape[1]
-    rows = batch // steps
+    block = width // blocks
     return pl.pallas_call(
         forward_kernel,
         out_shape=jax.ShapeDtypeStruct((batch, 2 * width), BF16),
-        grid=(steps,),
-        in_specs=[pl.BlockSpec((rows, depth), lambda i: (i, 0)), WHOLE, WHOLE],
-        out_specs=pl.BlockSpec((rows, 2 * width), lambda i: (i, 0)),
+        grid=(2 * blocks,),
+        in_specs=[
+            pl.BlockSpec((batch, depth), lambda i: (0, 0)),
+            WHOLE,
+            WHOLE,
+        ],
+        out_specs=pl.BlockSpec((batch, block), lambda i: (0, i)),
         name="times_weights",
     )(features, in_vmem(own), in_vmem(other))
 
 
 def backward_kernel(slope, own, other, out):
-    width = own.shape[1]
+    width, block = own.shape[1], out.shape[1]
+    mine = own[pl.ds(pl.multiple_of(pl.program_id(0) * block, block), block)]
     dims = (((1,), (1,)), ((), ()))
-    total = lax.dot_general(slope[:, :width], own[...], dims, preferred_element_type=F32)
+    total = lax.dot_general(slope[:, :width], mine, dims, preferred_element_type=F32)
     total += lax.dot_general(slope[:, width:], other[...], dims, preferred_element_type=F32)
     out[...] = total.astype(BF16)
 
@@ -69,12 +79,12 @@
         grid=(steps,),
         in_specs=[
             WHOLE,
-            pl.BlockSpec((block, width), lambda i: (i, 0)),
+            WHOLE,
             pl.BlockSpec((block, width), lambda i: (i, 0)),
         ],
         out_specs=pl.BlockSpec((batch, block), lambda i: (0, i)),
         name="times_weights_back",
-    )(in_vmem(slope), own, other)
+    )(in_vmem(slope), in_vmem(own), other)
 
 
 def either(flag, first, second, axis):

time: 139 us -> 139 us (level)
  no operation moved by 1% of the time
where the time goes in v7:
time: 139 us
  waiting for transfers between devices  49.5 us (36%)
  blocking collectives  40.8 us (29%)
  starting transfers between devices  33.9 us (24%)
  Pallas kernels  6.19 us (4%)
  matrix products  4.5 us (3%)
  other arithmetic  1.49 us (1%)
    all_to_all x1, blocking collectives, send_copies(): got = lax.all_to_all(copies, axis, 0, 0, axis_index_groups=groups)  36.4 us
    all_to_all x1, waiting for transfers between devices, send_shares(): got = lax.all_to_all(shares, axis, 0, 0, axis_index_groups=groups)  21.9 us
    all_to_all x1, waiting for transfers between devices, send_copies(): got = lax.all_to_all(copies, axis, 0, 0, axis_index_groups=groups)  17.8 us
    all_to_all x1, starting transfers between devices, send_shares(): got = lax.all_to_all(shares, axis, 0, 0, axis_index_groups=groups)  9.27 us
    all_to_all x1, waiting for transfers between devices, shards(): lax.all_to_all(partial_grad.reshape(cols // 2, mine_b, -1), 'col', 0, 0,...  7.5 us
    all_to_all x1, starting transfers between devices, send_copies(): got = lax.all_to_all(copies, axis, 0, 0, axis_index_groups=groups)  5.28 us
    ppermute x1, starting transfers between devices, shards(): far = lax.ppermute(acts[1], ('row', 'col'), collect_far)  4.73 us
    all_to_all x1, starting transfers between devices, shards(): lax.all_to_all(partial_grad.reshape(cols // 2, mine_b, -1), 'col', 0, 0,...  4.65 us
  transfers between devices with their start and end apart: 9, of which 4 were waited for; matrix products, arithmetic and copies ran while one was open for 4% of the time, Pallas kernels for 0%

profile of v7, /device:TPU:32, one launch (start us, length us, event | category | flops | bytes accessed | tf_op | source)
XLA Modules:
  0.0 138.6 jit_solution(11504443118725425670)
XLA Ops:
  0.6 0.0 copy-start
  0.7 2.1 %collective-permute-start.2 = (bf16[512,1024]{1,0:T(8,128)(2,1)}, bf16[512,1024]{1,0:T(8,128)(2,1)S(1)}, u32[]{:S(2)}, u32[]{:S(2)}) collective-permute-start(bf16[512,1024]{1,0:T(8,128)(2,1)} %own.3), channel_id=1, source_target_pairs={{0,1},{1,0},{2,3},{3,2},{4,5},{5,4},{6,7},{7,6},{8,9},{9,8},{10,11... | collective-permute-start | bytes 3145736 | tf_op jit(solution)/shard_map/ppermute | solution.py:127
  2.7 2.4 %fusion.1 = bf16[16,8,64]{2,1,0:T(8,128)(2,1)S(1)} fusion(bf16[16,256,256]{2,1,0:T(8,128)(2,1)} %param.4, s32[]{:T(128)S(6)} %select_n.56, bf16[256,64]{0,1:T(8,128)(2,1)S(1)} %copy-done), kind=kOutput, calls=%fused_computation.3 | convolution fusion | flops 21012480 | bytes 2211844 | tf_op jit(solution)/shard_map/bim,mr->bir/dot_general | solution.py:121
  5.2 0.1 broadcast_in_dim.6
  5.3 36.4 %all_to_all.20 = bf16[16,16,512]{2,1,0:T(8,128)(2,1)} all-to-all(bf16[16,16,512]{2,1,0:T(8,128)(2,1)S(1)} %broadcast_in_dim.14), channel_id=1, replica_groups={{0,2,4,6,8,10,12,14,16,18,20,22,24,26,28,30},{1,3,5,7,9,11,13,15,17,19,..., dimensions={0} | all-to-all | bytes 524288 | tf_op jit(solution)/shard_map/all_to_all | solution.py:20
  41.7 0.0 collective-permute-done.2.other
  41.8 0.0 copy-start.4
  41.8 3.5 %times_weights.1 = bf16[256,2048]{1,0:T(8,128)(2,1)} custom-call(bf16[256,512]{1,0:T(8,128)(2,1)} %bitcast.25, bf16[512,1024]{1,0:T(8,128)(2,1)S(1)} %copy-done.1, bf16[512,1024]{1,0:T(8,128)(2,1)S(1)} %collective-permute-done.2.other), custom_call_target="tpu_custom_call" | custom-call | tf_op jit(solution)/shard_map/times_weights/pallas_call | solution.py:50
  45.3 9.3 %all-to-all-start.1 = ((bf16[32,8,2048]{2,1,0:T(8,128)(2,1)}), bf16[32,8,2048]{2,1,0:T(8,128)(2,1)S(1)}, u32[]{:S(2)}, u32[]{:S(2)}) async-start(bf16[32,8,2048]{2,1,0:T(8,128)(2,1)} %bitcast.22), calls=%async_computation.1 | async-start | bytes 2097152 | tf_op jit(solution)/shard_map/all_to_all | solution.py:25
  54.6 0.7 collective-permute-start
  55.3 4.6 %collective-permute-start.1 = (bf16[8,1024]{1,0:T(8,128)(2,1)S(1)}, bf16[8,1024]{1,0:T(8,128)(2,1)S(1)}, u32[]{:S(2)}, u32[]{:S(2)}) collective-permute-start(bf16[8,1024]{1,0:T(8,128)(2,1)S(1)} %get-tuple-element.26), channel_id=1, source_target_pairs={{0,32},{1,0},{2,34},{3,2},{4,36},{5,4},{6,38},{7,6},{8,40},{9,8},{... | collective-permute-start | bytes 49160 | tf_op jit(solution)/shard_map/ppermute | solution.py:132
  60.0 21.9 %all-to-all-done.1 = bf16[32,8,2048]{2,1,0:T(8,128)(2,1)S(1)} async-done(((bf16[32,8,2048]{2,1,0:T(8,128)(2,1)}), bf16[32,8,2048]{2,1,0:T(8,128)(2,1)S(1)}, u32[]{:S(2)}, u32[]{:S(2)}) %all-to-all-start.1) | async-done | bytes 1048608 | tf_op jit(solution)/shard_map/all_to_all | solution.py:25
  81.8 0.2 convert_reduce_fusion
  82.0 0.0 collective-permute-done
  82.0 0.0 collective-permute-done.1
  82.0 1.1 broadcast_in_dim.15
  83.1 5.3 %all-to-all-start.2 = ((bf16[32,8,2048]{2,1,0:T(8,128)(2,1)}), bf16[32,8,2048]{2,1,0:T(8,128)(2,1)S(1)}, u32[]{:S(2)}, u32[]{:S(2)}) async-start(bf16[32,8,2048]{2,1,0:T(8,128)(2,1)} %broadcast_in_dim.15), calls=%async_computation.2 | async-start | bytes 2097152 | tf_op jit(solution)/shard_map/all_to_all | solution.py:20
  88.4 1.9 %collective-permute-start.5 = (bf16[256,512]{1,0:T(8,128)(2,1)S(1)}, bf16[256,512]{1,0:T(8,128)(2,1)S(1)}, u32[]{:S(2)}, u32[]{:S(2)}) collective-permute-start(bf16[256,512]{1,0:T(8,128)(2,1)S(1)} %bitcast.26), channel_id=1, source_target_pairs={{0,1},{1,0},{2,3},{3,2},{4,5},{5,4},{6,7},{7,6},{8,9},{9,8},{10,11... | collective-permute-start | bytes 786440 | tf_op jit(solution)/shard_map/ppermute | solution.py:148
  90.4 0.7 collective-permute-start.3
  91.1 4.7 %collective-permute-start.4 = (bf16[8,1024]{1,0:T(8,128)(2,1)S(1)}, bf16[8,1024]{1,0:T(8,128)(2,1)S(1)}, u32[]{:S(2)}, u32[]{:S(2)}) collective-permute-start(bf16[8,1024]{1,0:T(8,128)(2,1)S(1)} %get-tuple-element.22), channel_id=1, source_target_pairs={{32,0},{0,1},{34,2},{2,3},{36,4},{4,5},{38,6},{6,7},{40,8},{8,9},{... | collective-permute-start | bytes 49160 | tf_op jit(solution)/shard_map/ppermute | solution.py:145
  95.8 0.0 collective-permute-done.3
  95.8 2.3 %collective-permute-done.4 = bf16[8,1024]{1,0:T(8,128)(2,1)S(1)} collective-permute-done((bf16[8,1024]{1,0:T(8,128)(2,1)S(1)}, bf16[8,1024]{1,0:T(8,128)(2,1)S(1)}, u32[]{:S(2)}, u32[]{:S(2)}) %collective-permute-start.4) | collective-permute-done | bytes 16416 | tf_op jit(solution)/shard_map/ppermute | solution.py:145
  98.1 0.6 maximum_select_fusion.2
  98.8 0.0 collective-permute-done.5
  98.8 17.8 %all-to-all-done.2 = bf16[32,8,2048]{2,1,0:T(8,128)(2,1)S(1)} async-done(((bf16[32,8,2048]{2,1,0:T(8,128)(2,1)}), bf16[32,8,2048]{2,1,0:T(8,128)(2,1)S(1)}, u32[]{:S(2)}, u32[]{:S(2)}) %all-to-all-start.2) | async-done | bytes 1048608 | tf_op jit(solution)/shard_map/all_to_all | solution.py:20
  116.6 2.7 %times_weights_back.1 = bf16[256,512]{1,0:T(8,128)(2,1)} custom-call(bf16[256,2048]{1,0:T(8,128)(2,1)S(1)} %bitcast.19, bf16[512,1024]{1,0:T(8,128)(2,1)S(1)} %copy-done.1, bf16[512,1024]{1,0:T(8,128)(2,1)} %copy-done.2), custom_call_target="tpu_custom_call" | custom-call | tf_op jit(solution)/shard_map/times_weights_back/pallas_call | solution.py:76
  119.4 4.6 %all-to-all-start.3 = ((bf16[16,16,512]{2,1,0:T(8,128)(2,1)}), bf16[16,16,512]{2,1,0:T(8,128)(2,1)S(1)}, u32[]{:S(2)}, u32[]{:S(2)}) async-start(bf16[16,16,512]{2,1,0:T(8,128)(2,1)} %bitcast.7), calls=%async_computation.3 | async-start | bytes 524288 | tf_op jit(solution)/shard_map/all_to_all | solution.py:154
  124.0 2.2 %all-gather = bf16[256,1024]{1,0:T(8,128)(2,1)S(1)} all-gather(bf16[128,1024]{1,0:T(8,128)(2,1)S(1)} %get-tuple-element.17), channel_id=2, replica_groups={{0,1},{2,3},{4,5},{6,7},{8,9},{10,11},{12,13},{14,15},{16,17},{18,19},{..., dimensions={0}, use_global_device_ids=true | all-gather | bytes 786432 | tf_op jit(solution)/shard_map/all_gather | solution.py:161
  126.2 2.2 %all-gather.1 = bf16[256,1024]{1,0:T(8,128)(2,1)S(1)} all-gather(bf16[128,1024]{1,0:T(8,128)(2,1)S(1)} %get-tuple-element.18), channel_id=3, replica_groups={{0,1},{2,3},{4,5},{6,7},{8,9},{10,11},{12,13},{14,15},{16,17},{18,19},{..., dimensions={0}, use_global_device_ids=true | all-gather | bytes 786432 | tf_op jit(solution)/shard_map/all_gather | solution.py:161
  128.4 2.1 %fusion.2 = f32[512,1024]{1,0:T(8,128)} fusion(bf16[128,1024]{1,0:T(8,128)(2,1)S(1)} %dynamic-slice_bitcast_fusion, bf16[128,1024]{1,0:T(8,128)(2,1)S(1)} %dynamic-slice_bitcast_fusion.1, bf16[256,1024]{1,0:T(8,128)(2,1)S(1)} %slice.24, bf16[256,512]{1,0:T(8,128)(2,1)S(1)} %collective-permute-done.5, bf16[256,512]{1,0:T(8,128)(2,1)S(1)} %bitcast.27), kind=kOutput, calls=%fused_computation.4 | convolution fusion | flops 541065216 | bytes 3670016 | tf_op jit(solution)/shard_map/dot_general | solution.py:166
  130.5 7.5 %all-to-all-done.3 = bf16[16,16,512]{2,1,0:T(8,128)(2,1)S(1)} async-done(((bf16[16,16,512]{2,1,0:T(8,128)(2,1)}), bf16[16,16,512]{2,1,0:T(8,128)(2,1)S(1)}, u32[]{:S(2)}, u32[]{:S(2)}) %all-to-all-start.3) | async-done | bytes 262176 | tf_op jit(solution)/shard_map/all_to_all | solution.py:154
  138.0 0.7 convert_reduce_fusion.1
  (18 shorter events, 0.2 us)
Async XLA Ops:
  0.6 2.1 %copy-start = (bf16[256,64]{0,1:T(8,128)(2,1)S(1)}, bf16[256,64]{0,1:T(8,128)(2,1)}, u32[]{:S(2)}) copy-start(bf16[256,64]{0,1:T(8,128)(2,1)} %param.5) | copy-start | bytes 98308
  0.6 41.1 %copy-start.1 = (bf16[512,1024]{1,0:T(8,128)(2,1)S(1)}, bf16[512,1024]{1,0:T(8,128)(2,1)}, u32[]{:S(2)}) copy-start(bf16[512,1024]{1,0:T(8,128)(2,1)} %own.3) | copy-start | bytes 3145732
  0.7 41.1 %collective-permute-start.2 = (bf16[512,1024]{1,0:T(8,128)(2,1)}, bf16[512,1024]{1,0:T(8,128)(2,1)S(1)}, u32[]{:S(2)}, u32[]{:S(2)}) collective-permute-start(bf16[512,1024]{1,0:T(8,128)(2,1)} %own.3), channel_id=1, source_target_pairs={{0,1},{1,0},{2,3},{3,2},{4,5},{5,4},{6,7},{7,6},{8,9},{9,8},{10,11... | collective-permute-start | bytes 3145736 | tf_op jit(solution)/shard_map/ppermute | solution.py:127
  41.8 3.5 %copy-start.2 = (bf16[512,1024]{1,0:T(8,128)(2,1)}, bf16[512,1024]{1,0:T(8,128)(2,1)S(1)}, u32[]{:S(2)}) copy-start(bf16[512,1024]{1,0:T(8,128)(2,1)S(1)} %collective-permute-done.2.other) | copy-start | bytes 3145732
  41.8 12.8 %copy-start.4 = (bf16[16,1024]{1,0:T(8,128)(2,1)S(1)}, bf16[16,1024]{1,0:T(8,128)(2,1)}, u32[]{:S(2)}) copy-start(bf16[16,1024]{1,0:T(8,128)(2,1)} %param.7) | copy-start | bytes 98308
  45.3 36.5 %all-to-all-start.1 = ((bf16[32,8,2048]{2,1,0:T(8,128)(2,1)}), bf16[32,8,2048]{2,1,0:T(8,128)(2,1)S(1)}, u32[]{:S(2)}, u32[]{:S(2)}) async-start(bf16[32,8,2048]{2,1,0:T(8,128)(2,1)} %bitcast.22), calls=%async_computation.1 | async-start | bytes 2097152 | tf_op jit(solution)/shard_map/all_to_all | solution.py:25
  54.6 27.3 %collective-permute-start = (bf16[8,1024]{1,0:T(8,128)(2,1)S(1)}, bf16[8,1024]{1,0:T(8,128)(2,1)S(1)}, u32[]{:S(2)}, u32[]{:S(2)}) collective-permute-start(bf16[8,1024]{1,0:T(8,128)(2,1)S(1)} %get-tuple-element.25), channel_id=1, source_target_pairs={{0,0},{1,32},{2,2},{3,34},{4,4},{5,36},{6,6},{7,38},{8,8},{9,40},{... | collective-permute-start | bytes 49160 | tf_op jit(solution)/shard_map/ppermute | solution.py:129
  55.3 26.7 %collective-permute-start.1 = (bf16[8,1024]{1,0:T(8,128)(2,1)S(1)}, bf16[8,1024]{1,0:T(8,128)(2,1)S(1)}, u32[]{:S(2)}, u32[]{:S(2)}) collective-permute-start(bf16[8,1024]{1,0:T(8,128)(2,1)S(1)} %get-tuple-element.26), channel_id=1, source_target_pairs={{0,32},{1,0},{2,34},{3,2},{4,36},{5,4},{6,38},{7,6},{8,40},{9,8},{... | collective-permute-start | bytes 49160 | tf_op jit(solution)/shard_map/ppermute | solution.py:132
  60.0 28.5 %copy-start.3 = (bf16[16,16,512]{2,1,0:T(8,128)(2,1)S(1)}, bf16[16,16,512]{2,1,0:T(8,128)(2,1)}, u32[]{:S(2)}) copy-start(bf16[16,16,512]{2,1,0:T(8,128)(2,1)} %all_to_all.20) | copy-start | bytes 786436
  83.1 33.5 %all-to-all-start.2 = ((bf16[32,8,2048]{2,1,0:T(8,128)(2,1)}), bf16[32,8,2048]{2,1,0:T(8,128)(2,1)S(1)}, u32[]{:S(2)}, u32[]{:S(2)}) async-start(bf16[32,8,2048]{2,1,0:T(8,128)(2,1)} %broadcast_in_dim.15), calls=%async_computation.2 | async-start | bytes 2097152 | tf_op jit(solution)/shard_map/all_to_all | solution.py:20
  88.4 10.3 %collective-permute-start.5 = (bf16[256,512]{1,0:T(8,128)(2,1)S(1)}, bf16[256,512]{1,0:T(8,128)(2,1)S(1)}, u32[]{:S(2)}, u32[]{:S(2)}) collective-permute-start(bf16[256,512]{1,0:T(8,128)(2,1)S(1)} %bitcast.26), channel_id=1, source_target_pairs={{0,1},{1,0},{2,3},{3,2},{4,5},{5,4},{6,7},{7,6},{8,9},{9,8},{10,11... | collective-permute-start | bytes 786440 | tf_op jit(solution)/shard_map/ppermute | solution.py:148
  90.4 5.4 %collective-permute-start.3 = (bf16[8,1024]{1,0:T(8,128)(2,1)S(1)}, bf16[8,1024]{1,0:T(8,128)(2,1)S(1)}, u32[]{:S(2)}, u32[]{:S(2)}) collective-permute-start(bf16[8,1024]{1,0:T(8,128)(2,1)S(1)} %get-tuple-element.21), channel_id=1, source_target_pairs={{0,0},{32,1},{2,2},{34,3},{4,4},{36,5},{6,6},{38,7},{8,8},{40,9},{... | collective-permute-start | bytes 49160 | tf_op jit(solution)/shard_map/ppermute | solution.py:144
  91.1 7.1 %collective-permute-start.4 = (bf16[8,1024]{1,0:T(8,128)(2,1)S(1)}, bf16[8,1024]{1,0:T(8,128)(2,1)S(1)}, u32[]{:S(2)}, u32[]{:S(2)}) collective-permute-start(bf16[8,1024]{1,0:T(8,128)(2,1)S(1)} %get-tuple-element.22), channel_id=1, source_target_pairs={{32,0},{0,1},{34,2},{2,3},{36,4},{4,5},{38,6},{6,7},{40,8},{8,9},{... | collective-permute-start | bytes 49160 | tf_op jit(solution)/shard_map/ppermute | solution.py:145
  119.4 18.6 %all-to-all-start.3 = ((bf16[16,16,512]{2,1,0:T(8,128)(2,1)}), bf16[16,16,512]{2,1,0:T(8,128)(2,1)S(1)}, u32[]{:S(2)}, u32[]{:S(2)}) async-start(bf16[16,16,512]{2,1,0:T(8,128)(2,1)} %bitcast.7), calls=%async_computation.3 | async-start | bytes 524288 | tf_op jit(solution)/shard_map/all_to_all | solution.py:154

commit v8 on v5

--- a/solution.py
+++ b/solution.py
@@ -30,32 +30,33 @@
     return pltpu.with_memory_space_constraint(array, pltpu.VMEM)
 
 
-def forward_kernel(features, own, other, out):
-    width = own.shape[1]
-    out[:, :width] = jnp.dot(features[...], own[...], preferred_element_type=F32).astype(BF16)
-    out[:, width:] = jnp.dot(features[...], other[...], preferred_element_type=F32).astype(BF16)
-
-
 WHOLE = pl.BlockSpec(memory_space=pltpu.VMEM)
 
 
+def forward_kernel(features, own, other, out):
+    width, rows = own.shape[1], out.shape[0]
+    mine = features[pl.ds(pl.multiple_of(pl.program_id(0) * rows, rows), rows)]
+    out[:, :width] = jnp.dot(mine, own[...], preferred_element_type=F32).astype(BF16)
+    out[:, width:] = jnp.dot(mine, other[...], preferred_element_type=F32).astype(BF16)
+
+
 def times_weights(features, own, other, steps=2):
-    (batch, depth), width = features.shape, own.shape[1]
-    rows = batch // steps
+    batch, width = features.shape[0], own.shape[1]
     return pl.pallas_call(
         forward_kernel,
         out_shape=jax.ShapeDtypeStruct((batch, 2 * width), BF16),
         grid=(steps,),
-        in_specs=[pl.BlockSpec((rows, depth), lambda i: (i, 0)), WHOLE, WHOLE],
-        out_specs=pl.BlockSpec((rows, 2 * width), lambda i: (i, 0)),
+        in_specs=[WHOLE, WHOLE, WHOLE],
+        out_specs=pl.BlockSpec((batch // steps, 2 * width), lambda i: (i, 0)),
         name="times_weights",
-    )(features, in_vmem(own), in_vmem(other))
+    )(in_vmem(features), in_vmem(own), in_vmem(other))
 
 
 def backward_kernel(slope, own, other, out):
-    width = own.shape[1]
+    width, block = own.shape[1], out.shape[1]
+    mine = own[pl.ds(pl.multiple_of(pl.program_id(0) * block, block), block)]
     dims = (((1,), (1,)), ((), ()))
-    total = lax.dot_general(slope[:, :width], own[...], dims, preferred_element_type=F32)
+    total = lax.dot_general(slope[:, :width], mine, dims, preferred_element_type=F32)
     total += lax.dot_general(slope[:, width:], other[...], dims, preferred_element_type=F32)
     out[...] = total.astype(BF16)
 
@@ -69,12 +70,12 @@
         grid=(steps,),
         in_specs=[
             WHOLE,
-            pl.BlockSpec((block, width), lambda i: (i, 0)),
+            WHOLE,
             pl.BlockSpec((block, width), lambda i: (i, 0)),
         ],
         out_specs=pl.BlockSpec((batch, block), lambda i: (0, i)),
         name="times_weights_back",
-    )(in_vmem(slope), own, other)
+    )(in_vmem(slope), in_vmem(own), other)
 
 
 def either(flag, first, second, axis):
@@ -112,6 +113,7 @@
             "bim,mr->bir", interaction, projection, preferred_element_type=F32
         )
         local_features = local_features.astype(BF16).reshape(mine_b, -1)
+        local_features, own = lax.optimization_barrier((local_features, weight))
         features = send_copies(local_features, "col", cores)
 
         other_weight = lax.ppermute(weight, "col", swap)
@@ -124,7 +126,7 @@
         )
         both_grads = either(h == k, near, far, 1).astype(F32)
 
-        partial = times_weights(features, weight, other_weight)
+        partial = times_weights(features, own, other_weight)
         preact = send_shares(partial.reshape(rows, half, -1), "row")
         slope_mine = (both_grads * silu_slope(preact)).astype(BF16)
         slope = send_copies(slope_mine, "row")
@@ -139,7 +141,7 @@
         slope, activation, other_features = lax.optimization_barrier(
             (slope, activation, other_features)
         )
-        partial_grad = times_weights_back(slope, weight, other_weight)
+        partial_grad = times_weights_back(slope, own, other_weight)
         partial_grad, slope_late = lax.optimization_barrier((partial_grad, slope))
         grad_shares = lax.all_to_all(
             partial_grad.reshape(cols // 2, mine_b, -1),

time: 139 us -> 137 us (0.986)
  no operation moved by 1% of the time
where the time goes in v8:
time: 137 us
  waiting for transfers between devices  49.6 us (36%)
  blocking collectives  40.7 us (30%)
  starting transfers between devices  33.9 us (25%)
  matrix products  4.49 us (3%)
  Pallas kernels  4.4 us (3%)
  other arithmetic  1.49 us (1%)
  local copies, waits for them, and re-layouts  1.37 us (1%)
    all_to_all x1, blocking collectives, send_copies(): got = lax.all_to_all(copies, axis, 0, 0, axis_index_groups=groups)  36.3 us
    all_to_all x1, waiting for transfers between devices, send_shares(): got = lax.all_to_all(shares, axis, 0, 0, axis_index_groups=groups)  21.9 us
    all_to_all x1, waiting for transfers between devices, send_copies(): got = lax.all_to_all(copies, axis, 0, 0, axis_index_groups=groups)  17.9 us
    all_to_all x1, starting transfers between devices, send_shares(): got = lax.all_to_all(shares, axis, 0, 0, axis_index_groups=groups)  9.27 us
    all_to_all x1, waiting for transfers between devices, shards(): lax.all_to_all(partial_grad.reshape(cols // 2, mine_b, -1), 'col', 0, 0,...  7.51 us
    all_to_all x1, starting transfers between devices, send_copies(): got = lax.all_to_all(copies, axis, 0, 0, axis_index_groups=groups)  5.29 us
    ppermute x1, starting transfers between devices, shards(): far = lax.ppermute(acts[1], ('row', 'col'), collect_far)  4.73 us
    all_to_all x1, starting transfers between devices, shards(): lax.all_to_all(partial_grad.reshape(cols // 2, mine_b, -1), 'col', 0, 0,...  4.64 us
  transfers between devices with their start and end apart: 9, of which 4 were waited for; matrix products, arithmetic and copies ran while one was open for 4% of the time, Pallas kernels for 0%

profile of v8, /device:TPU:32, one launch (start us, length us, event | category | flops | bytes accessed | tf_op | source)
XLA Modules:
  0.0 136.8 jit_solution(10504750699833554460)
XLA Ops:
  0.6 0.0 copy-start
  0.7 2.1 %collective-permute-start.2 = (bf16[512,1024]{1,0:T(8,128)(2,1)}, bf16[512,1024]{1,0:T(8,128)(2,1)S(1)}, u32[]{:S(2)}, u32[]{:S(2)}) collective-permute-start(bf16[512,1024]{1,0:T(8,128)(2,1)} %own.1), channel_id=1, source_target_pairs={{0,1},{1,0},{2,3},{3,2},{4,5},{5,4},{6,7},{7,6},{8,9},{9,8},{10,11... | collective-permute-start | bytes 3145736 | tf_op jit(solution)/shard_map/ppermute | solution.py:119
  2.7 2.4 %fusion.1 = bf16[16,8,64]{2,1,0:T(8,128)(2,1)S(1)} fusion(bf16[16,256,256]{2,1,0:T(8,128)(2,1)} %param.4, s32[]{:T(128)S(6)} %select_n.56, bf16[256,64]{0,1:T(8,128)(2,1)S(1)} %copy-done), kind=kOutput, calls=%fused_computation.3 | convolution fusion | flops 21012480 | bytes 2211844 | tf_op jit(solution)/shard_map/bim,mr->bir/dot_general | solution.py:112
  5.2 0.1 reshape.73
  5.3 36.3 %all_to_all.20 = bf16[16,16,512]{2,1,0:T(8,128)(2,1)S(1)} all-to-all(bf16[16,16,512]{2,1,0:T(8,128)(2,1)S(1)} %broadcast_in_dim.4), channel_id=1, replica_groups={{0,2,4,6,8,10,12,14,16,18,20,22,24,26,28,30},{1,3,5,7,9,11,13,15,17,19,..., dimensions={0} | all-to-all | bytes 524288 | tf_op jit(solution)/shard_map/all_to_all | solution.py:20
  41.6 0.0 collective-permute-done.2.other
  41.7 0.0 copy-start.3
  41.7 1.7 %times_weights.1 = bf16[256,2048]{1,0:T(8,128)(2,1)} custom-call(bf16[256,512]{1,0:T(8,128)(2,1)S(1)} %bitcast.22, bf16[512,1024]{1,0:T(8,128)(2,1)S(1)} %copy-done.1, bf16[512,1024]{1,0:T(8,128)(2,1)S(1)} %collective-permute-done.2.other), custom_call_target="tpu_custom_call" | custom-call | tf_op jit(solution)/shard_map/times_weights/pallas_call | solution.py:45
  43.4 9.3 %all-to-all-start.1 = ((bf16[32,8,2048]{2,1,0:T(8,128)(2,1)}), bf16[32,8,2048]{2,1,0:T(8,128)(2,1)S(1)}, u32[]{:S(2)}, u32[]{:S(2)}) async-start(bf16[32,8,2048]{2,1,0:T(8,128)(2,1)} %bitcast.25), calls=%async_computation.1 | async-start | bytes 2097152 | tf_op jit(solution)/shard_map/all_to_all | solution.py:25
  52.7 0.7 collective-permute-start
  53.4 4.6 %collective-permute-start.1 = (bf16[8,1024]{1,0:T(8,128)(2,1)S(1)}, bf16[8,1024]{1,0:T(8,128)(2,1)S(1)}, u32[]{:S(2)}, u32[]{:S(2)}) collective-permute-start(bf16[8,1024]{1,0:T(8,128)(2,1)S(1)} %get-tuple-element.30), channel_id=1, source_target_pairs={{0,32},{1,0},{2,34},{3,2},{4,36},{5,4},{6,38},{7,6},{8,40},{9,8},{... | collective-permute-start | bytes 49160 | tf_op jit(solution)/shard_map/ppermute | solution.py:124
  58.1 21.9 %all-to-all-done.1 = bf16[32,8,2048]{2,1,0:T(8,128)(2,1)S(1)} async-done(((bf16[32,8,2048]{2,1,0:T(8,128)(2,1)}), bf16[32,8,2048]{2,1,0:T(8,128)(2,1)S(1)}, u32[]{:S(2)}, u32[]{:S(2)}) %all-to-all-start.1) | async-done | bytes 1048608 | tf_op jit(solution)/shard_map/all_to_all | solution.py:25
  79.9 0.2 convert_reduce_fusion
  80.1 0.0 collective-permute-done
  80.1 0.0 collective-permute-done.1
  80.1 1.1 broadcast_in_dim.5
  81.2 5.3 %all-to-all-start.2 = ((bf16[32,8,2048]{2,1,0:T(8,128)(2,1)}), bf16[32,8,2048]{2,1,0:T(8,128)(2,1)S(1)}, u32[]{:S(2)}, u32[]{:S(2)}) async-start(bf16[32,8,2048]{2,1,0:T(8,128)(2,1)} %broadcast_in_dim.5), calls=%async_computation.2 | async-start | bytes 2097152 | tf_op jit(solution)/shard_map/all_to_all | solution.py:20
  86.5 1.9 %collective-permute-start.5 = (bf16[256,512]{1,0:T(8,128)(2,1)S(1)}, bf16[256,512]{1,0:T(8,128)(2,1)S(1)}, u32[]{:S(2)}, u32[]{:S(2)}) collective-permute-start(bf16[256,512]{1,0:T(8,128)(2,1)S(1)} %bitcast.23), channel_id=1, source_target_pairs={{0,1},{1,0},{2,3},{3,2},{4,5},{5,4},{6,7},{7,6},{8,9},{9,8},{10,11... | collective-permute-start | bytes 786440 | tf_op jit(solution)/shard_map/ppermute | solution.py:140
  88.5 0.7 collective-permute-start.3
  89.2 4.7 %collective-permute-start.4 = (bf16[8,1024]{1,0:T(8,128)(2,1)S(1)}, bf16[8,1024]{1,0:T(8,128)(2,1)S(1)}, u32[]{:S(2)}, u32[]{:S(2)}) collective-permute-start(bf16[8,1024]{1,0:T(8,128)(2,1)S(1)} %get-tuple-element.26), channel_id=1, source_target_pairs={{32,0},{0,1},{34,2},{2,3},{36,4},{4,5},{38,6},{6,7},{40,8},{8,9},{... | collective-permute-start | bytes 49160 | tf_op jit(solution)/shard_map/ppermute | solution.py:137
  93.9 0.0 collective-permute-done.3
  93.9 2.3 %collective-permute-done.4 = bf16[8,1024]{1,0:T(8,128)(2,1)S(1)} collective-permute-done((bf16[8,1024]{1,0:T(8,128)(2,1)S(1)}, bf16[8,1024]{1,0:T(8,128)(2,1)S(1)}, u32[]{:S(2)}, u32[]{:S(2)}) %collective-permute-start.4) | collective-permute-done | bytes 16416 | tf_op jit(solution)/shard_map/ppermute | solution.py:137
  96.2 0.6 maximum_select_fusion.2
  96.9 0.0 collective-permute-done.5
  96.9 17.9 %all-to-all-done.2 = bf16[32,8,2048]{2,1,0:T(8,128)(2,1)S(1)} async-done(((bf16[32,8,2048]{2,1,0:T(8,128)(2,1)}), bf16[32,8,2048]{2,1,0:T(8,128)(2,1)S(1)}, u32[]{:S(2)}, u32[]{:S(2)}) %all-to-all-start.2) | async-done | bytes 1048608 | tf_op jit(solution)/shard_map/all_to_all | solution.py:20
  114.7 2.7 %times_weights_back.1 = bf16[256,512]{1,0:T(8,128)(2,1)} custom-call(bf16[256,2048]{1,0:T(8,128)(2,1)S(1)} %bitcast.19, bf16[512,1024]{1,0:T(8,128)(2,1)S(1)} %copy-done.1, bf16[512,1024]{1,0:T(8,128)(2,1)} %copy-done.2), custom_call_target="tpu_custom_call" | custom-call | tf_op jit(solution)/shard_map/times_weights_back/pallas_call | solution.py:67
  117.5 4.6 %all-to-all-start.3 = ((bf16[16,16,512]{2,1,0:T(8,128)(2,1)}), bf16[16,16,512]{2,1,0:T(8,128)(2,1)S(1)}, u32[]{:S(2)}, u32[]{:S(2)}) async-start(bf16[16,16,512]{2,1,0:T(8,128)(2,1)} %bitcast.7), calls=%async_computation.3 | async-start | bytes 524288 | tf_op jit(solution)/shard_map/all_to_all | solution.py:146
  122.1 2.2 %all-gather = bf16[256,1024]{1,0:T(8,128)(2,1)S(1)} all-gather(bf16[128,1024]{1,0:T(8,128)(2,1)S(1)} %get-tuple-element.21), channel_id=2, replica_groups={{0,1},{2,3},{4,5},{6,7},{8,9},{10,11},{12,13},{14,15},{16,17},{18,19},{..., dimensions={0}, use_global_device_ids=true | all-gather | bytes 786432 | tf_op jit(solution)/shard_map/all_gather | solution.py:153
  124.3 2.2 %all-gather.1 = bf16[256,1024]{1,0:T(8,128)(2,1)S(1)} all-gather(bf16[128,1024]{1,0:T(8,128)(2,1)S(1)} %get-tuple-element.22), channel_id=3, replica_groups={{0,1},{2,3},{4,5},{6,7},{8,9},{10,11},{12,13},{14,15},{16,17},{18,19},{..., dimensions={0}, use_global_device_ids=true | all-gather | bytes 786432 | tf_op jit(solution)/shard_map/all_gather | solution.py:153
  126.5 2.0 %fusion.2 = f32[512,1024]{1,0:T(8,128)} fusion(bf16[128,1024]{1,0:T(8,128)(2,1)S(1)} %dynamic-slice_bitcast_fusion, bf16[128,1024]{1,0:T(8,128)(2,1)S(1)} %dynamic-slice_bitcast_fusion.1, bf16[256,1024]{1,0:T(8,128)(2,1)S(1)} %slice.24, bf16[256,512]{1,0:T(8,128)(2,1)S(1)} %collective-permute-done.5, bf16[256,512]{1,0:T(8,128)(2,1)S(1)} %bitcast.24), kind=kOutput, calls=%fused_computation.4 | convolution fusion | flops 541065216 | bytes 3670016 | tf_op jit(solution)/shard_map/dot_general | solution.py:158
  128.6 7.5 %all-to-all-done.3 = bf16[16,16,512]{2,1,0:T(8,128)(2,1)S(1)} async-done(((bf16[16,16,512]{2,1,0:T(8,128)(2,1)}), bf16[16,16,512]{2,1,0:T(8,128)(2,1)S(1)}, u32[]{:S(2)}, u32[]{:S(2)}) %all-to-all-start.3) | async-done | bytes 262176 | tf_op jit(solution)/shard_map/all_to_all | solution.py:146
  136.1 0.7 convert_reduce_fusion.1
  (16 shorter events, 0.2 us)
Async XLA Ops:
  0.6 2.1 %copy-start = (bf16[256,64]{0,1:T(8,128)(2,1)S(1)}, bf16[256,64]{0,1:T(8,128)(2,1)}, u32[]{:S(2)}) copy-start(bf16[256,64]{0,1:T(8,128)(2,1)} %param.5) | copy-start | bytes 98308
  0.6 41.0 %copy-start.1 = (bf16[512,1024]{1,0:T(8,128)(2,1)S(1)}, bf16[512,1024]{1,0:T(8,128)(2,1)}, u32[]{:S(2)}) copy-start(bf16[512,1024]{1,0:T(8,128)(2,1)} %own.1) | copy-start | bytes 3145732
  0.7 41.0 %collective-permute-start.2 = (bf16[512,1024]{1,0:T(8,128)(2,1)}, bf16[512,1024]{1,0:T(8,128)(2,1)S(1)}, u32[]{:S(2)}, u32[]{:S(2)}) collective-permute-start(bf16[512,1024]{1,0:T(8,128)(2,1)} %own.1), channel_id=1, source_target_pairs={{0,1},{1,0},{2,3},{3,2},{4,5},{5,4},{6,7},{7,6},{8,9},{9,8},{10,11... | collective-permute-start | bytes 3145736 | tf_op jit(solution)/shard_map/ppermute | solution.py:119
  41.6 1.8 %copy-start.2 = (bf16[512,1024]{1,0:T(8,128)(2,1)}, bf16[512,1024]{1,0:T(8,128)(2,1)S(1)}, u32[]{:S(2)}) copy-start(bf16[512,1024]{1,0:T(8,128)(2,1)S(1)} %collective-permute-done.2.other) | copy-start | bytes 3145732
  41.7 11.1 %copy-start.3 = (bf16[16,1024]{1,0:T(8,128)(2,1)S(1)}, bf16[16,1024]{1,0:T(8,128)(2,1)}, u32[]{:S(2)}) copy-start(bf16[16,1024]{1,0:T(8,128)(2,1)} %param.7) | copy-start | bytes 98308
  43.4 36.5 %all-to-all-start.1 = ((bf16[32,8,2048]{2,1,0:T(8,128)(2,1)}), bf16[32,8,2048]{2,1,0:T(8,128)(2,1)S(1)}, u32[]{:S(2)}, u32[]{:S(2)}) async-start(bf16[32,8,2048]{2,1,0:T(8,128)(2,1)} %bitcast.25), calls=%async_computation.1 | async-start | bytes 2097152 | tf_op jit(solution)/shard_map/all_to_all | solution.py:25
  52.7 27.3 %collective-permute-start = (bf16[8,1024]{1,0:T(8,128)(2,1)S(1)}, bf16[8,1024]{1,0:T(8,128)(2,1)S(1)}, u32[]{:S(2)}, u32[]{:S(2)}) collective-permute-start(bf16[8,1024]{1,0:T(8,128)(2,1)S(1)} %get-tuple-element.29), channel_id=1, source_target_pairs={{0,0},{1,32},{2,2},{3,34},{4,4},{5,36},{6,6},{7,38},{8,8},{9,40},{... | collective-permute-start | bytes 49160 | tf_op jit(solution)/shard_map/ppermute | solution.py:121
  53.4 26.7 %collective-permute-start.1 = (bf16[8,1024]{1,0:T(8,128)(2,1)S(1)}, bf16[8,1024]{1,0:T(8,128)(2,1)S(1)}, u32[]{:S(2)}, u32[]{:S(2)}) collective-permute-start(bf16[8,1024]{1,0:T(8,128)(2,1)S(1)} %get-tuple-element.30), channel_id=1, source_target_pairs={{0,32},{1,0},{2,34},{3,2},{4,36},{5,4},{6,38},{7,6},{8,40},{9,8},{... | collective-permute-start | bytes 49160 | tf_op jit(solution)/shard_map/ppermute | solution.py:124
  81.2 33.5 %all-to-all-start.2 = ((bf16[32,8,2048]{2,1,0:T(8,128)(2,1)}), bf16[32,8,2048]{2,1,0:T(8,128)(2,1)S(1)}, u32[]{:S(2)}, u32[]{:S(2)}) async-start(bf16[32,8,2048]{2,1,0:T(8,128)(2,1)} %broadcast_in_dim.5), calls=%async_computation.2 | async-start | bytes 2097152 | tf_op jit(solution)/shard_map/all_to_all | solution.py:20
  86.5 10.3 %collective-permute-start.5 = (bf16[256,512]{1,0:T(8,128)(2,1)S(1)}, bf16[256,512]{1,0:T(8,128)(2,1)S(1)}, u32[]{:S(2)}, u32[]{:S(2)}) collective-permute-start(bf16[256,512]{1,0:T(8,128)(2,1)S(1)} %bitcast.23), channel_id=1, source_target_pairs={{0,1},{1,0},{2,3},{3,2},{4,5},{5,4},{6,7},{7,6},{8,9},{9,8},{10,11... | collective-permute-start | bytes 786440 | tf_op jit(solution)/shard_map/ppermute | solution.py:140
  88.5 5.4 %collective-permute-start.3 = (bf16[8,1024]{1,0:T(8,128)(2,1)S(1)}, bf16[8,1024]{1,0:T(8,128)(2,1)S(1)}, u32[]{:S(2)}, u32[]{:S(2)}) collective-permute-start(bf16[8,1024]{1,0:T(8,128)(2,1)S(1)} %get-tuple-element.25), channel_id=1, source_target_pairs={{0,0},{32,1},{2,2},{34,3},{4,4},{36,5},{6,6},{38,7},{8,8},{40,9},{... | collective-permute-start | bytes 49160 | tf_op jit(solution)/shard_map/ppermute | solution.py:136
  89.2 7.1 %collective-permute-start.4 = (bf16[8,1024]{1,0:T(8,128)(2,1)S(1)}, bf16[8,1024]{1,0:T(8,128)(2,1)S(1)}, u32[]{:S(2)}, u32[]{:S(2)}) collective-permute-start(bf16[8,1024]{1,0:T(8,128)(2,1)S(1)} %get-tuple-element.26), channel_id=1, source_target_pairs={{32,0},{0,1},{34,2},{2,3},{36,4},{4,5},{38,6},{6,7},{40,8},{8,9},{... | collective-permute-start | bytes 49160 | tf_op jit(solution)/shard_map/ppermute | solution.py:137
  117.5 18.6 %all-to-all-start.3 = ((bf16[16,16,512]{2,1,0:T(8,128)(2,1)}), bf16[16,16,512]{2,1,0:T(8,128)(2,1)S(1)}, u32[]{:S(2)}, u32[]{:S(2)}) async-start(bf16[16,16,512]{2,1,0:T(8,128)(2,1)} %bitcast.7), calls=%async_computation.3 | async-start | bytes 524288 | tf_op jit(solution)/shard_map/all_to_all | solution.py:146

commit v9 on v8

--- a/solution.py
+++ b/solution.py
@@ -7,6 +7,7 @@
 
 BF16 = jnp.bfloat16
 F32 = jnp.float32
+WEIGHT_PIECES = 4
 
 
 def silu_slope(values):
@@ -33,49 +34,56 @@
 WHOLE = pl.BlockSpec(memory_space=pltpu.VMEM)
 
 
-def forward_kernel(features, own, other, out):
+def forward_kernel(features, own, *rest):
+    *others, out = rest
     width, rows = own.shape[1], out.shape[0]
     mine = features[pl.ds(pl.multiple_of(pl.program_id(0) * rows, rows), rows)]
     out[:, :width] = jnp.dot(mine, own[...], preferred_element_type=F32).astype(BF16)
-    out[:, width:] = jnp.dot(mine, other[...], preferred_element_type=F32).astype(BF16)
+    first = width
+    for other in others:
+        part = jnp.dot(mine, other[...], preferred_element_type=F32)
+        out[:, first : first + other.shape[1]] = part.astype(BF16)
+        first += other.shape[1]
 
 
-def times_weights(features, own, other, steps=2):
+def times_weights(features, own, others, steps=2):
     batch, width = features.shape[0], own.shape[1]
     return pl.pallas_call(
         forward_kernel,
         out_shape=jax.ShapeDtypeStruct((batch, 2 * width), BF16),
         grid=(steps,),
-        in_specs=[WHOLE, WHOLE, WHOLE],
+        in_specs=[WHOLE] * (2 + len(others)),
         out_specs=pl.BlockSpec((batch // steps, 2 * width), lambda i: (i, 0)),
         name="times_weights",
-    )(in_vmem(features), in_vmem(own), in_vmem(other))
+    )(in_vmem(features), in_vmem(own), *map(in_vmem, others))
 
 
-def backward_kernel(slope, own, other, out):
+def backward_kernel(slope, own, *rest):
+    *others, out = rest
     width, block = own.shape[1], out.shape[1]
     mine = own[pl.ds(pl.multiple_of(pl.program_id(0) * block, block), block)]
     dims = (((1,), (1,)), ((), ()))
     total = lax.dot_general(slope[:, :width], mine, dims, preferred_element_type=F32)
-    total += lax.dot_general(slope[:, width:], other[...], dims, preferred_element_type=F32)
+    first = width
+    for other in others:
+        part = slope[:, first : first + other.shape[1]]
+        total += lax.dot_general(part, other[...], dims, preferred_element_type=F32)
+        first += other.shape[1]
     out[...] = total.astype(BF16)
 
 
-def times_weights_back(slope, own, other, steps=2):
-    batch, (depth, width) = slope.shape[0], own.shape
+def times_weights_back(slope, own, others, steps=2):
+    batch, depth = slope.shape[0], own.shape[0]
     block = depth // steps
     return pl.pallas_call(
         backward_kernel,
         out_shape=jax.ShapeDtypeStruct((batch, depth), BF16),
         grid=(steps,),
-        in_specs=[
-            WHOLE,
-            WHOLE,
-            pl.BlockSpec((block, width), lambda i: (i, 0)),
-        ],
+        in_specs=[WHOLE, WHOLE]
+        + [pl.BlockSpec((block, other.shape[1]), lambda i: (i, 0)) for other in others],
         out_specs=pl.BlockSpec((batch, block), lambda i: (0, i)),
         name="times_weights_back",
-    )(in_vmem(slope), in_vmem(own), other)
+    )(in_vmem(slope), in_vmem(own), *others)
 
 
 def either(flag, first, second, axis):
@@ -113,10 +121,13 @@
             "bim,mr->bir", interaction, projection, preferred_element_type=F32
         )
         local_features = local_features.astype(BF16).reshape(mine_b, -1)
-        local_features, own = lax.optimization_barrier((local_features, weight))
+        local_features, late_weight = lax.optimization_barrier((local_features, weight))
+        own = weight
         features = send_copies(local_features, "col", cores)
 
-        other_weight = lax.ppermute(weight, "col", swap)
+        other_weight = [
+            lax.ppermute(piece, "col", swap) for piece in jnp.split(late_weight, WEIGHT_PIECES, axis=1)
+        ]
         halves = act_grad.reshape(2, half, width)
         near = lax.ppermute(
             lax.dynamic_index_in_dim(halves, k, 0, False), ("row", "col"), spread

time: 137 us -> 140 us (1.022)
  blocking collectives: 40.7 us -> 4.36 us
  starting transfers between devices: 33.9 us -> 64.9 us
  waiting for transfers between devices: 49.6 us -> 55.6 us
  local copies, waits for them, and re-layouts: 1.37 us -> 2.9 us
    all_to_all x1 -> x0, blocking collectives: 36.3 us -> none  [send_copies(): got = lax.all_to_all(copies, axis, 0, 0, axis_index_groups=groups)]
    all_to_all x1 -> x2, starting transfers between devices: 5.29 us -> 26 us  [send_copies(): got = lax.all_to_all(copies, axis, 0, 0, axis_index_groups=groups)]
    ppermute x1 -> x4, starting transfers between devices: 2.05 us -> 8.65 us  [shards(): lax.ppermute(piece, 'col', swap)]
    all_to_all x1 -> x2, waiting for transfers between devices: 17.9 us -> 23.3 us  [send_copies(): got = lax.all_to_all(copies, axis, 0, 0, axis_index_groups=groups)]
    all_to_all x1, starting transfers between devices: 4.64 us -> 8.32 us  [shards(): lax.all_to_all(partial_grad.reshape(cols // 2, mine_b, -1), 'col', 0, 0,...]
  transfers between devices with their start and end apart: 9 -> 13, of which waited for: 4 -> 6; matrix products, arithmetic and copies ran while one was open for 4% -> 2% of each run, Pallas kernels for 0% -> 0%
where the time goes in v9:
time: 140 us; the launch traced here: 139 us
  starting transfers between devices  64.9 us (46%)
  waiting for transfers between devices  55.6 us (40%)
  matrix products  4.48 us (3%)
  Pallas kernels  4.44 us (3%)
  blocking collectives  4.36 us (3%)
  local copies, waits for them, and re-layouts  2.9 us (2%)
  other arithmetic  1.49 us (1%)
    all_to_all x2, starting transfers between devices, send_copies(): got = lax.all_to_all(copies, axis, 0, 0, axis_index_groups=groups)  26 us
    all_to_all x2, waiting for transfers between devices, send_copies(): got = lax.all_to_all(copies, axis, 0, 0, axis_index_groups=groups)  23.3 us
    all_to_all x1, waiting for transfers between devices, send_shares(): got = lax.all_to_all(shares, axis, 0, 0, axis_index_groups=groups)  21.6 us
    all_to_all x1, starting transfers between devices, send_shares(): got = lax.all_to_all(shares, axis, 0, 0, axis_index_groups=groups)  9.29 us
    ppermute x4, starting transfers between devices, shards(): lax.ppermute(piece, 'col', swap)  8.65 us
    all_to_all x1, starting transfers between devices, shards(): lax.all_to_all(partial_grad.reshape(cols // 2, mine_b, -1), 'col', 0, 0,...  8.32 us
    all_to_all x1, waiting for transfers between devices, shards(): lax.all_to_all(partial_grad.reshape(cols // 2, mine_b, -1), 'col', 0, 0,...  7.32 us
    ppermute x1, starting transfers between devices, shards(): far = lax.ppermute(acts[1], ('row', 'col'), collect_far)  4.73 us
  transfers between devices with their start and end apart: 13, of which 6 were waited for; matrix products, arithmetic and copies ran while one was open for 2% of the time, Pallas kernels for 0%

profile of v9, /device:TPU:32, one launch (start us, length us, event | category | flops | bytes accessed | tf_op | source)
XLA Modules:
  0.0 139.1 jit_solution(11772821395242997884)
XLA Ops:
  0.7 0.7 copy-done
  1.4 2.4 %fusion.1 = bf16[16,8,64]{2,1,0:T(8,128)(2,1)S(1)} fusion(bf16[16,256,256]{2,1,0:T(8,128)(2,1)} %param.4, s32[]{:T(128)S(6)} %select_n.56, bf16[256,64]{0,1:T(8,128)(2,1)S(1)} %copy-done), kind=kOutput, calls=%fused_computation.3 | convolution fusion | flops 21012480 | bytes 2211844 | tf_op jit(solution)/shard_map/bim,mr->bir/dot_general | solution.py:120
  3.8 0.1 reshape.73
  3.9 0.7 broadcast_in_dim.4
  4.7 20.7 %all-to-all-start = ((bf16[16,16,512]{2,1,0:T(8,128)(2,1)}), bf16[16,16,512]{2,1,0:T(8,128)(2,1)S(1)}, u32[]{:S(2)}, u32[]{:S(2)}) async-start(bf16[16,16,512]{2,1,0:T(8,128)(2,1)} %broadcast_in_dim.4), calls=%async_computation | async-start | bytes 524288 | tf_op jit(solution)/shard_map/all_to_all | solution.py:21
  25.5 1.9 %collective-permute-start.5 = (bf16[512,256]{1,0:T(8,128)(2,1)S(1)}, bf16[512,256]{1,0:T(8,128)(2,1)S(1)}, u32[]{:S(2)}, u32[]{:S(2)}) collective-permute-start(bf16[512,256]{1,0:T(8,128)(2,1)S(1)} %get-tuple-element.23), channel_id=1, source_target_pairs={{0,1},{1,0},{2,3},{3,2},{4,5},{5,4},{6,7},{7,6},{8,9},{9,8},{10,11... | collective-permute-start | bytes 786440 | tf_op jit(solution)/shard_map/ppermute | solution.py:129
  27.4 2.4 %collective-permute-start.4 = (bf16[512,256]{1,0:T(8,128)(2,1)S(1)}, bf16[512,256]{1,0:T(8,128)(2,1)S(1)}, u32[]{:S(2)}, u32[]{:S(2)}) collective-permute-start(bf16[512,256]{1,0:T(8,128)(2,1)S(1)} %get-tuple-element.24), channel_id=1, source_target_pairs={{0,1},{1,0},{2,3},{3,2},{4,5},{5,4},{6,7},{7,6},{8,9},{9,8},{10,11... | collective-permute-start | bytes 786440 | tf_op jit(solution)/shard_map/ppermute | solution.py:129
  29.8 1.9 %collective-permute-start.3 = (bf16[512,256]{1,0:T(8,128)(2,1)S(1)}, bf16[512,256]{1,0:T(8,128)(2,1)S(1)}, u32[]{:S(2)}, u32[]{:S(2)}) collective-permute-start(bf16[512,256]{1,0:T(8,128)(2,1)S(1)} %get-tuple-element.25), channel_id=1, source_target_pairs={{0,1},{1,0},{2,3},{3,2},{4,5},{5,4},{6,7},{7,6},{8,9},{9,8},{10,11... | collective-permute-start | bytes 786440 | tf_op jit(solution)/shard_map/ppermute | solution.py:129
  31.7 2.4 %collective-permute-start.2 = (bf16[512,256]{1,0:T(8,128)(2,1)S(1)}, bf16[512,256]{1,0:T(8,128)(2,1)S(1)}, u32[]{:S(2)}, u32[]{:S(2)}) collective-permute-start(bf16[512,256]{1,0:T(8,128)(2,1)S(1)} %get-tuple-element.26), channel_id=1, source_target_pairs={{0,1},{1,0},{2,3},{3,2},{4,5},{5,4},{6,7},{7,6},{8,9},{9,8},{10,11... | collective-permute-start | bytes 786440 | tf_op jit(solution)/shard_map/ppermute | solution.py:129
  34.2 1.1 collective-permute-done.2.rest_0_
  35.3 5.4 %all-to-all-done = bf16[16,16,512]{2,1,0:T(8,128)(2,1)S(1)} async-done(((bf16[16,16,512]{2,1,0:T(8,128)(2,1)}), bf16[16,16,512]{2,1,0:T(8,128)(2,1)S(1)}, u32[]{:S(2)}, u32[]{:S(2)}) %all-to-all-start) | async-done | bytes 262176 | tf_op jit(solution)/shard_map/all_to_all | solution.py:21
  40.7 1.7 %times_weights.1 = bf16[256,2048]{1,0:T(8,128)(2,1)} custom-call(bf16[256,512]{1,0:T(8,128)(2,1)S(1)} %bitcast.22, bf16[512,1024]{1,0:T(8,128)(2,1)S(1)} %copy-done.1, bf16[512,256]{1,0:T(8,128)(2,1)S(1)} %collective-permute-done.2.rest_0_, bf16[512,256]{1,0:T(8,128)(2,1)S(1)} %collective-permute-done.3.rest_1_, ...), custom_call_target="tpu_custom_call" | custom-call | tf_op jit(solution)/shard_map/times_weights/pallas_call | solution.py:51
  42.5 9.3 %all-to-all-start.1 = ((bf16[32,8,2048]{2,1,0:T(8,128)(2,1)}), bf16[32,8,2048]{2,1,0:T(8,128)(2,1)S(1)}, u32[]{:S(2)}, u32[]{:S(2)}) async-start(bf16[32,8,2048]{2,1,0:T(8,128)(2,1)} %bitcast.25), calls=%async_computation.1 | async-start | bytes 2097152 | tf_op jit(solution)/shard_map/all_to_all | solution.py:26
  51.8 0.7 collective-permute-start
  52.5 4.6 %collective-permute-start.1 = (bf16[8,1024]{1,0:T(8,128)(2,1)S(1)}, bf16[8,1024]{1,0:T(8,128)(2,1)S(1)}, u32[]{:S(2)}, u32[]{:S(2)}) collective-permute-start(bf16[8,1024]{1,0:T(8,128)(2,1)S(1)} %get-tuple-element.34), channel_id=1, source_target_pairs={{0,32},{1,0},{2,34},{3,2},{4,36},{5,4},{6,38},{7,6},{8,40},{9,8},{... | collective-permute-start | bytes 49160 | tf_op jit(solution)/shard_map/ppermute | solution.py:135
  57.2 21.6 %all-to-all-done.1 = bf16[32,8,2048]{2,1,0:T(8,128)(2,1)S(1)} async-done(((bf16[32,8,2048]{2,1,0:T(8,128)(2,1)}), bf16[32,8,2048]{2,1,0:T(8,128)(2,1)S(1)}, u32[]{:S(2)}, u32[]{:S(2)}) %all-to-all-start.1) | async-done | bytes 1048608 | tf_op jit(solution)/shard_map/all_to_all | solution.py:26
  78.7 0.2 convert_reduce_fusion
  78.9 1.1 broadcast_in_dim.5
  80.0 5.3 %all-to-all-start.2 = ((bf16[32,8,2048]{2,1,0:T(8,128)(2,1)}), bf16[32,8,2048]{2,1,0:T(8,128)(2,1)S(1)}, u32[]{:S(2)}, u32[]{:S(2)}) async-start(bf16[32,8,2048]{2,1,0:T(8,128)(2,1)} %broadcast_in_dim.5), calls=%async_computation.2 | async-start | bytes 2097152 | tf_op jit(solution)/shard_map/all_to_all | solution.py:21
  85.3 1.9 %collective-permute-start.8 = (bf16[256,512]{1,0:T(8,128)(2,1)S(1)}, bf16[256,512]{1,0:T(8,128)(2,1)S(1)}, u32[]{:S(2)}, u32[]{:S(2)}) collective-permute-start(bf16[256,512]{1,0:T(8,128)(2,1)S(1)} %bitcast.23), channel_id=1, source_target_pairs={{0,1},{1,0},{2,3},{3,2},{4,5},{5,4},{6,7},{7,6},{8,9},{9,8},{10,11... | collective-permute-start | bytes 786440 | tf_op jit(solution)/shard_map/ppermute | solution.py:151
  87.3 0.7 collective-permute-start.6
  88.0 4.7 %collective-permute-start.7 = (bf16[8,1024]{1,0:T(8,128)(2,1)S(1)}, bf16[8,1024]{1,0:T(8,128)(2,1)S(1)}, u32[]{:S(2)}, u32[]{:S(2)}) collective-permute-start(bf16[8,1024]{1,0:T(8,128)(2,1)S(1)} %get-tuple-element.30), channel_id=1, source_target_pairs={{32,0},{0,1},{34,2},{2,3},{36,4},{4,5},{38,6},{6,7},{40,8},{8,9},{... | collective-permute-start | bytes 49160 | tf_op jit(solution)/shard_map/ppermute | solution.py:148
  92.7 2.3 %collective-permute-done.7 = bf16[8,1024]{1,0:T(8,128)(2,1)S(1)} collective-permute-done((bf16[8,1024]{1,0:T(8,128)(2,1)S(1)}, bf16[8,1024]{1,0:T(8,128)(2,1)S(1)}, u32[]{:S(2)}, u32[]{:S(2)}) %collective-permute-start.7) | collective-permute-done | bytes 16416 | tf_op jit(solution)/shard_map/ppermute | solution.py:148
  95.0 0.6 maximum_select_fusion.2
  95.6 17.9 %all-to-all-done.2 = bf16[32,8,2048]{2,1,0:T(8,128)(2,1)S(1)} async-done(((bf16[32,8,2048]{2,1,0:T(8,128)(2,1)}), bf16[32,8,2048]{2,1,0:T(8,128)(2,1)S(1)}, u32[]{:S(2)}, u32[]{:S(2)}) %all-to-all-start.2) | async-done | bytes 1048608 | tf_op jit(solution)/shard_map/all_to_all | solution.py:21
  113.5 2.7 %times_weights_back.1 = bf16[256,512]{1,0:T(8,128)(2,1)} custom-call(bf16[256,2048]{1,0:T(8,128)(2,1)S(1)} %bitcast.19, bf16[512,1024]{1,0:T(8,128)(2,1)S(1)} %copy-done.2, bf16[512,256]{1,0:T(8,128)(2,1)} %copy-done.6, bf16[512,256]{1,0:T(8,128)(2,1)} %copy-done.5, bf16[512,256]{1,0:T(8,128)(2,1)} %copy-done.4, bf16[512,256]{1,0:T(8,128)(2,1)} %copy-done.3), custom_call_target="tpu_custom_call" | custom-call | tf_op jit(solution)/shard_map/times_weights_back/pallas_call | solution.py:78
  116.3 8.3 %all-to-all-start.3 = ((bf16[16,16,512]{2,1,0:T(8,128)(2,1)}), bf16[16,16,512]{2,1,0:T(8,128)(2,1)S(1)}, u32[]{:S(2)}, u32[]{:S(2)}) async-start(bf16[16,16,512]{2,1,0:T(8,128)(2,1)} %bitcast.7), calls=%async_computation.3 | async-start | bytes 524288 | tf_op jit(solution)/shard_map/all_to_all | solution.py:157
  124.7 2.2 %all-gather = bf16[256,1024]{1,0:T(8,128)(2,1)S(1)} all-gather(bf16[128,1024]{1,0:T(8,128)(2,1)S(1)} %get-tuple-element.21), channel_id=2, replica_groups={{0,1},{2,3},{4,5},{6,7},{8,9},{10,11},{12,13},{14,15},{16,17},{18,19},{..., dimensions={0}, use_global_device_ids=true | all-gather | bytes 786432 | tf_op jit(solution)/shard_map/all_gather | solution.py:164
  126.9 2.2 %all-gather.1 = bf16[256,1024]{1,0:T(8,128)(2,1)S(1)} all-gather(bf16[128,1024]{1,0:T(8,128)(2,1)S(1)} %get-tuple-element.22), channel_id=3, replica_groups={{0,1},{2,3},{4,5},{6,7},{8,9},{10,11},{12,13},{14,15},{16,17},{18,19},{..., dimensions={0}, use_global_device_ids=true | all-gather | bytes 786432 | tf_op jit(solution)/shard_map/all_gather | solution.py:164
  129.1 2.0 %fusion.2 = f32[512,1024]{1,0:T(8,128)} fusion(bf16[128,1024]{1,0:T(8,128)(2,1)S(1)} %dynamic-slice_bitcast_fusion, bf16[128,1024]{1,0:T(8,128)(2,1)S(1)} %dynamic-slice_bitcast_fusion.1, bf16[256,1024]{1,0:T(8,128)(2,1)S(1)} %slice.24, bf16[256,512]{1,0:T(8,128)(2,1)S(1)} %collective-permute-done.8, bf16[256,512]{1,0:T(8,128)(2,1)S(1)} %bitcast.24), kind=kOutput, calls=%fused_computation.4 | convolution fusion | flops 541065216 | bytes 3670016 | tf_op jit(solution)/shard_map/dot_general | solution.py:169
  131.1 7.3 %all-to-all-done.3 = bf16[16,16,512]{2,1,0:T(8,128)(2,1)S(1)} async-done(((bf16[16,16,512]{2,1,0:T(8,128)(2,1)}), bf16[16,16,512]{2,1,0:T(8,128)(2,1)S(1)}, u32[]{:S(2)}, u32[]{:S(2)}) %all-to-all-start.3) | async-done | bytes 262176 | tf_op jit(solution)/shard_map/all_to_all | solution.py:157
  138.4 0.7 convert_reduce_fusion.1
  (32 shorter events, 0.3 us)
Async XLA Ops:
  0.6 0.8 copy-start
  0.6 24.7 %copy-start.1 = (bf16[512,1024]{1,0:T(8,128)(2,1)S(1)}, bf16[512,1024]{1,0:T(8,128)(2,1)}, u32[]{:S(2)}) copy-start(bf16[512,1024]{1,0:T(8,128)(2,1)} %own.3) | copy-start | bytes 3145732
  4.7 36.1 %all-to-all-start = ((bf16[16,16,512]{2,1,0:T(8,128)(2,1)}), bf16[16,16,512]{2,1,0:T(8,128)(2,1)S(1)}, u32[]{:S(2)}, u32[]{:S(2)}) async-start(bf16[16,16,512]{2,1,0:T(8,128)(2,1)} %broadcast_in_dim.4), calls=%async_computation | async-start | bytes 524288 | tf_op jit(solution)/shard_map/all_to_all | solution.py:21
  25.5 8.7 %collective-permute-start.5 = (bf16[512,256]{1,0:T(8,128)(2,1)S(1)}, bf16[512,256]{1,0:T(8,128)(2,1)S(1)}, u32[]{:S(2)}, u32[]{:S(2)}) collective-permute-start(bf16[512,256]{1,0:T(8,128)(2,1)S(1)} %get-tuple-element.23), channel_id=1, source_target_pairs={{0,1},{1,0},{2,3},{3,2},{4,5},{5,4},{6,7},{7,6},{8,9},{9,8},{10,11... | collective-permute-start | bytes 786440 | tf_op jit(solution)/shard_map/ppermute | solution.py:129
  27.4 6.8 %collective-permute-start.4 = (bf16[512,256]{1,0:T(8,128)(2,1)S(1)}, bf16[512,256]{1,0:T(8,128)(2,1)S(1)}, u32[]{:S(2)}, u32[]{:S(2)}) collective-permute-start(bf16[512,256]{1,0:T(8,128)(2,1)S(1)} %get-tuple-element.24), channel_id=1, source_target_pairs={{0,1},{1,0},{2,3},{3,2},{4,5},{5,4},{6,7},{7,6},{8,9},{9,8},{10,11... | collective-permute-start | bytes 786440 | tf_op jit(solution)/shard_map/ppermute | solution.py:129
  29.8 4.4 %collective-permute-start.3 = (bf16[512,256]{1,0:T(8,128)(2,1)S(1)}, bf16[512,256]{1,0:T(8,128)(2,1)S(1)}, u32[]{:S(2)}, u32[]{:S(2)}) collective-permute-start(bf16[512,256]{1,0:T(8,128)(2,1)S(1)} %get-tuple-element.25), channel_id=1, source_target_pairs={{0,1},{1,0},{2,3},{3,2},{4,5},{5,4},{6,7},{7,6},{8,9},{9,8},{10,11... | collective-permute-start | bytes 786440 | tf_op jit(solution)/shard_map/ppermute | solution.py:129
  31.7 3.6 %collective-permute-start.2 = (bf16[512,256]{1,0:T(8,128)(2,1)S(1)}, bf16[512,256]{1,0:T(8,128)(2,1)S(1)}, u32[]{:S(2)}, u32[]{:S(2)}) collective-permute-start(bf16[512,256]{1,0:T(8,128)(2,1)S(1)} %get-tuple-element.26), channel_id=1, source_target_pairs={{0,1},{1,0},{2,3},{3,2},{4,5},{5,4},{6,7},{7,6},{8,9},{9,8},{10,11... | collective-permute-start | bytes 786440 | tf_op jit(solution)/shard_map/ppermute | solution.py:129
  34.2 8.3 %copy-start.3 = (bf16[512,256]{1,0:T(8,128)(2,1)}, bf16[512,256]{1,0:T(8,128)(2,1)S(1)}, u32[]{:S(2)}) copy-start(bf16[512,256]{1,0:T(8,128)(2,1)S(1)} %collective-permute-done.5.rest_3_) | copy-start | bytes 786436
  34.2 8.3 %copy-start.4 = (bf16[512,256]{1,0:T(8,128)(2,1)}, bf16[512,256]{1,0:T(8,128)(2,1)S(1)}, u32[]{:S(2)}) copy-start(bf16[512,256]{1,0:T(8,128)(2,1)S(1)} %collective-permute-done.4.rest_2_) | copy-start | bytes 786436
  34.2 8.2 %copy-start.5 = (bf16[512,256]{1,0:T(8,128)(2,1)}, bf16[512,256]{1,0:T(8,128)(2,1)S(1)}, u32[]{:S(2)}) copy-start(bf16[512,256]{1,0:T(8,128)(2,1)S(1)} %collective-permute-done.3.rest_1_) | copy-start | bytes 786436
  35.3 7.2 %copy-start.6 = (bf16[512,256]{1,0:T(8,128)(2,1)}, bf16[512,256]{1,0:T(8,128)(2,1)S(1)}, u32[]{:S(2)}) copy-start(bf16[512,256]{1,0:T(8,128)(2,1)S(1)} %collective-permute-done.2.rest_0_) | copy-start | bytes 786436
  40.7 11.0 %copy-start.7 = (bf16[16,1024]{1,0:T(8,128)(2,1)S(1)}, bf16[16,1024]{1,0:T(8,128)(2,1)}, u32[]{:S(2)}) copy-start(bf16[16,1024]{1,0:T(8,128)(2,1)} %param.7) | copy-start | bytes 98308
  42.5 36.2 %all-to-all-start.1 = ((bf16[32,8,2048]{2,1,0:T(8,128)(2,1)}), bf16[32,8,2048]{2,1,0:T(8,128)(2,1)S(1)}, u32[]{:S(2)}, u32[]{:S(2)}) async-start(bf16[32,8,2048]{2,1,0:T(8,128)(2,1)} %bitcast.25), calls=%async_computation.1 | async-start | bytes 2097152 | tf_op jit(solution)/shard_map/all_to_all | solution.py:26
  51.8 27.1 %collective-permute-start = (bf16[8,1024]{1,0:T(8,128)(2,1)S(1)}, bf16[8,1024]{1,0:T(8,128)(2,1)S(1)}, u32[]{:S(2)}, u32[]{:S(2)}) collective-permute-start(bf16[8,1024]{1,0:T(8,128)(2,1)S(1)} %get-tuple-element.33), channel_id=1, source_target_pairs={{0,0},{1,32},{2,2},{3,34},{4,4},{5,36},{6,6},{7,38},{8,8},{9,40},{... | collective-permute-start | bytes 49160 | tf_op jit(solution)/shard_map/ppermute | solution.py:132
  52.5 26.4 %collective-permute-start.1 = (bf16[8,1024]{1,0:T(8,128)(2,1)S(1)}, bf16[8,1024]{1,0:T(8,128)(2,1)S(1)}, u32[]{:S(2)}, u32[]{:S(2)}) collective-permute-start(bf16[8,1024]{1,0:T(8,128)(2,1)S(1)} %get-tuple-element.34), channel_id=1, source_target_pairs={{0,32},{1,0},{2,34},{3,2},{4,36},{5,4},{6,38},{7,6},{8,40},{9,8},{... | collective-permute-start | bytes 49160 | tf_op jit(solution)/shard_map/ppermute | solution.py:135
  57.1 56.4 %copy-start.2 = (bf16[512,1024]{1,0:T(8,128)(2,1)S(1)}, bf16[512,1024]{1,0:T(8,128)(2,1)}, u32[]{:S(2)}) copy-start(bf16[512,1024]{1,0:T(8,128)(2,1)} %own.3) | copy-start | bytes 3145732
  80.0 33.5 %all-to-all-start.2 = ((bf16[32,8,2048]{2,1,0:T(8,128)(2,1)}), bf16[32,8,2048]{2,1,0:T(8,128)(2,1)S(1)}, u32[]{:S(2)}, u32[]{:S(2)}) async-start(bf16[32,8,2048]{2,1,0:T(8,128)(2,1)} %broadcast_in_dim.5), calls=%async_computation.2 | async-start | bytes 2097152 | tf_op jit(solution)/shard_map/all_to_all | solution.py:21
  85.3 10.3 %collective-permute-start.8 = (bf16[256,512]{1,0:T(8,128)(2,1)S(1)}, bf16[256,512]{1,0:T(8,128)(2,1)S(1)}, u32[]{:S(2)}, u32[]{:S(2)}) collective-permute-start(bf16[256,512]{1,0:T(8,128)(2,1)S(1)} %bitcast.23), channel_id=1, source_target_pairs={{0,1},{1,0},{2,3},{3,2},{4,5},{5,4},{6,7},{7,6},{8,9},{9,8},{10,11... | collective-permute-start | bytes 786440 | tf_op jit(solution)/shard_map/ppermute | solution.py:151
  87.3 5.4 %collective-permute-start.6 = (bf16[8,1024]{1,0:T(8,128)(2,1)S(1)}, bf16[8,1024]{1,0:T(8,128)(2,1)S(1)}, u32[]{:S(2)}, u32[]{:S(2)}) collective-permute-start(bf16[8,1024]{1,0:T(8,128)(2,1)S(1)} %get-tuple-element.29), channel_id=1, source_target_pairs={{0,0},{32,1},{2,2},{34,3},{4,4},{36,5},{6,6},{38,7},{8,8},{40,9},{... | collective-permute-start | bytes 49160 | tf_op jit(solution)/shard_map/ppermute | solution.py:147
  88.0 7.1 %collective-permute-start.7 = (bf16[8,1024]{1,0:T(8,128)(2,1)S(1)}, bf16[8,1024]{1,0:T(8,128)(2,1)S(1)}, u32[]{:S(2)}, u32[]{:S(2)}) collective-permute-start(bf16[8,1024]{1,0:T(8,128)(2,1)S(1)} %get-tuple-element.30), channel_id=1, source_target_pairs={{32,0},{0,1},{34,2},{2,3},{36,4},{4,5},{38,6},{6,7},{40,8},{8,9},{... | collective-permute-start | bytes 49160 | tf_op jit(solution)/shard_map/ppermute | solution.py:148
  116.3 22.1 %all-to-all-start.3 = ((bf16[16,16,512]{2,1,0:T(8,128)(2,1)}), bf16[16,16,512]{2,1,0:T(8,128)(2,1)S(1)}, u32[]{:S(2)}, u32[]{:S(2)}) async-start(bf16[16,16,512]{2,1,0:T(8,128)(2,1)} %bitcast.7), calls=%async_computation.3 | async-start | bytes 524288 | tf_op jit(solution)/shard_map/all_to_all | solution.py:157

commit v10 on v9

--- a/solution.py
+++ b/solution.py
@@ -7,7 +7,7 @@
 
 BF16 = jnp.bfloat16
 F32 = jnp.float32
-WEIGHT_PIECES = 4
+WEIGHT_CUTS = (384, 768)
 
 
 def silu_slope(values):
@@ -126,7 +126,7 @@
         features = send_copies(local_features, "col", cores)
 
         other_weight = [
-            lax.ppermute(piece, "col", swap) for piece in jnp.split(late_weight, WEIGHT_PIECES, axis=1)
+            lax.ppermute(piece, "col", swap) for piece in jnp.split(late_weight, WEIGHT_CUTS, axis=1)
         ]
         halves = act_grad.reshape(2, half, width)
         near = lax.ppermute(

time: 140 us -> 139 us (level)
  starting transfers between devices: 64.9 us -> 60.5 us
  waiting for transfers between devices: 55.6 us -> 58.2 us
    ppermute x4 -> x3, starting transfers between devices: 8.65 us -> 6.25 us  [shards(): lax.ppermute(piece, 'col', swap)]
    all_to_all x1, starting transfers between devices: 8.32 us -> 6.3 us  [shards(): lax.all_to_all(partial_grad.reshape(cols // 2, mine_b, -1), 'col', 0, 0,...]
    all_to_all x2, waiting for transfers between devices: 23.3 us -> 25.3 us  [send_copies(): got = lax.all_to_all(copies, axis, 0, 0, axis_index_groups=groups)]
  transfers between devices with their start and end apart: 13 -> 12, of which waited for: 6 -> 6; matrix products, arithmetic and copies ran while one was open for 2% -> 3% of each run, Pallas kernels for 0% -> 0%
where the time goes in v10:
time: 139 us
  starting transfers between devices  60.5 us (44%)
  waiting for transfers between devices  58.2 us (42%)
  matrix products  4.49 us (3%)
  Pallas kernels  4.49 us (3%)
  blocking collectives  4.36 us (3%)
  local copies, waits for them, and re-layouts  2.94 us (2%)
  other arithmetic  2.72 us (2%)
    all_to_all x2, starting transfers between devices, send_copies(): got = lax.all_to_all(copies, axis, 0, 0, axis_index_groups=groups)  26 us
    all_to_all x2, waiting for transfers between devices, send_copies(): got = lax.all_to_all(copies, axis, 0, 0, axis_index_groups=groups)  25.3 us
    all_to_all x1, waiting for transfers between devices, send_shares(): got = lax.all_to_all(shares, axis, 0, 0, axis_index_groups=groups)  21.6 us
    all_to_all x1, starting transfers between devices, send_shares(): got = lax.all_to_all(shares, axis, 0, 0, axis_index_groups=groups)  9.35 us
    all_to_all x1, waiting for transfers between devices, shards(): lax.all_to_all(partial_grad.reshape(cols // 2, mine_b, -1), 'col', 0, 0,...  7.5 us
    all_to_all x1, starting transfers between devices, shards(): lax.all_to_all(partial_grad.reshape(cols // 2, mine_b, -1), 'col', 0, 0,...  6.3 us
    ppermute x3, starting transfers between devices, shards(): lax.ppermute(piece, 'col', swap)  6.25 us
    ppermute x1, starting transfers between devices, shards(): far = lax.ppermute(acts[1], ('row', 'col'), collect_far)  4.73 us
  transfers between devices with their start and end apart: 12, of which 6 were waited for; matrix products, arithmetic and copies ran while one was open for 3% of the time, Pallas kernels for 0%

profile of v10, /device:TPU:32, one launch (start us, length us, event | category | flops | bytes accessed | tf_op | source)
XLA Modules:
  0.0 138.7 jit_solution(13342960742630627442)
XLA Ops:
  0.7 0.7 copy-done
  1.4 2.4 %fusion.1 = bf16[16,8,64]{2,1,0:T(8,128)(2,1)S(1)} fusion(bf16[16,256,256]{2,1,0:T(8,128)(2,1)} %param.4, s32[]{:T(128)S(6)} %select_n.56, bf16[256,64]{0,1:T(8,128)(2,1)S(1)} %copy-done), kind=kOutput, calls=%fused_computation.3 | convolution fusion | flops 21012480 | bytes 2211844 | tf_op jit(solution)/shard_map/bim,mr->bir/dot_general | solution.py:120
  3.8 0.1 reshape.73
  3.9 0.7 broadcast_in_dim.4
  4.7 20.7 %all-to-all-start = ((bf16[16,16,512]{2,1,0:T(8,128)(2,1)}), bf16[16,16,512]{2,1,0:T(8,128)(2,1)S(1)}, u32[]{:S(2)}, u32[]{:S(2)}) async-start(bf16[16,16,512]{2,1,0:T(8,128)(2,1)} %broadcast_in_dim.4), calls=%async_computation | async-start | bytes 524288 | tf_op jit(solution)/shard_map/all_to_all | solution.py:21
  25.4 0.1 fusion.18
  25.5 1.9 %collective-permute-start.3 = (bf16[512,384]{1,0:T(8,128)(2,1)S(1)}, bf16[512,384]{1,0:T(8,128)(2,1)S(1)}, u32[]{:S(2)}, u32[]{:S(2)}) collective-permute-start(bf16[512,384]{1,0:T(8,128)(2,1)S(1)} %get-tuple-element.23), channel_id=1, source_target_pairs={{0,1},{1,0},{2,3},{3,2},{4,5},{5,4},{6,7},{7,6},{8,9},{9,8},{10,11... | collective-permute-start | bytes 1179656 | tf_op jit(solution)/shard_map/ppermute | solution.py:129
  27.4 2.4 %collective-permute-start.2 = (bf16[512,384]{1,0:T(8,128)(2,1)S(1)}, bf16[512,384]{1,0:T(8,128)(2,1)S(1)}, u32[]{:S(2)}, u32[]{:S(2)}) collective-permute-start(bf16[512,384]{1,0:T(8,128)(2,1)S(1)} %get-tuple-element.24), channel_id=1, source_target_pairs={{0,1},{1,0},{2,3},{3,2},{4,5},{5,4},{6,7},{7,6},{8,9},{9,8},{10,11... | collective-permute-start | bytes 1179656 | tf_op jit(solution)/shard_map/ppermute | solution.py:129
  29.9 1.9 %collective-permute-start.4 = (bf16[512,256]{1,0:T(8,128)(2,1)S(1)}, bf16[512,256]{1,0:T(8,128)(2,1)S(1)}, u32[]{:S(2)}, u32[]{:S(2)}) collective-permute-start(bf16[512,256]{1,0:T(8,128)(2,1)S(1)} %split.17), channel_id=1, source_target_pairs={{0,1},{1,0},{2,3},{3,2},{4,5},{5,4},{6,7},{7,6},{8,9},{9,8},{10,11... | collective-permute-start | bytes 786440 | tf_op jit(solution)/shard_map/ppermute | solution.py:129
  31.8 1.5 %collective-permute-done.4.rest_2_ = bf16[512,256]{1,0:T(8,128)(2,1)S(1)} collective-permute-done((bf16[512,256]{1,0:T(8,128)(2,1)S(1)}, bf16[512,256]{1,0:T(8,128)(2,1)S(1)}, u32[]{:S(2)}, u32[]{:S(2)}) %collective-permute-start.4) | collective-permute-done | bytes 262176 | tf_op jit(solution)/shard_map/ppermute | solution.py:129
  33.3 7.4 %all-to-all-done = bf16[16,16,512]{2,1,0:T(8,128)(2,1)S(1)} async-done(((bf16[16,16,512]{2,1,0:T(8,128)(2,1)}), bf16[16,16,512]{2,1,0:T(8,128)(2,1)S(1)}, u32[]{:S(2)}, u32[]{:S(2)}) %all-to-all-start) | async-done | bytes 262176 | tf_op jit(solution)/shard_map/all_to_all | solution.py:21
  40.7 1.8 %times_weights.1 = bf16[256,2048]{1,0:T(8,128)(2,1)} custom-call(bf16[256,512]{1,0:T(8,128)(2,1)S(1)} %bitcast.22, bf16[512,1024]{1,0:T(8,128)(2,1)S(1)} %copy-done.1, bf16[512,384]{1,0:T(8,128)(2,1)S(1)} %collective-permute-done.2.rest_0_, bf16[512,384]{1,0:T(8,128)(2,1)S(1)} %collective-permute-done.3.rest_1_, ...), custom_call_target="tpu_custom_call" | custom-call | tf_op jit(solution)/shard_map/times_weights/pallas_call | solution.py:51
  42.5 9.3 %all-to-all-start.1 = ((bf16[32,8,2048]{2,1,0:T(8,128)(2,1)}), bf16[32,8,2048]{2,1,0:T(8,128)(2,1)}, u32[]{:S(2)}, u32[]{:S(2)}) async-start(bf16[32,8,2048]{2,1,0:T(8,128)(2,1)} %bitcast.25), calls=%async_computation.1 | async-start | bytes 2097152 | tf_op jit(solution)/shard_map/all_to_all | solution.py:26
  51.9 0.7 collective-permute-start
  52.6 4.6 %collective-permute-start.1 = (bf16[8,1024]{1,0:T(8,128)(2,1)S(1)}, bf16[8,1024]{1,0:T(8,128)(2,1)S(1)}, u32[]{:S(2)}, u32[]{:S(2)}) collective-permute-start(bf16[8,1024]{1,0:T(8,128)(2,1)S(1)} %get-tuple-element.32), channel_id=1, source_target_pairs={{0,32},{1,0},{2,34},{3,2},{4,36},{5,4},{6,38},{7,6},{8,40},{9,8},{... | collective-permute-start | bytes 49160 | tf_op jit(solution)/shard_map/ppermute | solution.py:135
  57.2 21.6 %all-to-all-done.1 = bf16[32,8,2048]{2,1,0:T(8,128)(2,1)} async-done(((bf16[32,8,2048]{2,1,0:T(8,128)(2,1)}), bf16[32,8,2048]{2,1,0:T(8,128)(2,1)}, u32[]{:S(2)}, u32[]{:S(2)}) %all-to-all-start.1) | async-done | bytes 1048608 | tf_op jit(solution)/shard_map/all_to_all | solution.py:26
  78.9 1.4 convert_reduce_fusion
  80.3 1.1 broadcast_in_dim.5
  81.4 5.3 %all-to-all-start.2 = ((bf16[32,8,2048]{2,1,0:T(8,128)(2,1)}), bf16[32,8,2048]{2,1,0:T(8,128)(2,1)S(1)}, u32[]{:S(2)}, u32[]{:S(2)}) async-start(bf16[32,8,2048]{2,1,0:T(8,128)(2,1)} %broadcast_in_dim.5), calls=%async_computation.2 | async-start | bytes 2097152 | tf_op jit(solution)/shard_map/all_to_all | solution.py:21
  86.7 1.9 %collective-permute-start.7 = (bf16[256,512]{1,0:T(8,128)(2,1)S(1)}, bf16[256,512]{1,0:T(8,128)(2,1)S(1)}, u32[]{:S(2)}, u32[]{:S(2)}) collective-permute-start(bf16[256,512]{1,0:T(8,128)(2,1)S(1)} %bitcast.23), channel_id=1, source_target_pairs={{0,1},{1,0},{2,3},{3,2},{4,5},{5,4},{6,7},{7,6},{8,9},{9,8},{10,11... | collective-permute-start | bytes 786440 | tf_op jit(solution)/shard_map/ppermute | solution.py:151
  88.7 0.7 collective-permute-start.5
  89.4 4.7 %collective-permute-start.6 = (bf16[8,1024]{1,0:T(8,128)(2,1)S(1)}, bf16[8,1024]{1,0:T(8,128)(2,1)S(1)}, u32[]{:S(2)}, u32[]{:S(2)}) collective-permute-start(bf16[8,1024]{1,0:T(8,128)(2,1)S(1)} %get-tuple-element.28), channel_id=1, source_target_pairs={{32,0},{0,1},{34,2},{2,3},{36,4},{4,5},{38,6},{6,7},{40,8},{8,9},{... | collective-permute-start | bytes 49160 | tf_op jit(solution)/shard_map/ppermute | solution.py:148
  94.1 2.3 %collective-permute-done.6 = bf16[8,1024]{1,0:T(8,128)(2,1)S(1)} collective-permute-done((bf16[8,1024]{1,0:T(8,128)(2,1)S(1)}, bf16[8,1024]{1,0:T(8,128)(2,1)S(1)}, u32[]{:S(2)}, u32[]{:S(2)}) %collective-permute-start.6) | collective-permute-done | bytes 16416 | tf_op jit(solution)/shard_map/ppermute | solution.py:148
  96.4 0.6 maximum_select_fusion.2
  97.0 17.9 %all-to-all-done.2 = bf16[32,8,2048]{2,1,0:T(8,128)(2,1)S(1)} async-done(((bf16[32,8,2048]{2,1,0:T(8,128)(2,1)}), bf16[32,8,2048]{2,1,0:T(8,128)(2,1)S(1)}, u32[]{:S(2)}, u32[]{:S(2)}) %all-to-all-start.2) | async-done | bytes 1048608 | tf_op jit(solution)/shard_map/all_to_all | solution.py:21
  114.9 2.7 %times_weights_back.1 = bf16[256,512]{1,0:T(8,128)(2,1)} custom-call(bf16[256,2048]{1,0:T(8,128)(2,1)S(1)} %bitcast.19, bf16[512,1024]{1,0:T(8,128)(2,1)S(1)} %copy-done.1, bf16[512,384]{1,0:T(8,128)(2,1)} %copy-done.3, bf16[512,384]{1,0:T(8,128)(2,1)} %copy-done.2, bf16[512,256]{1,0:T(8,128)(2,1)} %copy-done.4), custom_call_target="tpu_custom_call" | custom-call | tf_op jit(solution)/shard_map/times_weights_back/pallas_call | solution.py:78
  117.7 6.3 %all-to-all-start.3 = ((bf16[16,16,512]{2,1,0:T(8,128)(2,1)}), bf16[16,16,512]{2,1,0:T(8,128)(2,1)S(1)}, u32[]{:S(2)}, u32[]{:S(2)}) async-start(bf16[16,16,512]{2,1,0:T(8,128)(2,1)} %bitcast.7), calls=%async_computation.3 | async-start | bytes 524288 | tf_op jit(solution)/shard_map/all_to_all | solution.py:157
  124.0 2.2 %all-gather = bf16[256,1024]{1,0:T(8,128)(2,1)S(1)} all-gather(bf16[128,1024]{1,0:T(8,128)(2,1)S(1)} %get-tuple-element.21), channel_id=2, replica_groups={{0,1},{2,3},{4,5},{6,7},{8,9},{10,11},{12,13},{14,15},{16,17},{18,19},{..., dimensions={0}, use_global_device_ids=true | all-gather | bytes 786432 | tf_op jit(solution)/shard_map/all_gather | solution.py:164
  126.2 2.2 %all-gather.1 = bf16[256,1024]{1,0:T(8,128)(2,1)S(1)} all-gather(bf16[128,1024]{1,0:T(8,128)(2,1)S(1)} %get-tuple-element.22), channel_id=3, replica_groups={{0,1},{2,3},{4,5},{6,7},{8,9},{10,11},{12,13},{14,15},{16,17},{18,19},{..., dimensions={0}, use_global_device_ids=true | all-gather | bytes 786432 | tf_op jit(solution)/shard_map/all_gather | solution.py:164
  128.4 2.1 %fusion.2 = f32[512,1024]{1,0:T(8,128)} fusion(bf16[128,1024]{1,0:T(8,128)(2,1)S(1)} %dynamic-slice_bitcast_fusion, bf16[128,1024]{1,0:T(8,128)(2,1)S(1)} %dynamic-slice_bitcast_fusion.1, bf16[256,1024]{1,0:T(8,128)(2,1)S(1)} %slice.24, bf16[256,512]{1,0:T(8,128)(2,1)S(1)} %collective-permute-done.7, bf16[256,512]{1,0:T(8,128)(2,1)S(1)} %bitcast.24), kind=kOutput, calls=%fused_computation.4 | convolution fusion | flops 541065216 | bytes 3670016 | tf_op jit(solution)/shard_map/dot_general | solution.py:169
  130.5 7.5 %all-to-all-done.3 = bf16[16,16,512]{2,1,0:T(8,128)(2,1)S(1)} async-done(((bf16[16,16,512]{2,1,0:T(8,128)(2,1)}), bf16[16,16,512]{2,1,0:T(8,128)(2,1)S(1)}, u32[]{:S(2)}, u32[]{:S(2)}) %all-to-all-start.3) | async-done | bytes 262176 | tf_op jit(solution)/shard_map/all_to_all | solution.py:157
  138.0 0.7 convert_reduce_fusion.1
  (27 shorter events, 0.3 us)
Async XLA Ops:
  0.6 0.8 copy-start
  0.6 24.7 %copy-start.1 = (bf16[512,1024]{1,0:T(8,128)(2,1)S(1)}, bf16[512,1024]{1,0:T(8,128)(2,1)}, u32[]{:S(2)}) copy-start(bf16[512,1024]{1,0:T(8,128)(2,1)} %own.3) | copy-start | bytes 3145732
  4.7 36.1 %all-to-all-start = ((bf16[16,16,512]{2,1,0:T(8,128)(2,1)}), bf16[16,16,512]{2,1,0:T(8,128)(2,1)S(1)}, u32[]{:S(2)}, u32[]{:S(2)}) async-start(bf16[16,16,512]{2,1,0:T(8,128)(2,1)} %broadcast_in_dim.4), calls=%async_computation | async-start | bytes 524288 | tf_op jit(solution)/shard_map/all_to_all | solution.py:21
  25.5 7.8 %collective-permute-start.3 = (bf16[512,384]{1,0:T(8,128)(2,1)S(1)}, bf16[512,384]{1,0:T(8,128)(2,1)S(1)}, u32[]{:S(2)}, u32[]{:S(2)}) collective-permute-start(bf16[512,384]{1,0:T(8,128)(2,1)S(1)} %get-tuple-element.23), channel_id=1, source_target_pairs={{0,1},{1,0},{2,3},{3,2},{4,5},{5,4},{6,7},{7,6},{8,9},{9,8},{10,11... | collective-permute-start | bytes 1179656 | tf_op jit(solution)/shard_map/ppermute | solution.py:129
  27.4 5.9 %collective-permute-start.2 = (bf16[512,384]{1,0:T(8,128)(2,1)S(1)}, bf16[512,384]{1,0:T(8,128)(2,1)S(1)}, u32[]{:S(2)}, u32[]{:S(2)}) collective-permute-start(bf16[512,384]{1,0:T(8,128)(2,1)S(1)} %get-tuple-element.24), channel_id=1, source_target_pairs={{0,1},{1,0},{2,3},{3,2},{4,5},{5,4},{6,7},{7,6},{8,9},{9,8},{10,11... | collective-permute-start | bytes 1179656 | tf_op jit(solution)/shard_map/ppermute | solution.py:129
  29.9 3.4 %collective-permute-start.4 = (bf16[512,256]{1,0:T(8,128)(2,1)S(1)}, bf16[512,256]{1,0:T(8,128)(2,1)S(1)}, u32[]{:S(2)}, u32[]{:S(2)}) collective-permute-start(bf16[512,256]{1,0:T(8,128)(2,1)S(1)} %split.17), channel_id=1, source_target_pairs={{0,1},{1,0},{2,3},{3,2},{4,5},{5,4},{6,7},{7,6},{8,9},{9,8},{10,11... | collective-permute-start | bytes 786440 | tf_op jit(solution)/shard_map/ppermute | solution.py:129
  33.3 9.2 %copy-start.4 = (bf16[512,256]{1,0:T(8,128)(2,1)}, bf16[512,256]{1,0:T(8,128)(2,1)S(1)}, u32[]{:S(2)}) copy-start(bf16[512,256]{1,0:T(8,128)(2,1)S(1)} %collective-permute-done.4.rest_2_) | copy-start | bytes 786436
  33.3 9.2 %copy-start.2 = (bf16[512,384]{1,0:T(8,128)(2,1)}, bf16[512,384]{1,0:T(8,128)(2,1)S(1)}, u32[]{:S(2)}) copy-start(bf16[512,384]{1,0:T(8,128)(2,1)S(1)} %collective-permute-done.3.rest_1_) | copy-start | bytes 1179652
  33.3 9.2 %copy-start.3 = (bf16[512,384]{1,0:T(8,128)(2,1)}, bf16[512,384]{1,0:T(8,128)(2,1)S(1)}, u32[]{:S(2)}) copy-start(bf16[512,384]{1,0:T(8,128)(2,1)S(1)} %collective-permute-done.2.rest_0_) | copy-start | bytes 1179652
  40.7 11.2 %copy-start.5 = (bf16[16,1024]{1,0:T(8,128)(2,1)S(1)}, bf16[16,1024]{1,0:T(8,128)(2,1)}, u32[]{:S(2)}) copy-start(bf16[16,1024]{1,0:T(8,128)(2,1)} %param.7) | copy-start | bytes 98308
  42.5 36.4 %all-to-all-start.1 = ((bf16[32,8,2048]{2,1,0:T(8,128)(2,1)}), bf16[32,8,2048]{2,1,0:T(8,128)(2,1)}, u32[]{:S(2)}, u32[]{:S(2)}) async-start(bf16[32,8,2048]{2,1,0:T(8,128)(2,1)} %bitcast.25), calls=%async_computation.1 | async-start | bytes 2097152 | tf_op jit(solution)/shard_map/all_to_all | solution.py:26
  51.9 28.3 %collective-permute-start = (bf16[8,1024]{1,0:T(8,128)(2,1)S(1)}, bf16[8,1024]{1,0:T(8,128)(2,1)S(1)}, u32[]{:S(2)}, u32[]{:S(2)}) collective-permute-start(bf16[8,1024]{1,0:T(8,128)(2,1)S(1)} %get-tuple-element.31), channel_id=1, source_target_pairs={{0,0},{1,32},{2,2},{3,34},{4,4},{5,36},{6,6},{7,38},{8,8},{9,40},{... | collective-permute-start | bytes 49160 | tf_op jit(solution)/shard_map/ppermute | solution.py:132
  52.6 27.7 %collective-permute-start.1 = (bf16[8,1024]{1,0:T(8,128)(2,1)S(1)}, bf16[8,1024]{1,0:T(8,128)(2,1)S(1)}, u32[]{:S(2)}, u32[]{:S(2)}) collective-permute-start(bf16[8,1024]{1,0:T(8,128)(2,1)S(1)} %get-tuple-element.32), channel_id=1, source_target_pairs={{0,32},{1,0},{2,34},{3,2},{4,36},{5,4},{6,38},{7,6},{8,40},{9,8},{... | collective-permute-start | bytes 49160 | tf_op jit(solution)/shard_map/ppermute | solution.py:135
  81.4 33.5 %all-to-all-start.2 = ((bf16[32,8,2048]{2,1,0:T(8,128)(2,1)}), bf16[32,8,2048]{2,1,0:T(8,128)(2,1)S(1)}, u32[]{:S(2)}, u32[]{:S(2)}) async-start(bf16[32,8,2048]{2,1,0:T(8,128)(2,1)} %broadcast_in_dim.5), calls=%async_computation.2 | async-start | bytes 2097152 | tf_op jit(solution)/shard_map/all_to_all | solution.py:21
  86.7 10.3 %collective-permute-start.7 = (bf16[256,512]{1,0:T(8,128)(2,1)S(1)}, bf16[256,512]{1,0:T(8,128)(2,1)S(1)}, u32[]{:S(2)}, u32[]{:S(2)}) collective-permute-start(bf16[256,512]{1,0:T(8,128)(2,1)S(1)} %bitcast.23), channel_id=1, source_target_pairs={{0,1},{1,0},{2,3},{3,2},{4,5},{5,4},{6,7},{7,6},{8,9},{9,8},{10,11... | collective-permute-start | bytes 786440 | tf_op jit(solution)/shard_map/ppermute | solution.py:151
  88.7 5.4 %collective-permute-start.5 = (bf16[8,1024]{1,0:T(8,128)(2,1)S(1)}, bf16[8,1024]{1,0:T(8,128)(2,1)S(1)}, u32[]{:S(2)}, u32[]{:S(2)}) collective-permute-start(bf16[8,1024]{1,0:T(8,128)(2,1)S(1)} %get-tuple-element.27), channel_id=1, source_target_pairs={{0,0},{32,1},{2,2},{34,3},{4,4},{36,5},{6,6},{38,7},{8,8},{40,9},{... | collective-permute-start | bytes 49160 | tf_op jit(solution)/shard_map/ppermute | solution.py:147
  89.4 7.1 %collective-permute-start.6 = (bf16[8,1024]{1,0:T(8,128)(2,1)S(1)}, bf16[8,1024]{1,0:T(8,128)(2,1)S(1)}, u32[]{:S(2)}, u32[]{:S(2)}) collective-permute-start(bf16[8,1024]{1,0:T(8,128)(2,1)S(1)} %get-tuple-element.28), channel_id=1, source_target_pairs={{32,0},{0,1},{34,2},{2,3},{36,4},{4,5},{38,6},{6,7},{40,8},{8,9},{... | collective-permute-start | bytes 49160 | tf_op jit(solution)/shard_map/ppermute | solution.py:148
  117.7 20.3 %all-to-all-start.3 = ((bf16[16,16,512]{2,1,0:T(8,128)(2,1)}), bf16[16,16,512]{2,1,0:T(8,128)(2,1)S(1)}, u32[]{:S(2)}, u32[]{:S(2)}) async-start(bf16[16,16,512]{2,1,0:T(8,128)(2,1)} %bitcast.7), calls=%async_computation.3 | async-start | bytes 524288 | tf_op jit(solution)/shard_map/all_to_all | solution.py:157
